TPU v7x, 128 devices: a whole 4x4x4 slice. The times are simulated.
128 devices in a mesh: seq: 32 (over x, z, core), head: 4 (over y).
Axes of the slice: x: 4, y: 4, z: 4, core: 2. Of those that a mesh axis runs over, the one named last changes fastest.
Arguments:
- inputs: bfloat16 [32768, 6144], P('seq'), may hold values from -6 to 6
- query_vectors: bfloat16 [32768, 4096], P('seq', 'head')
- key_vectors: bfloat16 [32768, 4096], P('seq', 'head'), may hold values from -6 to 6
- value_weight: bfloat16 [6144, 4096], P('seq', 'head'), may hold values from -0.078125 to 0.078125
- log_decay: float32 [32, 32768], P('head', 'seq'), may hold values from -0.8 to 0
- doc_start: int32 [128], P('seq'), may hold values 0 or 1
- norm_gain: float32 [4096], P('head'), may hold values from 0.1 to 1.9
Outputs:
- attended: bfloat16 [32768, 4096], P('seq', 'head')
All inputs are finite; a program needn't handle non-finite values. No bound on the sum of `doc_start` on one device may be relied on, other than what follows from the above.
Results may differ from a plain program's by a relative error of at most 0.0053.
Values may be sent and summed in bfloat16 or wider, within the bound.
No kernel may reach another device: no remote copies, remote signals or barrier semaphores. Data moves between devices by JAX's collectives and lax.ppermute only.
A program may use at most 128 MiB of HBM per device.

v0:
```python
import jax
import jax.numpy as jnp
from jax import lax
from jax.sharding import PartitionSpec as P

SHARD_ATTN_PARTS = 32
E = 128
SPAN = 256


def per_device(inputs, query_vectors, key_vectors, value_weight, log_decay, doc_start, norm_gain):
    tok_rows = inputs.shape[0]
    width_out = value_weight.shape[1]
    head_count = width_out // E
    blocks = tok_rows // SPAN
    values = jnp.dot(
        inputs,
        lax.all_gather(value_weight, "seq", axis=0, tiled=True),
        preferred_element_type=jnp.float32,
    ).astype(jnp.bfloat16)
    query_blocks = query_vectors.reshape(blocks, SPAN, head_count, E)
    key_blocks = key_vectors.reshape(blocks, SPAN, head_count, E)
    value_blocks = values.reshape(blocks, SPAN, head_count, E)
    cumulative = jnp.cumsum(log_decay.reshape(head_count, blocks, SPAN), axis=2)
    cum_blocks = jnp.transpose(cumulative, (1, 0, 2))
    causal = lax.broadcasted_iota(jnp.int32, (SPAN, SPAN), 0) >= lax.broadcasted_iota(
        jnp.int32, (SPAN, SPAN), 1
    )
    scores = jnp.einsum(
        "cihe,cjhe->chij", query_blocks, key_blocks, preferred_element_type=jnp.float32
    )
    gaps = cum_blocks[:, :, :, None] - cum_blocks[:, :, None, :]
    weights = (scores * jnp.exp(jnp.where(causal[None, None], gaps, -1e30))).astype(jnp.bfloat16)
    inner = jnp.einsum("chij,cjhe->cihe", weights, value_blocks, preferred_element_type=jnp.float32)
    span_end = cumulative[:, :, -1]
    key_scale = jnp.transpose(jnp.exp(span_end[:, :, None] - cumulative), (1, 2, 0))[:, :, :, None]
    key_decayed = (key_blocks * key_scale).astype(jnp.bfloat16)
    updates = jnp.einsum(
        "cjhe,cjhf->chef", key_decayed, value_blocks, preferred_element_type=jnp.float32
    )
    survive = 1.0 - doc_start.astype(jnp.float32)
    local_memory = jnp.zeros((head_count, E, E), jnp.float32)
    carry_factor = jnp.ones((head_count,), jnp.float32)
    start_states = []
    start_factors = []
    for block in range(blocks):
        local_memory = local_memory * survive[block]
        carry_factor = carry_factor * survive[block]
        start_states.append(local_memory)
        start_factors.append(carry_factor)
        block_decay = jnp.exp(span_end[:, block])
        local_memory = block_decay[:, None, None] * local_memory + updates[block]
        carry_factor = carry_factor * block_decay
    all_factors, all_states = (
        lax.all_gather(carry_factor[None], "seq", axis=0, tiled=True),
        lax.all_gather(local_memory[None], "seq", axis=0, tiled=True),
    )
    position_now = lax.axis_index("seq")
    ranks = jnp.arange(all_factors.shape[0])
    earlier = (ranks < position_now)[:, None]
    factors_used = jnp.where(earlier, all_factors, 1.0)
    suffix = jnp.cumprod(factors_used[::-1], axis=0)[::-1]
    after = jnp.concatenate([suffix[1:], jnp.ones((1, head_count), jnp.float32)], axis=0)
    weights_sum = jnp.where(earlier, after, 0.0)
    incoming = jnp.einsum("nh,nhef->hef", weights_sum, all_states, precision=lax.Precision.HIGHEST)
    block_states = jnp.stack(start_factors)[:, :, None, None] * incoming[None] + jnp.stack(
        start_states
    )
    query_scale = jnp.transpose(jnp.exp(cumulative), (1, 2, 0))[:, :, :, None]
    query_decayed = query_blocks.astype(jnp.float32) * query_scale
    outer = jnp.einsum(
        "cihe,chef->cihf", query_decayed, block_states, precision=lax.Precision.HIGHEST
    )
    combined = (inner + outer).reshape(tok_rows, width_out)
    local_squares = jnp.sum(combined * combined, axis=1)
    square_total = lax.psum(local_squares, "head")
    mean_square = square_total / (SHARD_ATTN_PARTS * E)
    return (combined * lax.rsqrt(mean_square + 1e-06)[:, None] * norm_gain[None, :]).astype(
        jnp.bfloat16
    )


def solution(mesh):
    placed = (
        P("seq", None),
        P("seq", "head"),
        P("seq", "head"),
        P("seq", "head"),
        P("head", "seq"),
        P("seq"),
        P("head"),
    )
    return jax.shard_map(
        per_device, mesh=mesh, in_specs=placed, out_specs=P("seq", "head"), check_vma=False
    )
```

profile of v0, /device:TPU:0, one launch (start us, length us, event | category | flops | bytes accessed | tf_op | source)
XLA Modules:
  0.0 226.2 jit_solution(371942434578229823)
XLA Ops:
  6.5 0.7 all-gather.4.cloned.1.call-update
  7.3 0.8 copy.41
  8.1 2.3 reduce-window.6
  10.3 0.2 slice_reduce_fusion
  10.5 0.7 convert_subtract_fusion
  11.2 0.6 fusion.50
  12.5 3.5 %copy.56 = bf16[128,8,8,128]{3,2,1,0:T(8,128)(2,1)} copy(bf16[128,8,8,128]{3,1,2,0:T(8,128)(2,1)} %bitcast.91) | data formatting | bytes 4194304
  16.0 3.0 %copy.44 = bf16[4,256,8,128]{1,3,2,0:T(8,128)(2,1)S(1)} copy(bf16[4,256,8,128]{3,2,1,0:T(8,128)(2,1)} %bitcast.89) | data formatting | bytes 4194304 | tf_op jit(solution)/shard_map/reshape | solution.py:22
  19.0 0.1 copy_bitcast_fusion
  19.1 0.2 slice_reduce_fusion.1
  19.3 0.1 exponential_bitcast_fusion
  19.4 55.7 %all-gather.4.cloned.1.call-done = bf16[6144,1024]{1,0:T(8,128)(2,1)} async-done(((bf16[192,1024]{1,0:T(8,128)(2,1)}), bf16[6144,1024]{1,0:T(8,128)(2,1)}) %all-gather.4.cloned.1.call-update) | async-done | bytes 12582928 | tf_op jit(solution)/shard_map/all_gather | solution.py:18
  75.1 17.4 %convert_bitcast_fusion = bf16[128,8,8,128]{3,1,2,0:T(8,128)(2,1)S(1)} fusion(bf16[1024,6144]{1,0:T(8,128)(2,1)} %param.7, bf16[6144,1024]{1,0:T(8,128)(2,1)} %all-gather.4.cloned.1.call-done), kind=kOutput, calls=%fused_computation.28 | convolution fusion | flops 12885950464 | bytes 27262976 | tf_op jit(solution)/shard_map/dot_general | solution.py:16
  92.5 0.6 copy.54
  93.1 0.8 fusion.16
  93.9 0.6 copy-done
  94.4 3.0 %slice_add_fusion = (f32[1,8,128,128]{3,2,1,0:T(8,128)}, f32[1,8,128,128]{3,2,1,0:T(8,128)S(1)}, f32[1,8,128,128]{3,2,1,0:T(8,128)S(1)}, f32[1,8,128,128]{3,2,1,0:T(8,128)}) fusion(f32[4,8,128,128]{3,2,1,0:T(8,128)S(1)} %fusion.16, f32[8]{0:T(128)S(1)} %get-tuple-element.18, f32[]{:T(128)} %bitcast.8, f32[8]{0:T(128)S(1)} %get-tuple-element.19, f32[]{:T(128)} %bitcast.6, ...), kind=kLoop, calls=%fused_computation.36 | loop fusion | flops 1310720 | bytes 4194444 | tf_op jit(solution)/shard_map/add | solution.py:52
  97.5 2.6 %fusion.36 = (f32[1,1,8]{2,1,0:T(1,128)S(1)}, f32[1,8]{1,0:T(1,128)S(1)}, f32[1,8]{1,0:T(1,128)S(1)}, f32[1,8]{1,0:T(1,128)S(1)}) fusion(f32[8,4]{0,1:T(4,128)S(1)} %slice_reduce_fusion.1, f32[]{:T(128)} %bitcast.8, f32[]{:T(128)} %bitcast.6, f32[]{:T(128)} %bitcast.3, f32[]{:T(128)} %bitcast.2), kind=kLoop, calls=%fused_computation.55 | loop fusion | flops 56 | bytes 272
  100.0 21.0 %all-gather = f32[32,1,8]{2,1,0:T(1,128)S(1)} all-gather(f32[1,1,8]{2,1,0:T(1,128)S(1)} %get-tuple-element.9), channel_id=1, replica_groups=mesh['seq'=32,'head'=4] {'seq'}, dimensions={0}, use_global_device_ids=true | all-gather | bytes 1056 | tf_op jit(solution)/shard_map/all_gather | solution.py:55
  121.0 0.1 broadcast_select_fusion
  121.2 0.1 select_bitcast_fusion
  121.2 0.1 copy.49
  121.3 0.7 pad.5.clone
  122.0 3.6 %copy.55 = bf16[128,8,8,128]{3,2,1,0:T(8,128)(2,1)} copy(bf16[128,8,8,128]{3,1,2,0:T(8,128)(2,1)} %bitcast.92) | data formatting | bytes 4194304
  125.6 0.1 pad_maximum_fusion
  125.7 6.5 %fusion.2 = f32[4,8,128,256]{3,2,1,0:T(8,128)} fusion(f32[4,8,256]{2,1,0:T(8,128)S(1)} %get-tuple-element.16, pred[256,256]{1,0:T(8,128)(4,1)S(1)} %iota_compare_fusion, bf16[4,256,8,128]{1,3,2,0:T(8,128)(2,1)S(1)} %copy.44, bf16[4,256,8,128]{3,2,1,0:T(8,128)(2,1)} %bitcast.86, bf16[4,256,8,128]{3,2,1,0:T(8,128)(2,1)} %bitcast.87), kind=kOutput, calls=%fused_computation.3 | convolution fusion | flops 1082130432 | bytes 10584064 | tf_op jit(solution)/shard_map/chij,cjhe->cihe/dot_general | solution.py:34
  132.2 37.6 %all-gather.6.cloned.1.call-done = f32[32,8,128,128]{3,2,1,0:T(8,128)} async-done(((f32[1,8,128,128]{3,2,1,0:T(8,128)}), f32[32,8,128,128]{3,2,1,0:T(8,128)}) %all-gather.6.cloned.1.call-update) | async-done | bytes 16777232 | tf_op jit(solution)/shard_map/all_gather | solution.py:56
  169.8 22.0 %fusion = f32[8,1,128,128]{3,1,2,0:T(1,128)S(1)} fusion(f32[32,8,1,1]{0,2,3,1:T(1,128)S(1)} %copy.49, f32[32,8,128,128]{3,2,1,0:T(8,128)} %all-gather.6.cloned.1.call-done), kind=kOutput, calls=%fused_computation | convolution fusion | flops 50331648 | bytes 17302528 | tf_op jit(solution)/shard_map/nh,nhef->hef/dot_general | solution.py:65
  191.8 7.6 %multiply_reduce_fusion = (f32[4,256]{1,0:T(4,128)S(1)}, f32[4,256,8,128]{1,3,2,0:T(8,128)}) fusion(f32[4,8,128,256]{3,2,1,0:T(8,128)S(1)} %copy-done.2, f32[4,256,8]{1,2,0:T(8,128)S(1)} %get-tuple-element.13, bf16[4,256,8,128]{3,2,1,0:T(8,128)(2,1)S(1)} %bitcast.88, f32[1,8,128,128]{3,2,1,0:T(8,128)S(1)} %get-tuple-element.6, ...), kind=kOutput, calls=%fused_computation.7 | convolution fusion | flops 1618476032 | bytes 12619920 | tf_op jit(solution)/shard_map/cihe,chef->cihf/dot_general | solution.py:71
  199.4 5.3 %copy.48 = f32[4,256,8,128]{3,2,1,0:T(8,128)} copy(f32[4,256,8,128]{1,3,2,0:T(8,128)} %get-tuple-element.26) | data formatting | bytes 8388608 | tf_op jit(solution)/shard_map/add | solution.py:74
  204.7 10.5 %psum.7 = f32[1024]{0:T(1024)S(1)} all-reduce(f32[1024]{0:T(1024)S(1)} %bitcast.97), channel_id=1, replica_groups=mesh['seq'=32,'head'=4] {'head'}, use_global_device_ids=true, to_apply=%region_4.5 | all-reduce | flops 1024 | bytes 8192 | tf_op jit(solution)/shard_map/psum | solution.py:76
  215.1 4.3 %fusion.4 = bf16[1024,1024]{1,0:T(8,128)(2,1)} fusion(f32[128,8,8,128]{3,2,1,0:T(8,128)} %bitcast.84, f32[1024]{0:T(1024)S(1)} %copy-done.4, f32[1024]{0:T(1024)S(1)} %add_rsqrt_fusion), kind=kLoop, calls=%fused_computation.6 | loop fusion | flops 3145728 | bytes 6299648 | tf_op jit(solution)/shard_map/convert_element_type | solution.py:78
  (23 shorter events, 0.2 us)
Async XLA Ops:
  6.5 68.5 %all-gather.4.cloned.1.call-start = ((), (), s32[]{:S(2)}) async-start(), calls=%async_computation | async-start | bytes 12976128 | tf_op jit(solution)/shard_map/all_gather | solution.py:18
  7.3 162.5 %all-gather.6.cloned.1.call-start = ((), (), s32[]{:S(2)}) async-start(), calls=%async_computation.1 | async-start | bytes 17301504 | tf_op jit(solution)/shard_map/all_gather | solution.py:56
  93.1 1.3 copy-start
  132.2 59.6 %copy-start.1 = (bf16[128,8,8,128]{3,2,1,0:T(8,128)(2,1)S(1)}, bf16[128,8,8,128]{3,2,1,0:T(8,128)(2,1)}, u32[]{:S(2)}) copy-start(bf16[128,8,8,128]{3,2,1,0:T(8,128)(2,1)} %copy.55) | copy-start | bytes 6291460
  169.8 22.0 %copy-start.2 = (f32[4,8,128,256]{3,2,1,0:T(8,128)S(1)}, f32[4,8,128,256]{3,2,1,0:T(8,128)}, u32[]{:S(2)}) copy-start(f32[4,8,128,256]{3,2,1,0:T(8,128)} %fusion.2) | copy-start | bytes 12582916
  169.8 22.0 %copy-start.3 = (f32[1,8,128,128]{3,2,1,0:T(8,128)S(1)}, f32[1,8,128,128]{3,2,1,0:T(8,128)}, u32[]{:S(2)}) copy-start(f32[1,8,128,128]{3,2,1,0:T(8,128)} %get-tuple-element.8) | copy-start | bytes 1572868
  199.4 15.7 %copy-start.4 = (f32[1024]{0:T(1024)S(1)}, f32[1024]{0:T(1024)}, u32[]{:S(2)}) copy-start(f32[1024]{0:T(1024)} %param.13) | copy-start | bytes 12292
Sparse Core Ops, SparseCore 0:
  9.6 65.4 all-gather.3
  97.6 72.1 all-gather.5
where the time goes:
time: 227 us; the launch traced here: 226 us
  waiting for transfers between devices  94 us (41%)
  matrix products  54.2 us (24%)
  blocking collectives  31.4 us (14%)
  local copies, waits for them, and re-layouts  19 us (8%)
  between operations  14.2 us (6%)
  other arithmetic  13.3 us (6%)
    all_gather x1, waiting for transfers between devices, per_device(): lax.all_gather(value_weight, 'seq', axis=0, tiled=True)  55.7 us
    all_gather x1, waiting for transfers between devices, per_device(): lax.all_gather(local_memory[None], 'seq', axis=0, tiled=True)  37.6 us
    dot_general x1, matrix products, per_device(): jnp.einsum('nh,nhef->hef', weights_sum, all_states, precision=lax.Precisi...  22 us
    all_gather x1, blocking collectives, per_device(): lax.all_gather(carry_factor[None], 'seq', axis=0, tiled=True)  21 us
    dot_general x1, matrix products, per_device(): jnp.dot(inputs, lax.all_gather(value_weight, 'seq', axis=0, tiled=True),...  17.4 us
    psum x1, blocking collectives, per_device(): square_total = lax.psum(local_squares, 'head')  10.5 us
    unnamed x14, local copies, waits for them, and re-layouts  8.29 us
    dot_general x1, matrix products, per_device(): jnp.einsum('cihe,chef->cihf', query_decayed, block_states, precision=lax....  7.58 us
  transfers between devices with their start and end apart: 2, of which 2 were waited for; matrix products, arithmetic and copies ran while one was open for 11% of the time, Pallas kernels for 0%

commit v1 on v0

v1 whole, which is shorter than its diff:
```python
import functools
import jax
import jax.numpy as jnp
from jax import lax
from jax.experimental import pallas as pl
from jax.experimental.pallas import tpu as pltpu
from jax.sharding import Mesh, PartitionSpec as P

SHARD_ATTN_PARTS = 32
E = 128
SPAN = 256
SEQ = ("x", "z", "core")
SWAP = [(0, 1), (1, 0)]
VM = pl.BlockSpec(memory_space=pltpu.VMEM)
HB = pl.BlockSpec(memory_space=pltpu.HBM)
MIB = 1024 * 1024
HALF = 512
LINE = 1536
CHIP = 384
f32, bf16 = jnp.float32, jnp.bfloat16


def swap(a):
    return lax.ppermute(a, "core", SWAP)


def ring(a, axis, step):
    return lax.ppermute(a, axis, [(i, (i + step) % 4) for i in range(4)])


def crossed(a, first, second, step0, step1):
    pairs = []
    for x in range(4):
        for z in range(4):
            for c in range(2):
                axis, step = ((first, step0), (second, step1))[c]
                tx = (x + step) % 4 if axis == "x" else x
                tz = (z + step) % 4 if axis == "z" else z
                pairs.append((x * 8 + z * 2 + c, tx * 8 + tz * 2 + c))
    return lax.ppermute(a, SEQ, pairs)


def dot(a, b, dims=((1,), (0,))):
    return lax.dot_general(a, b, (dims, ((), ())), preferred_element_type=f32)


def split_dot(a, m):
    high = m.astype(bf16)
    low = (m - high.astype(f32)).astype(bf16)
    return dot(a, high) + dot(a, low)


def block_cum(ld):
    lane = lax.broadcasted_iota(jnp.int32, ld.shape, 1)
    step = 1
    while step < SPAN:
        ld = ld + jnp.where(lane >= step, pltpu.roll(ld, step, 1), 0.0)
        step *= 2
    return ld


def vmem(a):
    return pltpu.with_memory_space_constraint(a, pltpu.VMEM)


def hbm(a):
    return pltpu.with_memory_space_constraint(a, pltpu.HBM)


def params(mib):
    return pltpu.CompilerParams(vmem_limit_bytes=mib * MIB)


def pre_kernel(ld_ref, q_hbm, k_hbm, w_hbm, kd_hbm, q_ref, k_ref, w_ref, kd_ref, sems):
    half = SPAN // 2
    low = lax.broadcasted_iota(jnp.int32, (half, half), 0) >= lax.broadcasted_iota(
        jnp.int32, (half, half), 1
    )

    def loads(h):
        lanes = pl.ds(pl.multiple_of(h * E, E), E)
        return (
            pltpu.make_async_copy(q_hbm.at[:, lanes], q_ref.at[:, lanes], sems.at[0, h]),
            pltpu.make_async_copy(k_hbm.at[:, lanes], k_ref.at[:, lanes], sems.at[1, h]),
        )

    def stores(h):
        lanes = pl.ds(pl.multiple_of(h * E, E), E)
        return (
            pltpu.make_async_copy(w_ref.at[h], w_hbm.at[h], sems.at[2, h]),
            pltpu.make_async_copy(kd_ref.at[:, lanes], kd_hbm.at[:, lanes], sems.at[3, h]),
        )

    for h in range(8):
        for c in loads(h):
            c.start()
    w_ref[:, :, :half, half:] = jnp.zeros((8, 4, half, half), bf16)
    cums = [block_cum(ld_ref[:, b * SPAN : (b + 1) * SPAN]) for b in range(4)]

    def one_head(h, carry):
        for c in loads(h):
            c.wait()
        head = lax.broadcasted_iota(jnp.int32, (8, SPAN), 0) == h
        lanes = pl.ds(pl.multiple_of(h * E, E), E)
        for b in range(4):
            row = jnp.sum(jnp.where(head, cums[b], 0.0), axis=0, keepdims=True)
            col = jnp.transpose(jnp.broadcast_to(row, (8, SPAN)))[:, 0:1]
            last = row[:, SPAN - 1 : SPAN]
            rows = slice(b * SPAN, (b + 1) * SPAN)
            k = k_ref[rows, lanes]
            kd_ref[rows, lanes] = (k.astype(f32) * jnp.exp(last - col)).astype(bf16)
            q = q_ref[rows, lanes]
            s = dot(q[:half], k[:half], ((1,), (1,)))
            g = jnp.exp(jnp.where(low, col[:half] - row[:, :half], -1e30))
            w_ref[h, b, :half, :half] = (s * g).astype(bf16)
            s = dot(q[half:], k, ((1,), (1,)))
            g = jnp.exp(col[half:] - row[:, :half])
            w_ref[h, b, half:, :half] = (s[:, :half] * g).astype(bf16)
            g = jnp.exp(jnp.where(low, col[half:] - row[:, half:], -1e30))
            w_ref[h, b, half:, half:] = (s[:, half:] * g).astype(bf16)
        for c in stores(h):
            c.start()
        return carry

    lax.fori_loop(0, 8, one_head, 0)
    for h in range(8):
        for c in stores(h):
            c.wait()


def pre(ld, q, k):
    shapes = ((8, 4, SPAN, SPAN), (1024, 1024))
    return pl.pallas_call(
        pre_kernel,
        in_specs=[VM, HB, HB],
        out_specs=[HB] * 2,
        out_shape=[pltpu.HBM(s, bf16) for s in shapes],
        scratch_shapes=[pltpu.VMEM((1024, 1024), bf16)] * 2
        + [pltpu.VMEM(s, bf16) for s in shapes]
        + [pltpu.SemaphoreType.DMA((4, 8))],
        compiler_params=params(20),
        cost_estimate=pl.CostEstimate(flops=10**9, transcendentals=2 * 10**6, bytes_accessed=10**7),
        name="pre",
    )(ld, hbm(q), hbm(k))


def input_copies(jobs, x_hbm, xv, sems):
    x, z, core = lax.axis_index("x"), lax.axis_index("z"), lax.axis_index("core")
    out = []
    for j, (mine, d) in enumerate(jobs):
        first = (core == 0) if mine else (core == 1)
        line = lax.rem(jnp.where(first, x, z) + 4 - d, 4)
        cs = []
        for e in range(4):
            other = lax.rem(jnp.where(first, z, x) + 4 - e, 4)
            at = jnp.where(first, line * LINE + other * CHIP, other * LINE + line * CHIP)
            cs.append(
                pltpu.make_async_copy(
                    x_hbm.at[:, pl.ds(pl.multiple_of(at, 128), CHIP)],
                    xv.at[j, :, pl.ds(e * CHIP, CHIP)],
                    sems.at[j, e],
                )
            )
        out.append(cs)
    return out


def multiply(j, xv, lo, hi, src, dst):
    for r in range(2):
        rows = slice(r * 512, (r + 1) * 512)
        part = dot(xv[j, rows, : 2 * CHIP], lo[...]) + dot(xv[j, rows, 2 * CHIP :], hi[...])
        if src is not None:
            part = part + src[rows, :]
        dst[rows, :] = part


def mm_kernel(jobs, ahead, has_acc, keep, x_hbm, *refs):
    n = 2 * len(jobs)
    refs = list(refs)
    take = lambda k: [refs.pop(0) for _ in range(k)]
    sides = [mine for mine, _ in jobs]
    halves = list(dict.fromkeys(sides))
    bufs = take(n)
    srcs = take(1) if has_acc else []
    outs = dict(zip(halves, take(len(halves))))
    nxt = take(1)[0] if ahead else None
    xv, sems, wv, wsems = take(4)
    acc, asems = take(2)
    lsems = take(1)[0] if ahead else None
    copies = input_copies(jobs, x_hbm, xv, sems)
    for i in range(n):
        copies[i // 2].append(pltpu.make_async_copy(bufs[i], wv.at[i], wsems.at[i]))
    for cs in copies:
        for c in cs:
            c.start()
    held = [pltpu.make_async_copy(s, acc.at[i], asems.at[i]) for i, s in enumerate(srcs)]
    for c in held:
        c.start()
    later = input_copies(ahead, x_hbm, nxt, lsems) if ahead else []
    for cs in later:
        for c in cs:
            c.start()
    for c in held:
        c.wait()
    seen = set()
    back = []
    for j, mine in enumerate(sides):
        for c in copies[j]:
            c.wait()
        i = halves.index(mine)
        dst = outs[mine] if keep else acc.at[i]
        src = dst if mine in seen else (acc.at[i] if has_acc else None)
        multiply(j, xv, wv.at[2 * j], wv.at[2 * j + 1], src, dst)
        seen.add(mine)
        if not keep and mine not in sides[j + 1 :]:
            back.append(pltpu.make_async_copy(acc.at[i], outs[mine], asems.at[i]))
            back[-1].start()
    for c in back:
        c.wait()
    for cs in later:
        for c in cs:
            c.wait()


def mm(jobs, ahead, keep, x, bufs, acc=None):
    n = len(jobs)
    halves = len(dict.fromkeys(mine for mine, _ in jobs))
    outs = [(pltpu.VMEM if keep else pltpu.HBM)((1024, HALF), f32)] * halves
    ospecs = [VM if keep else HB] * halves
    scratch = [
        pltpu.VMEM((n, 1024, LINE), bf16),
        pltpu.SemaphoreType.DMA((n, 4)),
        pltpu.VMEM((2 * n, 2 * CHIP, HALF), bf16),
        pltpu.SemaphoreType.DMA((2 * n,)),
        pltpu.VMEM((halves, 1024, HALF), f32),
        pltpu.SemaphoreType.DMA((halves,)),
    ]
    if ahead:
        outs.append(pltpu.VMEM((len(ahead), 1024, LINE), bf16))
        ospecs.append(VM)
        scratch.append(pltpu.SemaphoreType.DMA((len(ahead), 4)))
    extra = [] if acc is None else [hbm(acc)]
    return pl.pallas_call(
        functools.partial(mm_kernel, jobs, ahead, acc is not None, keep),
        in_specs=[HB] * (1 + len(bufs) + len(extra)),
        out_specs=ospecs,
        out_shape=outs,
        scratch_shapes=scratch,
        compiler_params=params(6 + 6 * n),
        cost_estimate=pl.CostEstimate(
            flops=2 * 1024 * LINE * HALF * n,
            transcendentals=0,
            bytes_accessed=n * 5 * 10**6,
        ),
        name="project",
    )(hbm(x), *[hbm(a) for a in bufs], *extra)


def head_col(ld_block):
    return jnp.transpose(jnp.exp(block_cum(ld_block)))


def post_kernel(jobs, dec, ld_ref, q_hbm, kd_hbm, w_hbm, mine_ref, their_ref, xv, *refs):
    bufs = refs[: 2 * len(jobs)]
    comb_hbm, keep_ref, give_ref, acc, q_ref, kd_ref, w_ref, comb_ref, sems, osems = refs[
        2 * len(jobs) :
    ]
    core = lax.axis_index("core")
    loads = [
        pltpu.make_async_copy(s, t, sems.at[i])
        for i, (s, t) in enumerate(((q_hbm, q_ref), (kd_hbm, kd_ref), (w_hbm, w_ref)))
    ]
    for c in loads:
        c.start()
    cols = [head_col(ld_ref[:, b * SPAN : (b + 1) * SPAN]) for b in range(4)]
    for j, (mine, _) in enumerate(jobs):
        src, half = (mine_ref, core) if mine else (their_ref, 1 - core)
        multiply(j, xv, bufs[2 * j], bufs[2 * j + 1], src, acc.at[half])
    for c in loads:
        c.wait()
    half = SPAN // 2
    stores = []
    for h in range(8):
        lanes = slice(h * E, (h + 1) * E)
        part = slice((h % 4) * E, (h % 4 + 1) * E)
        state = None
        for b in range(4):
            rows = slice(b * SPAN, (b + 1) * SPAN)
            v = acc[h // 4, rows, part].astype(bf16)
            top = dot(w_ref[h, b, :half, :half], v[:half])
            low = dot(w_ref[h, b, half:, :], v)
            inner = jnp.concatenate([top, low], axis=0)
            if b > 0:
                state = state * dec[32 + b : 33 + b, :]
                inner = inner + cols[b][:, h : h + 1] * split_dot(q_ref[rows, lanes], state)
            comb_ref[rows, lanes] = inner
            update = dot(kd_ref[rows, lanes], v, ((0,), (0,)))
            state = update if b == 0 else dec[h * 4 + b : h * 4 + b + 1, :] * state + update

        @pl.when(core == h // 4)
        def _():
            keep_ref[part, :] = state

        @pl.when(core != h // 4)
        def _():
            give_ref[part, :] = state

        stores.append(
            pltpu.make_async_copy(comb_ref.at[:, lanes], comb_hbm.at[:, lanes], osems.at[h])
        )
        stores[-1].start()
    for c in stores:
        c.wait()


def post(jobs, dec, ld, q, kd, w, mine, theirs, xv, bufs):
    return pl.pallas_call(
        functools.partial(post_kernel, jobs),
        in_specs=[VM, VM, HB, HB, HB] + [VM] * (3 + len(bufs)),
        out_specs=[HB, VM, VM],
        out_shape=[
            pltpu.HBM((1024, 1024), f32),
            pltpu.VMEM((HALF, E), f32),
            pltpu.VMEM((HALF, E), f32),
        ],
        scratch_shapes=[
            pltpu.VMEM((2, 1024, HALF), f32),
            pltpu.VMEM((1024, 1024), bf16),
            pltpu.VMEM((1024, 1024), bf16),
            pltpu.VMEM((8, 4, SPAN, SPAN), bf16),
            pltpu.VMEM((1024, 1024), f32),
            pltpu.SemaphoreType.DMA((3,)),
            pltpu.SemaphoreType.DMA((8,)),
        ],
        compiler_params=params(24),
        name="post",
    )(dec, ld, hbm(q), hbm(kd), hbm(w), mine, theirs, xv, *bufs)


def chip_kernel(cw, own_ref, recv_ref, f_ref, b_ref):
    for h in range(4):
        r = slice(h * E, (h + 1) * E)
        s = cw[h : h + 1, :] * own_ref[r, :] + cw[4 + h : 5 + h, :] * recv_ref[r, :]
        f_ref[r, :] = s
        b_ref[r, :] = s.astype(bf16)


def spread_kernel(sw, own_ref, r1, r2, r3, o0, o1, o2, o3):
    for h in range(4):
        r = slice(h * E, (h + 1) * E)
        src = [own_ref[r, :]] + [a[r, :].astype(f32) for a in (r1, r2, r3)]
        for d, o in enumerate((o0, o1, o2, o3)):
            s = None
            for e in range(4):
                at = (d * 4 + e) * 4 + h
                t = sw[at : at + 1, :] * src[e]
                s = t if s is None else s + t
            o[r, :] = s.astype(o.dtype)


def enter_kernel(ew, m0, r1, r2, r3, own_ref, recv_ref, mine_ref, other_ref):
    for h in range(4):
        r = slice(h * E, (h + 1) * E)
        i = m0[r, :]
        for a in (r1, r2, r3):
            i = i + a[r, :].astype(f32)
        w = [ew[4 * n + h : 4 * n + h + 1, :] for n in range(4)]
        mine_ref[r, :] = w[0] * i + w[1] * recv_ref[r, :]
        other_ref[r, :] = w[2] * i + w[3] * own_ref[r, :]


def small(kernel, name, args, outs):
    return pl.pallas_call(
        kernel,
        in_specs=[VM] * len(args),
        out_specs=[VM] * len(outs),
        out_shape=[pltpu.VMEM((HALF, E), t) for t in outs],
        compiler_params=params(4),
        name=name,
    )(*args)


def outer_kernel(
    sf, ld_ref, mine_ref, other_ref, q_hbm, comb_hbm, out_ref, sq_ref, q_ref, comb_ref, sems
):
    loads = []
    for b in range(4):
        rows = slice(b * SPAN, (b + 1) * SPAN)
        loads.append(
            [
                pltpu.make_async_copy(q_hbm.at[rows, :], q_ref.at[rows, :], sems.at[0, b]),
                pltpu.make_async_copy(comb_hbm.at[rows, :], comb_ref.at[rows, :], sems.at[1, b]),
            ]
        )
        for c in loads[b]:
            c.start()
    first = lax.axis_index("core") == 0
    high, low = [], []
    for h in range(8):
        r = slice((h % 4) * E, (h % 4 + 1) * E)
        a, b = mine_ref[r, :], other_ref[r, :]
        m = jnp.where(first, a, b) if h < 4 else jnp.where(first, b, a)
        high.append(m.astype(bf16))
        low.append((m - high[h].astype(f32)).astype(bf16))
    for b in range(4):
        for c in loads[b]:
            c.wait()
        rows = slice(b * SPAN, (b + 1) * SPAN)
        col = head_col(ld_ref[:, rows]) * sf[b : b + 1, :]
        total = None
        for h in range(8):
            lanes = slice(h * E, (h + 1) * E)
            q = q_ref[rows, lanes]
            o = (dot(q, high[h]) + dot(q, low[h])) * col[:, h : h + 1]
            o = comb_ref[rows, lanes] + o
            out_ref[rows, lanes] = o
            total = o * o if total is None else total + o * o
        for t in range(2):
            tt = jnp.transpose(total[t * E : (t + 1) * E, :])
            sq_ref[b * 2 + t : b * 2 + t + 1, :] = jnp.sum(tt, axis=0, keepdims=True)


def outer(sf, ld, q, mine, other, comb):
    return pl.pallas_call(
        outer_kernel,
        in_specs=[VM] * 4 + [HB] * 2,
        out_specs=[VM, VM],
        out_shape=[pltpu.VMEM((1024, 1024), f32), pltpu.VMEM((8, E), f32)],
        scratch_shapes=[
            pltpu.VMEM((1024, 1024), bf16),
            pltpu.VMEM((1024, 1024), f32),
            pltpu.SemaphoreType.DMA((2, 4)),
        ],
        compiler_params=params(12),
        name="outer",
    )(sf, ld, mine, other, hbm(q), hbm(comb))


def norm_kernel(out_ref, s0, s1, s2, s3, gain_ref, y_hbm, y_ref, sems):
    total = s0[...] + s1[...] + s2[...] + s3[...]
    scale = lax.rsqrt(total / (SHARD_ATTN_PARTS * E) + 1e-06)
    copies = []
    for t in range(8):
        col = jnp.transpose(jnp.broadcast_to(scale[t : t + 1, :], (E, E)))
        rows = slice(t * E, (t + 1) * E)
        for h in range(8):
            lanes = slice(h * E, (h + 1) * E)
            y_ref[rows, lanes] = (out_ref[rows, lanes] * col * gain_ref[:, lanes]).astype(bf16)
        c = pltpu.make_async_copy(y_ref.at[rows, :], y_hbm.at[rows, :], sems.at[t])
        c.start()
        copies.append(c)
    for c in copies:
        c.wait()


def norm(out, sqs, gain):
    return pl.pallas_call(
        norm_kernel,
        in_specs=[VM] * 6,
        out_specs=HB,
        out_shape=jax.ShapeDtypeStruct((1024, 1024), bf16),
        scratch_shapes=[pltpu.VMEM((1024, 1024), bf16), pltpu.SemaphoreType.DMA((8,))],
        compiler_params=params(8),
        name="norm",
    )(out, *sqs, gain)


def rows_of(a):
    return jnp.broadcast_to(a.reshape(-1, 1), (a.size, E))


def per_device(inputs, q, k, value_weight, ld, doc_start, gain):
    x, z, core = lax.axis_index("x"), lax.axis_index("z"), lax.axis_index("core")
    first = core == 0
    bar = lax.optimization_barrier

    my_w = lax.dynamic_slice(value_weight, (0, core * HALF), (CHIP // 2, HALF))
    their_w = lax.dynamic_slice(value_weight, (0, (1 - core) * HALF), (CHIP // 2, HALF))
    recv_w = swap(their_w)
    chip_w = jnp.where(
        first,
        jnp.concatenate([my_w, recv_w], axis=0),
        jnp.concatenate([recv_w, my_w], axis=0),
    )
    chip_w, ld, q, k = bar((chip_w, ld, q, k))
    line = [chip_w] + [crossed(chip_w, "z", "x", d, d) for d in (1, 2, 3)]

    sums = jnp.sum(ld.reshape(8, 4, SPAN), axis=2)
    bd = jnp.exp(sums)
    surv = 1.0 - doc_start.astype(f32)
    fac = bd * surv[None, :]
    f_own = jnp.prod(fac, axis=1)
    f_oth = swap(f_own)
    g = (f_own * f_oth)[None]

    def pair(g, axis, bit):
        return jnp.concatenate(
            [g, lax.ppermute(g, axis, [(i, i ^ bit) for i in range(4)])], axis=0
        )

    w, kd = pre(ld, q, k)
    g = pair(g, "z", 1)

    line, w, g = bar((tuple(line), w, g))
    p_lo = jnp.concatenate(line[:2], axis=0)
    p_hi = jnp.concatenate(line[2:], axis=0)
    up_lo = crossed(p_lo, "x", "z", 1, 1)
    dn_hi = crossed(p_hi, "x", "z", -1, -1)
    up_hi = crossed(p_hi, "x", "z", 1, 1)
    dn_lo = crossed(p_lo, "x", "z", -1, -1)
    mine, theirs = mm(
        ((True, 0), (False, 0)), (), False, inputs, (p_lo, p_hi, swap(p_lo), swap(p_hi))
    )
    up_lo, dn_hi, mine, theirs, g = bar((up_lo, dn_hi, mine, theirs, g))
    op_lo = crossed(up_lo, "x", "z", 1, 1)
    op_hi = crossed(dn_hi, "x", "z", -1, -1)
    g = pair(g, "z", 2)

    def my_heads(a):
        return jnp.where(first, a[..., :4], a[..., 4:])

    fo, ft = my_heads(f_own), my_heads(f_oth)
    one, zero = jnp.ones((4,), f32), jnp.zeros((4,), f32)
    cw = rows_of(jnp.where(first, jnp.concatenate([ft, one]), jnp.concatenate([one, fo])))
    ew = rows_of(
        jnp.where(
            first,
            jnp.concatenate([one, zero, fo, one]),
            jnp.concatenate([ft, one, one, zero]),
        )
    )
    dec = jnp.concatenate([rows_of(bd), rows_of(surv), jnp.zeros((4, E), f32)], axis=0)
    sf = jnp.stack([surv[b] * jnp.prod(fac[:, :b], axis=1) for b in range(4)], axis=0)

    bufs = [up_lo, up_hi, dn_lo, dn_hi]
    mine = mm(((True, 1), (True, 3)), (), True, inputs, bufs, mine)[0]
    mine, g, bufs = bar((mine, g, tuple(swap(a) for a in bufs)))
    g = pair(g, "x", 1)
    last = ((True, 2), (False, 2))
    theirs, xv = mm(((False, 1), (False, 3)), last, True, inputs, bufs, theirs)
    theirs, cw, ew, dec, sf, g = bar((theirs, cw, ew, dec, sf, g))
    g16 = pair(g, "x", 2)
    bufs = [op_lo, op_hi, swap(op_lo), swap(op_hi)]
    comb, own, give = post(
        last, vmem(dec), ld, q, kd, w, mine, theirs, xv, [vmem(a) for a in bufs]
    )
    give, g16 = bar((give, g16))
    off = jnp.arange(4)
    k_at = ((x ^ off)[:, None] * 4 + (z ^ off)[None, :]).reshape(16)
    src = jnp.where(first, x * 4 + (z - off) % 4, ((x - off) % 4) * 4 + z)
    tgt = jnp.where(first, ((x + off) % 4) * 4 + z, x * 4 + (z + off) % 4)
    between = (k_at[None, None, :] > src[None, :, None]) & (
        k_at[None, None, :] < tgt[:, None, None]
    )
    w16 = jnp.prod(jnp.where(between[..., None], my_heads(g16)[None, None], 1.0), axis=2)
    w16 = jnp.where((src[None, :] < tgt[:, None])[..., None], w16, 0.0)
    sw = rows_of(w16)

    recv = vmem(swap(give))
    chip, chip16 = small(chip_kernel, "chip", (vmem(cw), own, recv), (f32, bf16))
    got = [vmem(crossed(chip16, "z", "x", d, d)) for d in (1, 2, 3)]
    sent = small(spread_kernel, "spread", (vmem(sw), chip, *got), (f32, bf16, bf16, bf16))
    got = [vmem(crossed(sent[d], "x", "z", d, d)) for d in (1, 2, 3)]
    mine, give = small(
        enter_kernel, "enter", (vmem(ew), sent[0], *got, own, recv), (f32, f32)
    )
    other = vmem(swap(give))
    out, sq = outer(vmem(sf), ld, q, mine, other, comb)
    sqs = [sq] + [vmem(ring(sq, "head", d)) for d in (1, 2, 3)]
    return norm(out, sqs, gain.reshape(1, -1))


def solution(mesh):
    mesh = Mesh(mesh.devices.reshape(4, 4, 2, 4), ("x", "z", "core", "head"))
    placed = (
        P(SEQ, None),
        P(SEQ, "head"),
        P(SEQ, "head"),
        P(SEQ, "head"),
        P("head", SEQ),
        P(SEQ),
        P("head"),
    )
    return jax.shard_map(
        per_device, mesh=mesh, in_specs=placed, out_specs=P(SEQ, "head"), check_vma=False
    )
```

time: 227 us -> 132 us (0.58)
  waiting for transfers between devices: 94 us -> 22.5 us
  Pallas kernels: 0 us -> 56 us
  matrix products: 54.2 us -> 0 us
  starting transfers between devices: 0.04 us -> 43.3 us
  blocking collectives: 31.4 us -> 0 us
  local copies, waits for them, and re-layouts: 19 us -> 4.72 us
  between operations: 14.2 us -> 0.58 us
  other arithmetic: 13.3 us -> 4.87 us
    all_gather x2 -> x0, waiting for transfers between devices: 93.3 us -> none  [the longest x1 55.7 us: per_device(): lax.all_gather(value_weight, 'seq', axis=0, tiled=True)]
    pallas_call x0 -> x10, Pallas kernels: none -> 56 us  [the longest x3 25.8 us: mm(): pl.pallas_call(functools.partial(mm_kernel, jobs, ahead, acc is not None,...]
    dot_general x5 -> x0, matrix products: 54.2 us -> none  [the longest x1 22 us: per_device(): jnp.einsum('nh,nhef->hef', weights_sum, all_states, precision=lax.Precisi...]
    ppermute x0 -> x34, starting transfers between devices: none -> 43.3 us  [the longest x15 25.5 us: crossed(): return lax.ppermute(a, SEQ, pairs)]
    ppermute x0 -> x34, waiting for transfers between devices: none -> 22.5 us  [the longest x15 10.1 us: crossed(): return lax.ppermute(a, SEQ, pairs)]
    all_gather x1 -> x0, blocking collectives: 21 us -> none  [per_device(): lax.all_gather(carry_factor[None], 'seq', axis=0, tiled=True)]
    psum x1 -> x0, blocking collectives: 10.5 us -> none  [per_device(): square_total = lax.psum(local_squares, 'head')]
    unnamed x14 -> x20, local copies, waits for them, and re-layouts: 8.29 us -> 1.69 us
  transfers between devices with their start and end apart: 2 -> 34, of which waited for: 2 -> 14; matrix products, arithmetic and copies ran while one was open for 11% -> 5% of each run, Pallas kernels for 0% -> 27%
where the time goes in v1:
time: 132 us
  Pallas kernels  56 us (42%)
  starting transfers between devices  43.3 us (33%)
  waiting for transfers between devices  22.5 us (17%)
  other arithmetic  4.87 us (4%)
  local copies, waits for them, and re-layouts  4.72 us (4%)
    pallas_call x3, Pallas kernels, mm(): pl.pallas_call(functools.partial(mm_kernel, jobs, ahead, acc is not None,...  25.8 us
    ppermute x15, starting transfers between devices, crossed(): return lax.ppermute(a, SEQ, pairs)  25.5 us
    pallas_call x1, Pallas kernels, post(): pl.pallas_call(functools.partial(post_kernel, jobs), in_specs=[VM, VM, HB...  12.2 us
    pallas_call x1, Pallas kernels, pre(): pl.pallas_call(pre_kernel, in_specs=[VM, HB, HB], out_specs=[HB] * 2, out...  10.2 us
    ppermute x15, waiting for transfers between devices, crossed(): return lax.ppermute(a, SEQ, pairs)  10.1 us
    ppermute x4, waiting for transfers between devices, pair(): lax.ppermute(g, axis, [(i, i ^ bit) for i in range(4)])  7.54 us
    ppermute x4, starting transfers between devices, pair(): lax.ppermute(g, axis, [(i, i ^ bit) for i in range(4)])  6.76 us
    ppermute x3, starting transfers between devices, ring(): return lax.ppermute(a, axis, [(i, (i + step) % 4) for i in range(4)])  5.9 us
  transfers between devices with their start and end apart: 34, of which 14 were waited for; matrix products, arithmetic and copies ran while one was open for 5% of the time, Pallas kernels for 27%

profile of v1, /device:TPU:0, one launch (start us, length us, event | category | flops | bytes accessed | tf_op | source)
XLA Modules:
  0.0 132.0 jit_solution(4635122063376237797)
XLA Ops:
  2.7 2.1 %collective-permute-start.1 = (bf16[384,512]{1,0:T(8,128)(2,1)S(1)}, bf16[384,512]{1,0:T(8,128)(2,1)S(1)}, u32[]{:S(2)}, u32[]{:S(2)}) collective-permute-start(bf16[384,512]{1,0:T(8,128)(2,1)S(1)} %maximum_select_fusion), channel_id=1, source_target_pairs={{0,8},{4,36},{8,16},{12,44},{16,24},{20,52},{24,0},{28,60},{32,40}... | collective-permute-start | bytes 1179656 | tf_op jit(solution)/shard_map/ppermute | solution.py:40
  4.8 3.6 %collective-permute-start.2 = (bf16[384,512]{1,0:T(8,128)(2,1)S(1)}, bf16[384,512]{1,0:T(8,128)(2,1)S(1)}, u32[]{:S(2)}, u32[]{:S(2)}) collective-permute-start(bf16[384,512]{1,0:T(8,128)(2,1)S(1)} %maximum_select_fusion), channel_id=1, source_target_pairs={{0,16},{4,68},{8,24},{12,76},{16,0},{20,84},{24,8},{28,92},{32,48}... | collective-permute-start | bytes 1179656 | tf_op jit(solution)/shard_map/ppermute | solution.py:40
  11.1 10.2 %pre.1 = (bf16[8,4,256,256]{3,2,1,0:T(8,128)(2,1)}, bf16[1024,1024]{1,0:T(8,128)(2,1)}) custom-call(f32[8,1024]{1,0:T(8,128)S(1)} %copy-done, bf16[1024,1024]{1,0:T(8,128)(2,1)} %q_hbm.2, bf16[1024,1024]{1,0:T(8,128)(2,1)} %k_hbm), custom_call_target="tpu_custom_call" | custom-call | flops 1000000000 | bytes 10000000 | tf_op jit(solution)/shard_map/pre/pallas_call | solution.py:133
  22.4 2.5 %collective-permute-done.5 = f32[1,8]{1,0:T(1,128)S(1)} collective-permute-done((f32[1,8]{1,0:T(1,128)S(1)}, f32[1,8]{1,0:T(1,128)S(1)}, u32[]{:S(2)}, u32[]{:S(2)}) %collective-permute-start.5) | collective-permute-done | bytes 64 | tf_op jit(solution)/shard_map/ppermute | solution.py:498
  26.5 1.5 %collective-permute-start.6 = (bf16[768,512]{1,0:T(8,128)(2,1)S(1)}, bf16[768,512]{1,0:T(8,128)(2,1)}, u32[]{:S(2)}, u32[]{:S(2)}) collective-permute-start(bf16[768,512]{1,0:T(8,128)(2,1)S(1)} %constant_dynamic-update-slice_fusion.refs_0_), channel_id=1, source_target_pairs={{0,32},{4,12},{8,40},{12,20},{16,48},{20,28},{24,56},{28,4},{32,64... | collective-permute-start | bytes 2359304 | tf_op jit(solution)/shard_map/ppermute | solution.py:40
  28.0 1.7 %collective-permute-start.7 = (bf16[768,512]{1,0:T(8,128)(2,1)S(1)}, bf16[768,512]{1,0:T(8,128)(2,1)S(1)}, u32[]{:S(2)}, u32[]{:S(2)}) collective-permute-start(bf16[768,512]{1,0:T(8,128)(2,1)S(1)} %constant_dynamic-update-slice_fusion.2.refs_1_), channel_id=1, source_target_pairs={{0,96},{4,28},{8,104},{12,4},{16,112},{20,12},{24,120},{28,20},{32... | collective-permute-start | bytes 2359304 | tf_op jit(solution)/shard_map/ppermute | solution.py:40
  30.2 3.0 %collective-permute-start.11 = (bf16[768,512]{1,0:T(8,128)(2,1)S(1)}, bf16[768,512]{1,0:T(8,128)(2,1)}, u32[]{:S(2)}, u32[]{:S(2)}) collective-permute-start(bf16[768,512]{1,0:T(8,128)(2,1)S(1)} %constant_dynamic-update-slice_fusion.refs_0_), channel_id=1, source_target_pairs={{0,96},{4,28},{8,104},{12,4},{16,112},{20,12},{24,120},{28,20},{32... | collective-permute-start | bytes 2359304 | tf_op jit(solution)/shard_map/ppermute | solution.py:40
  33.1 7.5 %project.3 = (f32[1024,512]{1,0:T(8,128)}, f32[1024,512]{1,0:T(8,128)}) custom-call(bf16[1024,6144]{1,0:T(8,128)(2,1)} %x_hbm.5, bf16[768,512]{1,0:T(8,128)(2,1)} %copy-done.4, bf16[768,512]{1,0:T(8,128)(2,1)} %copy-done.3, bf16[768,512]{1,0:T(8,128)(2,1)} %collective-permute-done.8.refs_2_, bf16[768,512]{1,0:T(8,128)(2,1)} %collective-permute-done.9.refs_3_), custom_call_target="tpu_custom_call" | custom-call | flops 3221225472 | bytes 10000000 | tf_op jit(solution)/shard_map/project/pallas_call | solution.py:243
  40.9 1.3 multiply_bitcast_fusion
  43.7 2.4 %collective-permute-start.19 = (bf16[768,512]{1,0:T(8,128)(2,1)S(1)}, bf16[768,512]{1,0:T(8,128)(2,1)S(1)}, u32[]{:S(2)}, u32[]{:S(2)}) collective-permute-start(bf16[768,512]{1,0:T(8,128)(2,1)S(1)} %collective-permute-done.7.refs_3_), channel_id=1, source_target_pairs={{0,96},{4,28},{8,104},{12,4},{16,112},{20,12},{24,120},{28,20},{32... | collective-permute-start | bytes 2359304 | tf_op jit(solution)/shard_map/ppermute | solution.py:40
  46.2 2.1 %collective-permute-done.10.refs_1_ = bf16[768,512]{1,0:T(8,128)(2,1)} collective-permute-done((bf16[768,512]{1,0:T(8,128)(2,1)S(1)}, bf16[768,512]{1,0:T(8,128)(2,1)}, u32[]{:S(2)}, u32[]{:S(2)}) %collective-permute-start.10) | collective-permute-done | bytes 786464 | tf_op jit(solution)/shard_map/ppermute | solution.py:40
  48.3 2.7 %collective-permute-start.12 = (f32[2,8]{1,0:T(2,128)S(1)}, f32[2,8]{1,0:T(2,128)S(1)}, u32[]{:S(2)}, u32[]{:S(2)}) collective-permute-start(f32[2,8]{1,0:T(2,128)S(1)} %pad_maximum_fusion.4), channel_id=1, source_target_pairs={{0,16},{8,24},{16,0},{24,8},{1,17},{9,25},{17,1},{25,9},{2,18},{10... | collective-permute-start | bytes 200 | tf_op jit(solution)/shard_map/ppermute | solution.py:498
  50.9 2.5 %collective-permute-done.12 = f32[2,8]{1,0:T(2,128)S(1)} collective-permute-done((f32[2,8]{1,0:T(2,128)S(1)}, f32[2,8]{1,0:T(2,128)S(1)}, u32[]{:S(2)}, u32[]{:S(2)}) %collective-permute-start.12) | collective-permute-done | bytes 96 | tf_op jit(solution)/shard_map/ppermute | solution.py:498
  53.4 3.3 %collective-permute-start.14 = (bf16[768,512]{1,0:T(8,128)(2,1)}, bf16[768,512]{1,0:T(8,128)(2,1)S(1)}, u32[]{:S(2)}, u32[]{:S(2)}) collective-permute-start(bf16[768,512]{1,0:T(8,128)(2,1)} %collective-permute-done.10.refs_1_), channel_id=1, source_target_pairs={{0,4},{4,0},{1,5},{5,1},{2,6},{6,2},{3,7},{7,3},{8,12},{12,8},{9,1... | collective-permute-start | bytes 2359304 | tf_op jit(solution)/shard_map/ppermute | solution.py:24
  56.9 8.2 %project.4.mine_ref = f32[1024,512]{1,0:T(8,128)S(1)} custom-call(bf16[1024,6144]{1,0:T(8,128)(2,1)} %x_hbm.5, bf16[768,512]{1,0:T(8,128)(2,1)} %collective-permute-done.6.refs_0_, bf16[768,512]{1,0:T(8,128)(2,1)} %collective-permute-done.10.refs_1_, bf16[768,512]{1,0:T(8,128)(2,1)} %collective-permute-done.11.refs_2_, bf16[768,512]{1,0:T(8,128)(2,1)} %copy-done.5, ...), custom_call_target="tpu_custom_call" | custom-call | flops 3221225472 | bytes 10000000 | tf_op jit(solution)/shard_map/project/pallas_call | solution.py:243
  67.5 10.1 %project.5 = (f32[1024,512]{1,0:T(8,128)S(1)}, bf16[2,1024,1536]{2,1,0:T(8,128)(2,1)S(1)}) custom-call(bf16[1024,6144]{1,0:T(8,128)(2,1)} %x_hbm.5, bf16[768,512]{1,0:T(8,128)(2,1)} %collective-permute-done.13.refs_0_, bf16[768,512]{1,0:T(8,128)(2,1)} %copy-done.7, bf16[768,512]{1,0:T(8,128)(2,1)} %copy-done.8, bf16[768,512]{1,0:T(8,128)(2,1)} %copy-done.6, ...), custom_call_target="tpu_custom_call" | custom-call | flops 3221225472 | bytes 10000000 | tf_op jit(solution)/shard_map/project/pallas_call | solution.py:243
  77.8 2.5 %collective-permute-start.22 = (f32[8,8]{1,0:T(8,128)S(1)}, f32[8,8]{1,0:T(8,128)S(1)}, u32[]{:S(2)}, u32[]{:S(2)}) collective-permute-start(f32[8,8]{1,0:T(8,128)S(1)} %pad_maximum_fusion.1), channel_id=1, source_target_pairs={{0,64},{32,96},{64,0},{96,32},{1,65},{33,97},{65,1},{97,33},{2,66}... | collective-permute-start | bytes 776 | tf_op jit(solution)/shard_map/ppermute | solution.py:498
  80.4 2.5 %collective-permute-done.22 = f32[8,8]{1,0:T(8,128)S(1)} collective-permute-done((f32[8,8]{1,0:T(8,128)S(1)}, f32[8,8]{1,0:T(8,128)S(1)}, u32[]{:S(2)}, u32[]{:S(2)}) %collective-permute-start.22) | collective-permute-done | bytes 288 | tf_op jit(solution)/shard_map/ppermute | solution.py:498
  83.0 12.2 %post.1 = (f32[1024,1024]{1,0:T(8,128)}, f32[512,128]{1,0:T(8,128)S(1)}, f32[512,128]{1,0:T(8,128)S(1)}) custom-call(f32[40,128]{1,0:T(8,128)S(1)} %broadcast.437.dec, f32[8,1024]{1,0:T(8,128)S(1)} %copy-done.1, bf16[1024,1024]{1,0:T(8,128)(2,1)} %q_hbm.2, bf16[1024,1024]{1,0:T(8,128)(2,1)} %get-tuple-element.79.kd_hbm, ...), custom_call_target="tpu_custom_call" | custom-call | tf_op jit(solution)/shard_map/post/pallas_call | solution.py:317
  97.9 1.7 %collective-permute-start.25 = (bf16[512,128]{1,0:T(8,128)(2,1)S(1)}, bf16[512,128]{1,0:T(8,128)(2,1)S(1)}, u32[]{:S(2)}, u32[]{:S(2)}) collective-permute-start(bf16[512,128]{1,0:T(8,128)(2,1)S(1)} %get-tuple-element.91), channel_id=1, source_target_pairs={{0,16},{4,68},{8,24},{12,76},{16,0},{20,84},{24,8},{28,92},{32,48}... | collective-permute-start | bytes 393224 | tf_op jit(solution)/shard_map/ppermute | solution.py:40
  100.9 2.2 %collective-permute-done.24.r1 = bf16[512,128]{1,0:T(8,128)(2,1)S(1)} collective-permute-done((bf16[512,128]{1,0:T(8,128)(2,1)S(1)}, bf16[512,128]{1,0:T(8,128)(2,1)S(1)}, u32[]{:S(2)}, u32[]{:S(2)}) %collective-permute-start.24) | collective-permute-done | bytes 131104 | tf_op jit(solution)/shard_map/ppermute | solution.py:40
  103.1 1.4 %collective-permute-done.25.r2 = bf16[512,128]{1,0:T(8,128)(2,1)S(1)} collective-permute-done((bf16[512,128]{1,0:T(8,128)(2,1)S(1)}, bf16[512,128]{1,0:T(8,128)(2,1)S(1)}, u32[]{:S(2)}, u32[]{:S(2)}) %collective-permute-start.25) | collective-permute-done | bytes 131104 | tf_op jit(solution)/shard_map/ppermute | solution.py:40
  106.6 2.9 %collective-permute-start.28 = (bf16[512,128]{1,0:T(8,128)(2,1)S(1)}, bf16[512,128]{1,0:T(8,128)(2,1)S(1)}, u32[]{:S(2)}, u32[]{:S(2)}) collective-permute-start(bf16[512,128]{1,0:T(8,128)(2,1)S(1)} %get-tuple-element.94), channel_id=1, source_target_pairs={{0,64},{4,20},{8,72},{12,28},{16,80},{20,4},{24,88},{28,12},{32,96... | collective-permute-start | bytes 393224 | tf_op jit(solution)/shard_map/ppermute | solution.py:40
  109.5 1.4 %collective-permute-start.29 = (bf16[512,128]{1,0:T(8,128)(2,1)S(1)}, bf16[512,128]{1,0:T(8,128)(2,1)S(1)}, u32[]{:S(2)}, u32[]{:S(2)}) collective-permute-start(bf16[512,128]{1,0:T(8,128)(2,1)S(1)} %get-tuple-element.95), channel_id=1, source_target_pairs={{0,96},{4,28},{8,104},{12,4},{16,112},{20,12},{24,120},{28,20},{32... | collective-permute-start | bytes 393224 | tf_op jit(solution)/shard_map/ppermute | solution.py:40
  112.0 1.9 %collective-permute-done.28.r2 = bf16[512,128]{1,0:T(8,128)(2,1)S(1)} collective-permute-done((bf16[512,128]{1,0:T(8,128)(2,1)S(1)}, bf16[512,128]{1,0:T(8,128)(2,1)S(1)}, u32[]{:S(2)}, u32[]{:S(2)}) %collective-permute-start.28) | collective-permute-done | bytes 131104 | tf_op jit(solution)/shard_map/ppermute | solution.py:40
  114.7 1.5 %collective-permute-done.30.other_ref = f32[512,128]{1,0:T(8,128)S(1)} collective-permute-done((f32[512,128]{1,0:T(8,128)S(1)}, f32[512,128]{1,0:T(8,128)S(1)}, u32[]{:S(2)}, u32[]{:S(2)}) %collective-permute-start.30) | collective-permute-done | bytes 262176 | tf_op jit(solution)/shard_map/ppermute | solution.py:24
  116.2 5.8 %outer.1 = (f32[1024,1024]{1,0:T(8,128)S(1)}, f32[8,128]{1,0:T(8,128)S(1)}) custom-call(f32[4,8]{1,0:T(4,128)S(1)} %pad_maximum_fusion.3.sf, f32[8,1024]{1,0:T(8,128)S(1)} %copy-done.1, f32[512,128]{1,0:T(8,128)S(1)} %get-tuple-element.96.mine_ref, f32[512,128]{1,0:T(8,128)S(1)} %collective-permute-done.30.other_ref, bf16[1024,1024]{1,0:T(8,128)(2,1)} %q_hbm.2, ...), custom_call_target="tpu_custom_call" | custom-call | tf_op jit(solution)/shard_map/outer/pallas_call | solution.py:424
  122.1 1.6 %collective-permute-start.31 = (f32[8,128]{1,0:T(8,128)S(1)}, f32[8,128]{1,0:T(8,128)S(1)}, u32[]{:S(2)}, u32[]{:S(2)}) collective-permute-start(f32[8,128]{1,0:T(8,128)S(1)} %get-tuple-element.100.s0), channel_id=1, source_target_pairs={{0,1},{1,2},{2,3},{3,0},{4,5},{5,6},{6,7},{7,4},{8,9},{9,10},{10,1... | collective-permute-start | bytes 12296 | tf_op jit(solution)/shard_map/ppermute | solution.py:28
  123.7 2.9 %collective-permute-start.32 = (f32[8,128]{1,0:T(8,128)S(1)}, f32[8,128]{1,0:T(8,128)S(1)}, u32[]{:S(2)}, u32[]{:S(2)}) collective-permute-start(f32[8,128]{1,0:T(8,128)S(1)} %get-tuple-element.100.s0), channel_id=1, source_target_pairs={{0,2},{1,3},{2,0},{3,1},{4,6},{5,7},{6,4},{7,5},{8,10},{9,11},{10,... | collective-permute-start | bytes 12296 | tf_op jit(solution)/shard_map/ppermute | solution.py:28
  126.6 1.3 %collective-permute-start.33 = (f32[8,128]{1,0:T(8,128)S(1)}, f32[8,128]{1,0:T(8,128)S(1)}, u32[]{:S(2)}, u32[]{:S(2)}) collective-permute-start(f32[8,128]{1,0:T(8,128)S(1)} %get-tuple-element.100.s0), channel_id=1, source_target_pairs={{0,3},{1,0},{2,1},{3,2},{4,7},{5,4},{6,5},{7,6},{8,11},{9,8},{10,9... | collective-permute-start | bytes 12296 | tf_op jit(solution)/shard_map/ppermute | solution.py:28
  128.8 1.4 %collective-permute-done.33.s3 = f32[8,128]{1,0:T(8,128)S(1)} collective-permute-done((f32[8,128]{1,0:T(8,128)S(1)}, f32[8,128]{1,0:T(8,128)S(1)}, u32[]{:S(2)}, u32[]{:S(2)}) %collective-permute-start.33) | collective-permute-done | bytes 4128 | tf_op jit(solution)/shard_map/ppermute | solution.py:28
  130.2 1.6 %norm.1 = bf16[1024,1024]{1,0:T(8,128)(2,1)} custom-call(f32[1024,1024]{1,0:T(8,128)S(1)} %get-tuple-element.99.out_ref, f32[8,128]{1,0:T(8,128)S(1)} %get-tuple-element.100.s0, f32[8,128]{1,0:T(8,128)S(1)} %collective-permute-done.31.s1, f32[8,128]{1,0:T(8,128)S(1)} %collective-permute-done.32.s2, f32[8,128]{1,0:T(8,128)S(1)} %collective-permute-done.33.s3, ...), custom_call_target="tpu_custom_call" | custom-call | tf_op jit(solution)/shard_map/norm/pallas_call | solution.py:457
  (111 shorter events, 21.8 us)
Async XLA Ops:
  2.7 22.2 %collective-permute-start.1 = (bf16[384,512]{1,0:T(8,128)(2,1)S(1)}, bf16[384,512]{1,0:T(8,128)(2,1)S(1)}, u32[]{:S(2)}, u32[]{:S(2)}) collective-permute-start(bf16[384,512]{1,0:T(8,128)(2,1)S(1)} %maximum_select_fusion), channel_id=1, source_target_pairs={{0,8},{4,36},{8,16},{12,44},{16,24},{20,52},{24,0},{28,60},{32,40}... | collective-permute-start | bytes 1179656 | tf_op jit(solution)/shard_map/ppermute | solution.py:40
  4.8 20.2 %collective-permute-start.2 = (bf16[384,512]{1,0:T(8,128)(2,1)S(1)}, bf16[384,512]{1,0:T(8,128)(2,1)S(1)}, u32[]{:S(2)}, u32[]{:S(2)}) collective-permute-start(bf16[384,512]{1,0:T(8,128)(2,1)S(1)} %maximum_select_fusion), channel_id=1, source_target_pairs={{0,16},{4,68},{8,24},{12,76},{16,0},{20,84},{24,8},{28,92},{32,48}... | collective-permute-start | bytes 1179656 | tf_op jit(solution)/shard_map/ppermute | solution.py:40
  8.4 16.6 %collective-permute-start.3 = (bf16[384,512]{1,0:T(8,128)(2,1)S(1)}, bf16[384,512]{1,0:T(8,128)(2,1)S(1)}, u32[]{:S(2)}, u32[]{:S(2)}) collective-permute-start(bf16[384,512]{1,0:T(8,128)(2,1)S(1)} %maximum_select_fusion), channel_id=1, source_target_pairs={{0,24},{4,100},{8,0},{12,108},{16,8},{20,116},{24,16},{28,124},{32... | collective-permute-start | bytes 1179656 | tf_op jit(solution)/shard_map/ppermute | solution.py:40
  10.3 11.0 %collective-permute-start.4 = (f32[8]{0:T(128)S(1)}, f32[8]{0:T(128)S(1)}, u32[]{:S(2)}, u32[]{:S(2)}) collective-permute-start(f32[8]{0:T(128)S(1)} %get-tuple-element.101), channel_id=1, source_target_pairs={{0,4},{4,0},{1,5},{5,1},{2,6},{6,2},{3,7},{7,3},{8,12},{12,8},{9,1... | collective-permute-start | bytes 104 | tf_op jit(solution)/shard_map/ppermute | solution.py:24
  21.3 3.6 %collective-permute-start.5 = (f32[1,8]{1,0:T(1,128)S(1)}, f32[1,8]{1,0:T(1,128)S(1)}, u32[]{:S(2)}, u32[]{:S(2)}) collective-permute-start(f32[1,8]{1,0:T(1,128)S(1)} %multiply_bitcast_fusion.3), channel_id=1, source_target_pairs={{0,8},{8,0},{16,24},{24,16},{1,9},{9,1},{17,25},{25,17},{2,10},{10... | collective-permute-start | bytes 104 | tf_op jit(solution)/shard_map/ppermute | solution.py:498
  25.1 5.1 %collective-permute-start.8 = (bf16[768,512]{1,0:T(8,128)(2,1)S(1)}, bf16[768,512]{1,0:T(8,128)(2,1)}, u32[]{:S(2)}, u32[]{:S(2)}) collective-permute-start(bf16[768,512]{1,0:T(8,128)(2,1)S(1)} %constant_dynamic-update-slice_fusion.refs_0_), channel_id=1, source_target_pairs={{0,4},{4,0},{1,5},{5,1},{2,6},{6,2},{3,7},{7,3},{8,12},{12,8},{9,1... | collective-permute-start | bytes 2359304 | tf_op jit(solution)/shard_map/ppermute | solution.py:24
  25.2 7.9 %collective-permute-start.9 = (bf16[768,512]{1,0:T(8,128)(2,1)S(1)}, bf16[768,512]{1,0:T(8,128)(2,1)}, u32[]{:S(2)}, u32[]{:S(2)}) collective-permute-start(bf16[768,512]{1,0:T(8,128)(2,1)S(1)} %constant_dynamic-update-slice_fusion.2.refs_1_), channel_id=1, source_target_pairs={{0,4},{4,0},{1,5},{5,1},{2,6},{6,2},{3,7},{7,3},{8,12},{12,8},{9,1... | collective-permute-start | bytes 2359304 | tf_op jit(solution)/shard_map/ppermute | solution.py:24
  26.5 14.1 %collective-permute-start.6 = (bf16[768,512]{1,0:T(8,128)(2,1)S(1)}, bf16[768,512]{1,0:T(8,128)(2,1)}, u32[]{:S(2)}, u32[]{:S(2)}) collective-permute-start(bf16[768,512]{1,0:T(8,128)(2,1)S(1)} %constant_dynamic-update-slice_fusion.refs_0_), channel_id=1, source_target_pairs={{0,32},{4,12},{8,40},{12,20},{16,48},{20,28},{24,56},{28,4},{32,64... | collective-permute-start | bytes 2359304 | tf_op jit(solution)/shard_map/ppermute | solution.py:40
  28.0 12.6 %collective-permute-start.7 = (bf16[768,512]{1,0:T(8,128)(2,1)S(1)}, bf16[768,512]{1,0:T(8,128)(2,1)S(1)}, u32[]{:S(2)}, u32[]{:S(2)}) collective-permute-start(bf16[768,512]{1,0:T(8,128)(2,1)S(1)} %constant_dynamic-update-slice_fusion.2.refs_1_), channel_id=1, source_target_pairs={{0,96},{4,28},{8,104},{12,4},{16,112},{20,12},{24,120},{28,20},{32... | collective-permute-start | bytes 2359304 | tf_op jit(solution)/shard_map/ppermute | solution.py:40
  29.9 18.4 %collective-permute-start.10 = (bf16[768,512]{1,0:T(8,128)(2,1)S(1)}, bf16[768,512]{1,0:T(8,128)(2,1)}, u32[]{:S(2)}, u32[]{:S(2)}) collective-permute-start(bf16[768,512]{1,0:T(8,128)(2,1)S(1)} %constant_dynamic-update-slice_fusion.2.refs_1_), channel_id=1, source_target_pairs={{0,32},{4,12},{8,40},{12,20},{16,48},{20,28},{24,56},{28,4},{32,64... | collective-permute-start | bytes 2359304 | tf_op jit(solution)/shard_map/ppermute | solution.py:40
  30.2 20.8 %collective-permute-start.11 = (bf16[768,512]{1,0:T(8,128)(2,1)S(1)}, bf16[768,512]{1,0:T(8,128)(2,1)}, u32[]{:S(2)}, u32[]{:S(2)}) collective-permute-start(bf16[768,512]{1,0:T(8,128)(2,1)S(1)} %constant_dynamic-update-slice_fusion.refs_0_), channel_id=1, source_target_pairs={{0,96},{4,28},{8,104},{12,4},{16,112},{20,12},{24,120},{28,20},{32... | collective-permute-start | bytes 2359304 | tf_op jit(solution)/shard_map/ppermute | solution.py:40
  40.6 16.1 %collective-permute-start.13 = (bf16[768,512]{1,0:T(8,128)(2,1)}, bf16[768,512]{1,0:T(8,128)(2,1)}, u32[]{:S(2)}, u32[]{:S(2)}) collective-permute-start(bf16[768,512]{1,0:T(8,128)(2,1)} %collective-permute-done.6.refs_0_), channel_id=1, source_target_pairs={{0,4},{4,0},{1,5},{5,1},{2,6},{6,2},{3,7},{7,3},{8,12},{12,8},{9,1... | collective-permute-start | bytes 2359304 | tf_op jit(solution)/shard_map/ppermute | solution.py:24
  42.9 22.3 %collective-permute-start.18 = (bf16[768,512]{1,0:T(8,128)(2,1)}, bf16[768,512]{1,0:T(8,128)(2,1)S(1)}, u32[]{:S(2)}, u32[]{:S(2)}) collective-permute-start(bf16[768,512]{1,0:T(8,128)(2,1)} %collective-permute-done.6.refs_0_), channel_id=1, source_target_pairs={{0,32},{4,12},{8,40},{12,20},{16,48},{20,28},{24,56},{28,4},{32,64... | collective-permute-start | bytes 2359304 | tf_op jit(solution)/shard_map/ppermute | solution.py:40
  43.7 22.2 %collective-permute-start.19 = (bf16[768,512]{1,0:T(8,128)(2,1)S(1)}, bf16[768,512]{1,0:T(8,128)(2,1)S(1)}, u32[]{:S(2)}, u32[]{:S(2)}) collective-permute-start(bf16[768,512]{1,0:T(8,128)(2,1)S(1)} %collective-permute-done.7.refs_3_), channel_id=1, source_target_pairs={{0,96},{4,28},{8,104},{12,4},{16,112},{20,12},{24,120},{28,20},{32... | collective-permute-start | bytes 2359304 | tf_op jit(solution)/shard_map/ppermute | solution.py:40
  48.3 5.2 %collective-permute-start.12 = (f32[2,8]{1,0:T(2,128)S(1)}, f32[2,8]{1,0:T(2,128)S(1)}, u32[]{:S(2)}, u32[]{:S(2)}) collective-permute-start(f32[2,8]{1,0:T(2,128)S(1)} %pad_maximum_fusion.4), channel_id=1, source_target_pairs={{0,16},{8,24},{16,0},{24,8},{1,17},{9,25},{17,1},{25,9},{2,18},{10... | collective-permute-start | bytes 200 | tf_op jit(solution)/shard_map/ppermute | solution.py:498
  50.9 15.2 %collective-permute-start.16 = (bf16[768,512]{1,0:T(8,128)(2,1)S(1)}, bf16[768,512]{1,0:T(8,128)(2,1)S(1)}, u32[]{:S(2)}, u32[]{:S(2)}) collective-permute-start(bf16[768,512]{1,0:T(8,128)(2,1)S(1)} %collective-permute-done.7.refs_3_), channel_id=1, source_target_pairs={{0,4},{4,0},{1,5},{5,1},{2,6},{6,2},{3,7},{7,3},{8,12},{12,8},{9,1... | collective-permute-start | bytes 2359304 | tf_op jit(solution)/shard_map/ppermute | solution.py:24
  53.4 12.6 %collective-permute-start.14 = (bf16[768,512]{1,0:T(8,128)(2,1)}, bf16[768,512]{1,0:T(8,128)(2,1)S(1)}, u32[]{:S(2)}, u32[]{:S(2)}) collective-permute-start(bf16[768,512]{1,0:T(8,128)(2,1)} %collective-permute-done.10.refs_1_), channel_id=1, source_target_pairs={{0,4},{4,0},{1,5},{5,1},{2,6},{6,2},{3,7},{7,3},{8,12},{12,8},{9,1... | collective-permute-start | bytes 2359304 | tf_op jit(solution)/shard_map/ppermute | solution.py:24
  56.7 9.4 %collective-permute-start.15 = (bf16[768,512]{1,0:T(8,128)(2,1)}, bf16[768,512]{1,0:T(8,128)(2,1)S(1)}, u32[]{:S(2)}, u32[]{:S(2)}) collective-permute-start(bf16[768,512]{1,0:T(8,128)(2,1)} %collective-permute-done.11.refs_2_), channel_id=1, source_target_pairs={{0,4},{4,0},{1,5},{5,1},{2,6},{6,2},{3,7},{7,3},{8,12},{12,8},{9,1... | collective-permute-start | bytes 2359304 | tf_op jit(solution)/shard_map/ppermute | solution.py:24
  65.2 17.8 %collective-permute-start.20 = (bf16[768,512]{1,0:T(8,128)(2,1)S(1)}, bf16[768,512]{1,0:T(8,128)(2,1)S(1)}, u32[]{:S(2)}, u32[]{:S(2)}) collective-permute-start(bf16[768,512]{1,0:T(8,128)(2,1)S(1)} %collective-permute-done.18.refs_0_), channel_id=1, source_target_pairs={{0,4},{4,0},{1,5},{5,1},{2,6},{6,2},{3,7},{7,3},{8,12},{12,8},{9,1... | collective-permute-start | bytes 2359304 | tf_op jit(solution)/shard_map/ppermute | solution.py:24
  65.9 17.0 %collective-permute-start.21 = (bf16[768,512]{1,0:T(8,128)(2,1)S(1)}, bf16[768,512]{1,0:T(8,128)(2,1)S(1)}, u32[]{:S(2)}, u32[]{:S(2)}) collective-permute-start(bf16[768,512]{1,0:T(8,128)(2,1)S(1)} %collective-permute-done.19.refs_1_), channel_id=1, source_target_pairs={{0,4},{4,0},{1,5},{5,1},{2,6},{6,2},{3,7},{7,3},{8,12},{12,8},{9,1... | collective-permute-start | bytes 2359304 | tf_op jit(solution)/shard_map/ppermute | solution.py:24
  66.1 11.5 %collective-permute-start.17 = (f32[4,8]{1,0:T(4,128)S(1)}, f32[4,8]{1,0:T(4,128)S(1)}, u32[]{:S(2)}, u32[]{:S(2)}) collective-permute-start(f32[4,8]{1,0:T(4,128)S(1)} %pad_maximum_fusion.2), channel_id=1, source_target_pairs={{0,32},{32,0},{64,96},{96,64},{1,33},{33,1},{65,97},{97,65},{2,34}... | collective-permute-start | bytes 392 | tf_op jit(solution)/shard_map/ppermute | solution.py:498
  77.8 5.1 %collective-permute-start.22 = (f32[8,8]{1,0:T(8,128)S(1)}, f32[8,8]{1,0:T(8,128)S(1)}, u32[]{:S(2)}, u32[]{:S(2)}) collective-permute-start(f32[8,8]{1,0:T(8,128)S(1)} %pad_maximum_fusion.1), channel_id=1, source_target_pairs={{0,64},{32,96},{64,0},{96,32},{1,65},{33,97},{65,1},{97,33},{2,66}... | collective-permute-start | bytes 776 | tf_op jit(solution)/shard_map/ppermute | solution.py:498
  95.2 1.6 %collective-permute-start.23 = (f32[512,128]{1,0:T(8,128)S(1)}, f32[512,128]{1,0:T(8,128)S(1)}, u32[]{:S(2)}, u32[]{:S(2)}) collective-permute-start(f32[512,128]{1,0:T(8,128)S(1)} %get-tuple-element.89), channel_id=1, source_target_pairs={{0,4},{4,0},{1,5},{5,1},{2,6},{6,2},{3,7},{7,3},{8,12},{12,8},{9,1... | collective-permute-start | bytes 786440 | tf_op jit(solution)/shard_map/ppermute | solution.py:24
  96.9 6.3 %collective-permute-start.24 = (bf16[512,128]{1,0:T(8,128)(2,1)S(1)}, bf16[512,128]{1,0:T(8,128)(2,1)S(1)}, u32[]{:S(2)}, u32[]{:S(2)}) collective-permute-start(bf16[512,128]{1,0:T(8,128)(2,1)S(1)} %get-tuple-element.91), channel_id=1, source_target_pairs={{0,8},{4,36},{8,16},{12,44},{16,24},{20,52},{24,0},{28,60},{32,40}... | collective-permute-start | bytes 393224 | tf_op jit(solution)/shard_map/ppermute | solution.py:40
  97.9 6.6 %collective-permute-start.25 = (bf16[512,128]{1,0:T(8,128)(2,1)S(1)}, bf16[512,128]{1,0:T(8,128)(2,1)S(1)}, u32[]{:S(2)}, u32[]{:S(2)}) collective-permute-start(bf16[512,128]{1,0:T(8,128)(2,1)S(1)} %get-tuple-element.91), channel_id=1, source_target_pairs={{0,16},{4,68},{8,24},{12,76},{16,0},{20,84},{24,8},{28,92},{32,48}... | collective-permute-start | bytes 393224 | tf_op jit(solution)/shard_map/ppermute | solution.py:40
  99.6 5.7 %collective-permute-start.26 = (bf16[512,128]{1,0:T(8,128)(2,1)S(1)}, bf16[512,128]{1,0:T(8,128)(2,1)S(1)}, u32[]{:S(2)}, u32[]{:S(2)}) collective-permute-start(bf16[512,128]{1,0:T(8,128)(2,1)S(1)} %get-tuple-element.91), channel_id=1, source_target_pairs={{0,24},{4,100},{8,0},{12,108},{16,8},{20,116},{24,16},{28,124},{32... | collective-permute-start | bytes 393224 | tf_op jit(solution)/shard_map/ppermute | solution.py:40
  105.7 6.2 %collective-permute-start.27 = (bf16[512,128]{1,0:T(8,128)(2,1)S(1)}, bf16[512,128]{1,0:T(8,128)(2,1)S(1)}, u32[]{:S(2)}, u32[]{:S(2)}) collective-permute-start(bf16[512,128]{1,0:T(8,128)(2,1)S(1)} %get-tuple-element.93), channel_id=1, source_target_pairs={{0,32},{4,12},{8,40},{12,20},{16,48},{20,28},{24,56},{28,4},{32,64... | collective-permute-start | bytes 393224 | tf_op jit(solution)/shard_map/ppermute | solution.py:40
  106.6 7.3 %collective-permute-start.28 = (bf16[512,128]{1,0:T(8,128)(2,1)S(1)}, bf16[512,128]{1,0:T(8,128)(2,1)S(1)}, u32[]{:S(2)}, u32[]{:S(2)}) collective-permute-start(bf16[512,128]{1,0:T(8,128)(2,1)S(1)} %get-tuple-element.94), channel_id=1, source_target_pairs={{0,64},{4,20},{8,72},{12,28},{16,80},{20,4},{24,88},{28,12},{32,96... | collective-permute-start | bytes 393224 | tf_op jit(solution)/shard_map/ppermute | solution.py:40
  109.5 5.0 %collective-permute-start.29 = (bf16[512,128]{1,0:T(8,128)(2,1)S(1)}, bf16[512,128]{1,0:T(8,128)(2,1)S(1)}, u32[]{:S(2)}, u32[]{:S(2)}) collective-permute-start(bf16[512,128]{1,0:T(8,128)(2,1)S(1)} %get-tuple-element.95), channel_id=1, source_target_pairs={{0,96},{4,28},{8,104},{12,4},{16,112},{20,12},{24,120},{28,20},{32... | collective-permute-start | bytes 393224 | tf_op jit(solution)/shard_map/ppermute | solution.py:40
  122.1 5.9 %collective-permute-start.31 = (f32[8,128]{1,0:T(8,128)S(1)}, f32[8,128]{1,0:T(8,128)S(1)}, u32[]{:S(2)}, u32[]{:S(2)}) collective-permute-start(f32[8,128]{1,0:T(8,128)S(1)} %get-tuple-element.100.s0), channel_id=1, source_target_pairs={{0,1},{1,2},{2,3},{3,0},{4,5},{5,6},{6,7},{7,4},{8,9},{9,10},{10,1... | collective-permute-start | bytes 12296 | tf_op jit(solution)/shard_map/ppermute | solution.py:28
  123.7 5.1 %collective-permute-start.32 = (f32[8,128]{1,0:T(8,128)S(1)}, f32[8,128]{1,0:T(8,128)S(1)}, u32[]{:S(2)}, u32[]{:S(2)}) collective-permute-start(f32[8,128]{1,0:T(8,128)S(1)} %get-tuple-element.100.s0), channel_id=1, source_target_pairs={{0,2},{1,3},{2,0},{3,1},{4,6},{5,7},{6,4},{7,5},{8,10},{9,11},{10,... | collective-permute-start | bytes 12296 | tf_op jit(solution)/shard_map/ppermute | solution.py:28
  126.6 3.6 %collective-permute-start.33 = (f32[8,128]{1,0:T(8,128)S(1)}, f32[8,128]{1,0:T(8,128)S(1)}, u32[]{:S(2)}, u32[]{:S(2)}) collective-permute-start(f32[8,128]{1,0:T(8,128)S(1)} %get-tuple-element.100.s0), channel_id=1, source_target_pairs={{0,3},{1,0},{2,1},{3,2},{4,7},{5,4},{6,5},{7,6},{8,11},{9,8},{10,9... | collective-permute-start | bytes 12296 | tf_op jit(solution)/shard_map/ppermute | solution.py:28
  (11 other events, 70.4 us)

commit v2 on v1

v2 whole, which is shorter than its diff:
```python
import functools
import jax
import jax.numpy as jnp
from jax import lax
from jax.experimental import pallas as pl
from jax.experimental.pallas import tpu as pltpu
from jax.sharding import Mesh, PartitionSpec as P

SHARD_ATTN_PARTS = 32
E = 128
SPAN = 256
SEQ = ("x", "z", "core")
SWAP = [(0, 1), (1, 0)]
VM = pl.BlockSpec(memory_space=pltpu.VMEM)
HB = pl.BlockSpec(memory_space=pltpu.HBM)
MIB = 1024 * 1024
HALF = 512
LINE = 1536
CHIP = 384
ROOM = 2
ROOM_P = 4
f32, bf16 = jnp.float32, jnp.bfloat16


def swap(a):
    return lax.ppermute(a, "core", SWAP)


def ring(a, axis, step):
    return lax.ppermute(a, axis, [(i, (i + step) % 4) for i in range(4)])


def crossed(a, first, second, step0, step1):
    pairs = []
    for x in range(4):
        for z in range(4):
            for c in range(2):
                axis, step = ((first, step0), (second, step1))[c]
                tx = (x + step) % 4 if axis == "x" else x
                tz = (z + step) % 4 if axis == "z" else z
                pairs.append((x * 8 + z * 2 + c, tx * 8 + tz * 2 + c))
    return lax.ppermute(a, SEQ, pairs)


def dot(a, b, dims=((1,), (0,))):
    return lax.dot_general(a, b, (dims, ((), ())), preferred_element_type=f32)


def block_cum(ld):
    lane = lax.broadcasted_iota(jnp.int32, ld.shape, 1)
    step = 1
    while step < SPAN:
        ld = ld + jnp.where(lane >= step, pltpu.roll(ld, step, 1), 0.0)
        step *= 2
    return ld


def vmem(a):
    return pltpu.with_memory_space_constraint(a, pltpu.VMEM)


def hbm(a):
    return pltpu.with_memory_space_constraint(a, pltpu.HBM)


def params(mib):
    return pltpu.CompilerParams(vmem_limit_bytes=mib * MIB)


def prep_kernel(doc, ld_ref, fx_ref, dec_ref, sf_ref):
    lane = lax.broadcasted_iota(jnp.int32, (E, E), 1)
    mat = jnp.zeros((E, E), f32)
    surv = []
    for b in range(4):
        total = jnp.sum(ld_ref[:, b * SPAN : (b + 1) * SPAN], axis=1, keepdims=True)
        decay = jnp.broadcast_to(jnp.exp(total), (8, E))
        dec_ref[b * 8 : b * 8 + 8, :] = decay
        tall = jnp.concatenate([decay, jnp.zeros((E - 8, E), f32)], axis=0)
        mat = jnp.where(lane == b, tall, mat)
        surv.append(1.0 - jnp.full((1, E), doc[b], jnp.int32).astype(f32))
    dec_ref[32:40, :] = jnp.concatenate(surv + [jnp.zeros((4, E), f32)], axis=0)
    rows = jnp.transpose(mat)
    f = None
    sfs = []
    for b in range(4):
        f = surv[b] if b == 0 else f * surv[b]
        sfs.append(f)
        f = f * rows[b : b + 1, :]
    sf_ref[...] = jnp.concatenate(sfs + [jnp.zeros((4, E), f32)], axis=0)
    high = f.astype(bf16).astype(f32)
    mid = (f - high).astype(bf16).astype(f32)
    low = f - high - mid
    tile = jnp.concatenate([high, mid, low, jnp.zeros((13, E), f32)], axis=0)
    fx_ref[:, E:] = jnp.zeros((16, HALF - E), bf16)
    fx_ref[:, :E] = tile.astype(bf16)


def prep(doc, ld):
    return pl.pallas_call(
        prep_kernel,
        in_specs=[pl.BlockSpec(memory_space=pltpu.SMEM), VM],
        out_specs=[VM] * 3,
        out_shape=[
            pltpu.VMEM((16, HALF), bf16),
            jax.ShapeDtypeStruct((40, E), f32),
            jax.ShapeDtypeStruct((8, E), f32),
        ],
        compiler_params=params(4),
        name="prep",
    )(doc, ld)


def pre_kernel(
    ld_ref, q_hbm, k_hbm, x_hbm, w_hbm, kd_hbm, x_ref, q_ref, k_ref, w_ref, kd_ref, sems, xsems
):
    half = SPAN // 2
    low = lax.broadcasted_iota(jnp.int32, (half, half), 0) >= lax.broadcasted_iota(
        jnp.int32, (half, half), 1
    )

    def loads(h):
        lanes = pl.ds(pl.multiple_of(h * E, E), E)
        return (
            pltpu.make_async_copy(q_hbm.at[:, lanes], q_ref.at[:, lanes], sems.at[0, h]),
            pltpu.make_async_copy(k_hbm.at[:, lanes], k_ref.at[:, lanes], sems.at[1, h]),
        )

    def stores(h):
        return (
            pltpu.make_async_copy(w_ref.at[h], w_hbm.at[h], sems.at[2, h]),
            pltpu.make_async_copy(kd_ref.at[h], kd_hbm.at[h], sems.at[3, h]),
        )

    for h in range(8):
        for c in loads(h):
            c.start()
    inputs = []
    for r in range(8):
        rows = slice(r * E, (r + 1) * E)
        inputs.append(
            pltpu.make_async_copy(x_hbm.at[rows, :], x_ref.at[rows, :], xsems.at[r])
        )
        inputs[r].start()
    w_ref[:, :, :half, half:] = jnp.zeros((8, 4, half, half), bf16)
    cums = [block_cum(ld_ref[:, b * SPAN : (b + 1) * SPAN]) for b in range(4)]

    def one_head(h, carry):
        for c in loads(h):
            c.wait()
        head = lax.broadcasted_iota(jnp.int32, (8, SPAN), 0) == h
        lanes = pl.ds(pl.multiple_of(h * E, E), E)
        for b in range(4):
            row = jnp.sum(jnp.where(head, cums[b], 0.0), axis=0, keepdims=True)
            col = jnp.transpose(jnp.broadcast_to(row, (8, SPAN)))[:, 0:1]
            last = row[:, SPAN - 1 : SPAN]
            rows = slice(b * SPAN, (b + 1) * SPAN)
            k = k_ref[rows, lanes]
            kt = jnp.transpose(k.astype(f32))
            kd_ref[h, b] = (kt * jnp.exp(last - row)).astype(bf16)
            q = q_ref[rows, lanes]
            s = dot(q[:half], k[:half], ((1,), (1,)))
            g = jnp.exp(jnp.where(low, col[:half] - row[:, :half], -1e30))
            w_ref[h, b, :half, :half] = (s * g).astype(bf16)
            s = dot(q[half:], k, ((1,), (1,)))
            g = jnp.exp(col[half:] - row[:, :half])
            w_ref[h, b, half:, :half] = (s[:, :half] * g).astype(bf16)
            g = jnp.exp(jnp.where(low, col[half:] - row[:, half:], -1e30))
            w_ref[h, b, half:, half:] = (s[:, half:] * g).astype(bf16)
        for c in stores(h):
            c.start()
        return carry

    lax.fori_loop(0, 8, one_head, 0)
    for h in range(8):
        for c in stores(h):
            c.wait()
    for c in inputs:
        c.wait()


def pre(ld, q, k, x):
    shapes = ((8, 4, SPAN, SPAN), (8, 4, E, SPAN))
    return pl.pallas_call(
        pre_kernel,
        in_specs=[VM, HB, HB, HB],
        out_specs=[HB, HB, VM],
        out_shape=[pltpu.HBM(s, bf16) for s in shapes] + [pltpu.VMEM(x.shape, bf16)],
        scratch_shapes=[pltpu.VMEM((1024, 1024), bf16)] * 2
        + [pltpu.VMEM(s, bf16) for s in shapes]
        + [pltpu.SemaphoreType.DMA((4, 8)), pltpu.SemaphoreType.DMA((8,))],
        compiler_params=params(14),
        cost_estimate=pl.CostEstimate(flops=10**9, transcendentals=2 * 10**6, bytes_accessed=10**7),
        name="pre",
    )(ld, hbm(q), hbm(k), hbm(x))


def multiply(mine, d, x_ref, lo, hi, src, dst):
    x, z, core = lax.axis_index("x"), lax.axis_index("z"), lax.axis_index("core")
    first = (core == 0) if mine else (core == 1)
    line = lax.rem(jnp.where(first, x, z) + 4 - d, 4)
    spans = []
    for e in range(4):
        other = lax.rem(jnp.where(first, z, x) + 4 - e, 4)
        at = jnp.where(first, line * LINE + other * CHIP, other * LINE + line * CHIP)
        spans.append(pl.ds(pl.multiple_of(at, 128), CHIP))
    for r in range(2):
        rows = slice(r * 512, (r + 1) * 512)
        part = src[rows, :] if src is not None else None
        for w, (s0, s1) in ((lo, spans[:2]), (hi, spans[2:])):
            lhs = jnp.concatenate([x_ref[rows, s0], x_ref[rows, s1]], axis=1)
            p = dot(lhs, w[: 2 * CHIP, :])
            part = p if part is None else part + p
        dst[rows, :] = part


def mm_kernel(jobs, tails, plane, x_ref, *refs):
    n = 2 * len(jobs)
    bufs, refs = refs[:n], refs[n:]
    src = refs[0].at[plane] if plane is not None else None
    out = refs[0 if plane is None else 1]
    wv, sems = refs[-2:]
    copies = [
        pltpu.make_async_copy(b.at[: 2 * CHIP, :], wv.at[i], sems.at[i])
        for i, b in enumerate(bufs)
    ]
    if tails:
        for j in range(len(jobs)):
            copies.append(
                pltpu.make_async_copy(
                    bufs[2 * j].at[2 * CHIP :, :E], refs[-3].at[j], sems.at[n + j]
                )
            )
    for c in copies:
        c.start()
    for j, (mine, d) in enumerate(jobs):
        copies[2 * j].wait()
        copies[2 * j + 1].wait()
        if plane is None:
            dst, before = out.at[j], None
        else:
            dst, before = out, (out if j else src)
        multiply(mine, d, x_ref, wv.at[2 * j], wv.at[2 * j + 1], before, dst)
    for c in copies[n:]:
        c.wait()


def mm(jobs, x, bufs, tails, plane=None, before=None):
    n = 2 * len(jobs)
    outs = [pltpu.VMEM((ROOM_P, 1024, HALF) if plane is None else (1024, HALF), f32)]
    if tails:
        outs.append(pltpu.VMEM((len(jobs), 64, E), bf16))
    extra = [] if before is None else [before]
    return pl.pallas_call(
        functools.partial(mm_kernel, jobs, tails, plane),
        in_specs=[VM] + [HB] * n + [VM] * len(extra),
        out_specs=[VM] * len(outs),
        out_shape=outs,
        scratch_shapes=[
            pltpu.VMEM((n, 2 * CHIP, HALF), bf16),
            pltpu.SemaphoreType.DMA((n + len(jobs),)),
        ],
        compiler_params=params(10),
        cost_estimate=pl.CostEstimate(
            flops=1024 * LINE * HALF * n, transcendentals=0, bytes_accessed=n * 5 * 10**6
        ),
        name="project",
    )(x, *[hbm(a) for a in bufs], *extra)


def head_col(ld_block):
    return jnp.transpose(jnp.exp(block_cum(ld_block)))


def post_kernel(jobs, dec, q_hbm, kd_hbm, w_hbm, mine_ref, their_ref, x_ref, *refs):
    bufs = refs[: 2 * len(jobs)]
    v_ref, keep_ref, give_ref, tail_ref, st_ref, q_ref, w_ref, acc, kd_ref, sems = refs[
        2 * len(jobs) :
    ]
    tail_ref[...] = bufs[0][2 * CHIP :, :E]
    core = lax.axis_index("core")
    loads = [
        pltpu.make_async_copy(s, t, sems.at[i])
        for i, (s, t) in enumerate(((kd_hbm, kd_ref), (q_hbm, q_ref), (w_hbm, w_ref)))
    ]
    for c in loads:
        c.start()
    for j, (mine, d) in enumerate(jobs):
        src, half = (mine_ref, core) if mine else (their_ref, 1 - core)
        multiply(mine, d, x_ref, bufs[2 * j], bufs[2 * j + 1], src, acc.at[half])
    loads[0].wait()
    states = [None] * 8
    for b in range(4):
        rows = slice(b * SPAN, (b + 1) * SPAN)
        for h in range(8):
            lanes = slice(h * E, (h + 1) * E)
            part = slice((h % 4) * E, (h % 4 + 1) * E)
            v = acc[h // 4, rows, part].astype(bf16)
            v_ref[rows, lanes] = v
            state = states[h]
            if b > 0:
                state = state * dec[32 + b : 33 + b, :]
                high = state.astype(bf16)
                st_ref[h, b - 1, :, :E] = high
                st_ref[h, b - 1, :, E:] = (state - high.astype(f32)).astype(bf16)
            update = dot(kd_ref[h, b], v)
            at = b * 8 + h
            states[h] = update if b == 0 else dec[at : at + 1, :] * state + update
    for h in range(4):
        part = slice(h * E, (h + 1) * E)
        keep_ref[part, :] = jnp.where(core == 0, states[h], states[h + 4])
        give_ref[part, :] = jnp.where(core == 0, states[h + 4], states[h])
    for c in loads[1:]:
        c.wait()


def post(jobs, dec, q, kd, w, mine, theirs, x, bufs):
    return pl.pallas_call(
        functools.partial(post_kernel, jobs),
        in_specs=[VM, HB, HB, HB] + [VM] * (3 + len(bufs)),
        out_specs=[VM] * 7,
        out_shape=[
            pltpu.VMEM((1024, 1024), bf16),
            pltpu.VMEM((HALF, E), f32),
            pltpu.VMEM((HALF, E), f32),
            pltpu.VMEM((64, E), bf16),
            pltpu.VMEM((8, 3, E, 2 * E), bf16),
            pltpu.VMEM((1024, 1024), bf16),
            pltpu.VMEM((8, 4, SPAN, SPAN), bf16),
        ],
        scratch_shapes=[
            pltpu.VMEM((2, 1024, HALF), f32),
            pltpu.VMEM((8, 4, E, SPAN), bf16),
            pltpu.SemaphoreType.DMA((3,)),
        ],
        compiler_params=params(10),
        name="post",
    )(dec, hbm(q), hbm(kd), hbm(w), mine, theirs, x, *bufs)


def within_kernel(ld_ref, v_ref, st_ref, q_ref, w_ref, comb_ref):
    half = SPAN // 2
    for b in range(4):
        rows = slice(b * SPAN, (b + 1) * SPAN)
        col = head_col(ld_ref[:, rows])
        for h in range(8):
            lanes = slice(h * E, (h + 1) * E)
            v = v_ref[rows, lanes]
            top = dot(w_ref[h, b, :half, :half], v[:half])
            low = dot(w_ref[h, b, half:, :], v)
            inner = jnp.concatenate([top, low], axis=0)
            if b > 0:
                o = dot(q_ref[rows, lanes], st_ref[h, b - 1])
                inner = inner + col[:, h : h + 1] * (o[:, :E] + o[:, E:])
            comb_ref[0, rows, lanes] = inner


def within(ld, v, st, q, w):
    return pl.pallas_call(
        within_kernel,
        in_specs=[VM] * 5,
        out_specs=VM,
        out_shape=pltpu.VMEM((ROOM, 1024, 1024), f32),
        compiler_params=params(6),
        cost_estimate=pl.CostEstimate(
            flops=3 * 10**9, transcendentals=0, bytes_accessed=10**7
        ),
        name="within",
    )(ld, v, st, q, w)


def weights_kernel(tails, tail, out_ref):
    x, z, core = lax.axis_index("x"), lax.axis_index("z"), lax.axis_index("core")
    first = core == 0
    rows, own = [], []
    for n in range(4):
        t = (tail[...] if n == 2 else tails[(0, 1, None, 2)[n]]).astype(f32)
        for e in range(4):
            f0 = t[16 * e : 16 * e + 1] + t[16 * e + 1 : 16 * e + 2] + t[16 * e + 2 : 16 * e + 3]
            at = 16 * e + 8
            f1 = t[at : at + 1] + t[at + 1 : at + 2] + t[at + 2 : at + 3]
            if not rows:
                own = [f0, f1]
            rows.append(f0 * f1)
    g = jnp.concatenate(rows, axis=0)
    n = lax.broadcasted_iota(jnp.int32, (16, E), 0)
    px = jnp.where(first, n // 4, n % 4)
    pz = jnp.where(first, n % 4, n // 4)
    k_at = ((x + 4 - px) % 4) * 4 + (z + 4 - pz) % 4
    out = []
    for d in range(4):
        tgt = jnp.where(first, lax.rem(x + d, 4) * 4 + z, x * 4 + lax.rem(z + d, 4))
        for e in range(4):
            src = jnp.where(
                first, x * 4 + lax.rem(z + 4 - e, 4), lax.rem(x + 4 - e, 4) * 4 + z
            )
            p = jnp.where((k_at > src) & (k_at < tgt), g, 1.0)
            p = p[:8] * p[8:]
            p = p[:4] * p[4:]
            p = p[:2] * p[2:]
            p = p[:1] * p[1:]
            out.append(jnp.where(src < tgt, p, 0.0))
    flat = jnp.concatenate(out + own + [jnp.zeros((E - 18, E), f32)], axis=0)
    turned = jnp.transpose(flat)
    out_ref[...] = jnp.where(first, turned[:8], jnp.concatenate([turned[4:8]] * 2, axis=0))


def weights(tails, tail):
    return pl.pallas_call(
        weights_kernel,
        in_specs=[VM] * 2,
        out_specs=VM,
        out_shape=pltpu.VMEM((8, E), f32),
        compiler_params=params(4),
        name="weights",
    )(tails, tail)


def one(ref, h, i):
    return jnp.broadcast_to(ref[h : h + 1, i : i + 1], (E, E))


def chip_kernel(wt, own_ref, recv_ref, f_ref, b_ref):
    first = lax.axis_index("core") == 0
    for h in range(4):
        r = slice(h * E, (h + 1) * E)
        a, b = own_ref[r, :], recv_ref[r, :]
        s = jnp.where(first, one(wt, h, 17) * a + b, a + one(wt, h, 16) * b)
        f_ref[r, :] = s
        b_ref[r, :] = s.astype(bf16)


def spread_kernel(wt, own_ref, r1, r2, r3, o0, o1, o2, o3):
    for h in range(4):
        r = slice(h * E, (h + 1) * E)
        src = [own_ref[r, :]] + [a[r, :].astype(f32) for a in (r1, r2, r3)]
        for d, o in enumerate((o0, o1, o2, o3)):
            s = None
            for e in range(4):
                t = one(wt, h, d * 4 + e) * src[e]
                s = t if s is None else s + t
            o[r, :] = s.astype(o.dtype)


def enter_kernel(wt, m0, r1, r2, r3, own_ref, recv_ref, mine_ref, other_ref):
    first = lax.axis_index("core") == 0
    for h in range(4):
        r = slice(h * E, (h + 1) * E)
        i = m0[r, :]
        for a in (r1, r2, r3):
            i = i + a[r, :].astype(f32)
        mine_ref[r, :] = jnp.where(first, i, one(wt, h, 17) * i + recv_ref[r, :])
        other_ref[r, :] = jnp.where(first, one(wt, h, 16) * i + own_ref[r, :], i)


def small(kernel, name, args, outs):
    return pl.pallas_call(
        kernel,
        in_specs=[VM] * len(args),
        out_specs=[VM] * len(outs),
        out_shape=[pltpu.VMEM((HALF, E), t) for t in outs],
        compiler_params=params(4),
        name=name,
    )(*args)


def outer_kernel(
    sf, ld_ref, mine_ref, other_ref, comb_ref, q_ref, out_ref, sq_ref
):
    first = lax.axis_index("core") == 0
    pairs = []
    for h in range(8):
        r = slice((h % 4) * E, (h % 4 + 1) * E)
        a, b = mine_ref[r, :], other_ref[r, :]
        m = jnp.where(first, a, b) if h < 4 else jnp.where(first, b, a)
        high = m.astype(bf16)
        pairs.append(jnp.concatenate([high, (m - high.astype(f32)).astype(bf16)], axis=1))
    for b in range(4):
        rows = slice(b * SPAN, (b + 1) * SPAN)
        col = head_col(ld_ref[:, rows]) * sf[b : b + 1, :8]
        total = None
        for h in range(8):
            lanes = slice(h * E, (h + 1) * E)
            q = q_ref[rows, lanes]
            o = dot(q, pairs[h])
            o = (o[:, :E] + o[:, E:]) * col[:, h : h + 1]
            o = comb_ref[0, rows, lanes] + o
            out_ref[rows, lanes] = o
            total = o * o if total is None else total + o * o
        for t in range(2):
            tt = jnp.transpose(total[t * E : (t + 1) * E, :])
            sq_ref[b * 2 + t : b * 2 + t + 1, :] = jnp.sum(tt, axis=0, keepdims=True)


def outer(sf, ld, q, mine, other, comb):
    return pl.pallas_call(
        outer_kernel,
        in_specs=[VM] * 6,
        out_specs=[VM, VM],
        out_shape=[pltpu.VMEM((1024, 1024), f32), pltpu.VMEM((8, E), f32)],
        compiler_params=params(6),
        name="outer",
    )(sf, ld, mine, other, comb, vmem(q))


def norm_kernel(out_ref, s0, s1, s2, s3, gain_ref, y_hbm, y_ref, sems):
    total = s0[...] + s1[...] + s2[...] + s3[...]
    scale = lax.rsqrt(total / (SHARD_ATTN_PARTS * E) + 1e-06)
    copies = []
    for t in range(8):
        col = jnp.transpose(jnp.broadcast_to(scale[t : t + 1, :], (E, E)))
        rows = slice(t * E, (t + 1) * E)
        for h in range(8):
            lanes = slice(h * E, (h + 1) * E)
            y_ref[rows, lanes] = (out_ref[rows, lanes] * col * gain_ref[:, lanes]).astype(bf16)
        c = pltpu.make_async_copy(y_ref.at[rows, :], y_hbm.at[rows, :], sems.at[t])
        c.start()
        copies.append(c)
    for c in copies:
        c.wait()


def norm(out, sqs, gain):
    return pl.pallas_call(
        norm_kernel,
        in_specs=[VM] * 6,
        out_specs=HB,
        out_shape=jax.ShapeDtypeStruct((1024, 1024), bf16),
        scratch_shapes=[pltpu.VMEM((1024, 1024), bf16), pltpu.SemaphoreType.DMA((8,))],
        compiler_params=params(8),
        name="norm",
    )(out, *sqs, gain)


def per_device(inputs, q, k, value_weight, ld, doc_start, gain):
    x, z, core = lax.axis_index("x"), lax.axis_index("z"), lax.axis_index("core")
    first = core == 0
    bar = lax.optimization_barrier

    fx, dec, sf = prep(doc_start, ld)
    my_w = lax.dynamic_slice(value_weight, (0, core * HALF), (CHIP // 2, HALF))
    their_w = lax.dynamic_slice(value_weight, (0, (1 - core) * HALF), (CHIP // 2, HALF))
    got = swap(jnp.concatenate([their_w, fx], axis=0))
    recv_w, recv_f = got[: CHIP // 2], got[CHIP // 2 :]
    chip_w = jnp.where(
        first,
        jnp.concatenate([my_w, recv_w], axis=0),
        jnp.concatenate([recv_w, my_w], axis=0),
    )
    chip_w = jnp.concatenate([chip_w, fx[:8], recv_f[:8]], axis=0)
    chip_w, ld, q, k = bar((chip_w, ld, q, k))
    line = [chip_w] + [crossed(chip_w, "z", "x", d, d) for d in (1, 2, 3)]
    w, kd, xv = pre(ld, q, k, inputs)
    line, w = bar((tuple(line), w))
    p_lo = jnp.concatenate([a[:CHIP] for a in line[:2]] + [a[CHIP:] for a in line], axis=0)
    p_hi = jnp.concatenate([a[:CHIP] for a in line[2:]], axis=0)
    up_lo = crossed(p_lo, "x", "z", 1, 1)
    dn_hi = crossed(p_hi, "x", "z", -1, -1)
    up_hi = crossed(p_hi, "x", "z", 1, 1)
    dn_lo = crossed(p_lo, "x", "z", -1, -1)
    sums = mm(((True, 0), (False, 0)), xv, (p_lo, p_hi, swap(p_lo), swap(p_hi)), False)[0]
    up_lo, dn_hi, sums = bar((up_lo, dn_hi, sums))
    op_lo = crossed(up_lo, "x", "z", 1, 1)
    op_hi = crossed(dn_hi, "x", "z", -1, -1)
    bufs = (up_lo, up_hi, dn_lo, dn_hi)
    mine = mm(((True, 1), (True, 3)), xv, bufs, False, 0, sums)[0]
    bufs = tuple(swap(a) for a in bufs)
    op_lo, op_hi, mine = bar((op_lo, op_hi, mine))
    theirs, = mm(((False, 1), (False, 3)), xv, bufs, False, 1, sums)
    tails = jnp.stack([a[2 * CHIP :, :E] for a in (p_lo, up_lo, dn_lo)])
    bufs = [op_lo, op_hi, swap(op_lo), swap(op_hi)]
    theirs, tails = bar((theirs, tails))
    v, own, give, tail, st, qv, wv = post(
        ((True, 2), (False, 2)), vmem(dec), q, kd, w, mine, theirs, xv, [vmem(a) for a in bufs]
    )
    recv = vmem(swap(give))
    wt = weights(tails, tail)
    chip, chip16 = small(chip_kernel, "chip", (wt, own, recv), (f32, bf16))
    got = [vmem(crossed(chip16, "z", "x", d, d)) for d in (1, 2, 3)]
    v, chip = bar((v, chip))
    comb = within(ld, v, st, qv, wv)
    *got, comb = bar((*got, comb))
    sent = small(spread_kernel, "spread", (wt, chip, *got), (f32, bf16, bf16, bf16))
    got = [vmem(crossed(sent[d], "x", "z", d, d)) for d in (1, 2, 3)]
    mine, give = small(enter_kernel, "enter", (wt, sent[0], *got, own, recv), (f32, f32))
    other = vmem(swap(give))
    out, sq = outer(vmem(sf), ld, q, mine, other, comb)
    sqs = [sq] + [vmem(ring(sq, "head", d)) for d in (1, 2, 3)]
    return norm(out, sqs, gain.reshape(1, -1))


def solution(mesh):
    mesh = Mesh(mesh.devices.reshape(4, 4, 2, 4), ("x", "z", "core", "head"))
    placed = (
        P(SEQ, None),
        P(SEQ, "head"),
        P(SEQ, "head"),
        P(SEQ, "head"),
        P("head", SEQ),
        P(SEQ),
        P("head"),
    )
    return jax.shard_map(
        per_device, mesh=mesh, in_specs=placed, out_specs=P(SEQ, "head"), check_vma=False
    )
```

time: 132 us -> 109 us (0.83)
  Pallas kernels: 56 us -> 39.4 us
  starting transfers between devices: 43.3 us -> 35 us
  other arithmetic: 4.87 us -> 0.25 us
  waiting for transfers between devices: 22.5 us -> 26.6 us
  local copies, waits for them, and re-layouts: 4.72 us -> 7.11 us
    pallas_call x6 -> x9, Pallas kernels: 54 us -> 37.1 us  [the longest x3 15.2 us: mm(): pl.pallas_call(functools.partial(mm_kernel, jobs, tails, plane), in_specs...]
    ppermute x15, waiting for transfers between devices: 10.1 us -> 20.1 us  [crossed(): return lax.ppermute(a, SEQ, pairs)]
    ppermute x4 -> x0, waiting for transfers between devices: 7.54 us -> none  [pair(): lax.ppermute(g, axis, [(i, i ^ bit) for i in range(4)])]
    ppermute x4 -> x0, starting transfers between devices: 6.76 us -> none  [pair(): lax.ppermute(g, axis, [(i, i ^ bit) for i in range(4)])]
    unnamed x20 -> x36, local copies, waits for them, and re-layouts: 1.69 us -> 4.53 us
    ppermute x12 -> x11, starting transfers between devices: 5.17 us -> 2.8 us  [swap(): return lax.ppermute(a, 'core', SWAP)]
    mul x2 -> x0, other arithmetic: 1.87 us -> none  [per_device(): surv[b] * jnp.prod(fac[:, :b], axis=1)]
    ppermute x12 -> x11, waiting for transfers between devices: 2.55 us -> 4.17 us  [swap(): return lax.ppermute(a, 'core', SWAP)]
  transfers between devices with their start and end apart: 34 -> 29, of which waited for: 14 -> 14; matrix products, arithmetic and copies ran while one was open for 5% -> 1% of each run, Pallas kernels for 27% -> 25%
where the time goes in v2:
time: 109 us
  Pallas kernels  39.4 us (36%)
  starting transfers between devices  35 us (32%)
  waiting for transfers between devices  26.6 us (24%)
  local copies, waits for them, and re-layouts  7.11 us (7%)
    ppermute x15, starting transfers between devices, crossed(): return lax.ppermute(a, SEQ, pairs)  26.4 us
    ppermute x15, waiting for transfers between devices, crossed(): return lax.ppermute(a, SEQ, pairs)  20.1 us
    pallas_call x3, Pallas kernels, mm(): pl.pallas_call(functools.partial(mm_kernel, jobs, tails, plane), in_specs...  15.2 us
    pallas_call x1, Pallas kernels, pre(): pl.pallas_call(pre_kernel, in_specs=[VM, HB, HB, HB], out_specs=[HB, HB,...  9.24 us
    ppermute x3, starting transfers between devices, ring(): return lax.ppermute(a, axis, [(i, (i + step) % 4) for i in range(4)])  5.89 us
    pallas_call x1, Pallas kernels, post(): pl.pallas_call(functools.partial(post_kernel, jobs), in_specs=[VM, HB, HB...  5.59 us
    unnamed x36, local copies, waits for them, and re-layouts  4.53 us
    ppermute x11, waiting for transfers between devices, swap(): return lax.ppermute(a, 'core', SWAP)  4.17 us
  transfers between devices with their start and end apart: 29, of which 14 were waited for; matrix products, arithmetic and copies ran while one was open for 1% of the time, Pallas kernels for 25%

profile of v2, /device:TPU:0, one launch (start us, length us, event | category | flops | bytes accessed | tf_op | source)
XLA Modules:
  0.0 108.9 jit_solution(15035332655746225950)
XLA Ops:
  2.1 1.1 constant_dynamic-slice_fusion.1
  3.3 1.4 %collective-permute-done = bf16[208,512]{1,0:T(8,128)(2,1)S(1)} collective-permute-done((bf16[208,512]{1,0:T(8,128)(2,1)S(1)}, bf16[208,512]{1,0:T(8,128)(2,1)S(1)}, u32[]{:S(2)}, u32[]{:S(2)}) %collective-permute-start) | collective-permute-done | bytes 213024 | tf_op jit(solution)/shard_map/ppermute | solution.py:26
  5.0 2.1 %collective-permute-start.1 = (bf16[400,512]{1,0:T(8,128)(2,1)S(1)}, bf16[400,512]{1,0:T(8,128)(2,1)S(1)}, u32[]{:S(2)}, u32[]{:S(2)}) collective-permute-start(bf16[400,512]{1,0:T(8,128)(2,1)S(1)} %pad_maximum_fusion.1), channel_id=1, source_target_pairs={{0,8},{4,36},{8,16},{12,44},{16,24},{20,52},{24,0},{28,60},{32,40}... | collective-permute-start | bytes 1228808 | tf_op jit(solution)/shard_map/ppermute | solution.py:42
  7.0 3.6 %collective-permute-start.2 = (bf16[400,512]{1,0:T(8,128)(2,1)S(1)}, bf16[400,512]{1,0:T(8,128)(2,1)S(1)}, u32[]{:S(2)}, u32[]{:S(2)}) collective-permute-start(bf16[400,512]{1,0:T(8,128)(2,1)S(1)} %pad_maximum_fusion.1), channel_id=1, source_target_pairs={{0,16},{4,68},{8,24},{12,76},{16,0},{20,84},{24,8},{28,92},{32,48}... | collective-permute-start | bytes 1228808 | tf_op jit(solution)/shard_map/ppermute | solution.py:42
  10.6 1.0 collective-permute-start.3
  11.6 9.2 %pre.1 = (bf16[8,4,256,256]{3,2,1,0:T(8,128)(2,1)}, bf16[8,4,128,256]{3,2,1,0:T(8,128)(2,1)}, bf16[1024,6144]{1,0:T(8,128)(2,1)S(1)}) custom-call(f32[8,1024]{1,0:T(8,128)S(1)} %copy-done.2, bf16[1024,1024]{1,0:T(8,128)(2,1)} %q_ref, bf16[1024,1024]{1,0:T(8,128)(2,1)} %k_hbm, bf16[1024,6144]{1,0:T(8,128)(2,1)} %x_hbm.1), custom_call_target="tpu_custom_call" | custom-call | flops 1000000000 | bytes 10000000 | tf_op jit(solution)/shard_map/pre/pallas_call | solution.py:183
  21.9 1.5 %collective-permute-start.4 = (bf16[832,512]{1,0:T(8,128)(2,1)S(1)}, bf16[832,512]{1,0:T(8,128)(2,1)S(1)}, u32[]{:S(2)}, u32[]{:S(2)}) collective-permute-start(bf16[832,512]{1,0:T(8,128)(2,1)S(1)} %get-tuple-element.104.refs_0_), channel_id=1, source_target_pairs={{0,32},{4,12},{8,40},{12,20},{16,48},{20,28},{24,56},{28,4},{32,64... | collective-permute-start | bytes 2555912 | tf_op jit(solution)/shard_map/ppermute | solution.py:42
  23.4 1.7 %collective-permute-start.5 = (bf16[768,512]{1,0:T(8,128)(2,1)S(1)}, bf16[768,512]{1,0:T(8,128)(2,1)S(1)}, u32[]{:S(2)}, u32[]{:S(2)}) collective-permute-start(bf16[768,512]{1,0:T(8,128)(2,1)S(1)} %pad_maximum_fusion.refs_1_), channel_id=1, source_target_pairs={{0,96},{4,28},{8,104},{12,4},{16,112},{20,12},{24,120},{28,20},{32... | collective-permute-start | bytes 2359304 | tf_op jit(solution)/shard_map/ppermute | solution.py:42
  25.4 3.0 %collective-permute-start.11 = (bf16[832,512]{1,0:T(8,128)(2,1)S(1)}, bf16[832,512]{1,0:T(8,128)(2,1)S(1)}, u32[]{:S(2)}, u32[]{:S(2)}) collective-permute-start(bf16[832,512]{1,0:T(8,128)(2,1)S(1)} %get-tuple-element.104.refs_0_), channel_id=1, source_target_pairs={{0,96},{4,28},{8,104},{12,4},{16,112},{20,12},{24,120},{28,20},{32... | collective-permute-start | bytes 2555912 | tf_op jit(solution)/shard_map/ppermute | solution.py:42
  29.3 5.1 %project.3.refs_4_ = f32[4,1024,512]{2,1,0:T(8,128)S(1)} custom-call(bf16[1024,6144]{1,0:T(8,128)(2,1)S(1)} %get-tuple-element.56.x_ref, bf16[832,512]{1,0:T(8,128)(2,1)} %copy-done.6, bf16[768,512]{1,0:T(8,128)(2,1)} %copy-done.5, bf16[832,512]{1,0:T(8,128)(2,1)} %copy-done.11, bf16[768,512]{1,0:T(8,128)(2,1)} %copy-done.16), custom_call_target="tpu_custom_call" | custom-call | flops 3221225472 | bytes 20000000 | tf_op jit(solution)/shard_map/project/pallas_call | solution.py:253
  34.4 1.0 collective-permute-done.5.refs_3_
  35.8 2.6 %collective-permute-start.15 = (bf16[768,512]{1,0:T(8,128)(2,1)S(1)}, bf16[768,512]{1,0:T(8,128)(2,1)S(1)}, u32[]{:S(2)}, u32[]{:S(2)}) collective-permute-start(bf16[768,512]{1,0:T(8,128)(2,1)S(1)} %collective-permute-done.5.refs_3_), channel_id=1, source_target_pairs={{0,96},{4,28},{8,104},{12,4},{16,112},{20,12},{24,120},{28,20},{32... | collective-permute-start | bytes 2359304 | tf_op jit(solution)/shard_map/ppermute | solution.py:42
  38.4 5.8 %collective-permute-done.9.refs_1_ = bf16[768,512]{1,0:T(8,128)(2,1)S(1)} collective-permute-done((bf16[768,512]{1,0:T(8,128)(2,1)S(1)}, bf16[768,512]{1,0:T(8,128)(2,1)S(1)}, u32[]{:S(2)}, u32[]{:S(2)}) %collective-permute-start.9) | collective-permute-done | bytes 786464 | tf_op jit(solution)/shard_map/ppermute | solution.py:42
  44.8 8.1 %collective-permute-done.15.refs_1_ = bf16[768,512]{1,0:T(8,128)(2,1)S(1)} collective-permute-done((bf16[768,512]{1,0:T(8,128)(2,1)S(1)}, bf16[768,512]{1,0:T(8,128)(2,1)S(1)}, u32[]{:S(2)}, u32[]{:S(2)}) %collective-permute-start.15) | collective-permute-done | bytes 786464 | tf_op jit(solution)/shard_map/ppermute | solution.py:42
  52.9 5.1 %project.5.mine_ref = f32[1024,512]{1,0:T(8,128)S(1)} custom-call(bf16[1024,6144]{1,0:T(8,128)(2,1)S(1)} %get-tuple-element.56.x_ref, bf16[832,512]{1,0:T(8,128)(2,1)} %copy-done.7, bf16[768,512]{1,0:T(8,128)(2,1)} %copy-done.13, bf16[832,512]{1,0:T(8,128)(2,1)} %copy-done.8, bf16[768,512]{1,0:T(8,128)(2,1)} %copy-done.12, f32[4,1024,512]{2,1,0:T(8,128)S(1)} %project.3.refs_4_), custom_call_target="tpu_custom_call" | custom-call | flops 3221225472 | bytes 20000000 | tf_op jit(solution)/shard_map/project/pallas_call | solution.py:253
  62.5 5.1 %project.4.their_ref = f32[1024,512]{1,0:T(8,128)S(1)} custom-call(bf16[1024,6144]{1,0:T(8,128)(2,1)S(1)} %get-tuple-element.56.x_ref, bf16[832,512]{1,0:T(8,128)(2,1)} %copy-done.9, bf16[768,512]{1,0:T(8,128)(2,1)} %copy-done.14, bf16[832,512]{1,0:T(8,128)(2,1)} %copy-done.10, bf16[768,512]{1,0:T(8,128)(2,1)} %copy-done.15, f32[4,1024,512]{2,1,0:T(8,128)S(1)} %project.3.refs_4_), custom_call_target="tpu_custom_call" | custom-call | flops 3221225472 | bytes 20000000 | tf_op jit(solution)/shard_map/project/pallas_call | solution.py:253
  67.6 5.6 %post.1 = (bf16[1024,1024]{1,0:T(8,128)(2,1)S(1)}, f32[512,128]{1,0:T(8,128)S(1)}, f32[512,128]{1,0:T(8,128)S(1)}, bf16[64,128]{1,0:T(8,128)(2,1)S(1)}, bf16[8,3...) custom-call(f32[40,128]{1,0:T(8,128)S(1)} %get-tuple-element.67.dec, ...), custom_call_target="tpu_custom_call" | custom-call | tf_op jit(solution)/shard_map/post/pallas_call | solution.py:317
  73.6 1.2 %collective-permute-done.18.recv_ref = f32[512,128]{1,0:T(8,128)S(1)} collective-permute-done((f32[512,128]{1,0:T(8,128)S(1)}, f32[512,128]{1,0:T(8,128)S(1)}, u32[]{:S(2)}, u32[]{:S(2)}) %collective-permute-start.18) | collective-permute-done | bytes 262176 | tf_op jit(solution)/shard_map/ppermute | solution.py:26
  75.0 1.5 %collective-permute-start.19 = (bf16[512,128]{1,0:T(8,128)(2,1)S(1)}, bf16[512,128]{1,0:T(8,128)(2,1)S(1)}, u32[]{:S(2)}, u32[]{:S(2)}) collective-permute-start(bf16[512,128]{1,0:T(8,128)(2,1)S(1)} %get-tuple-element.80), channel_id=1, source_target_pairs={{0,8},{4,36},{8,16},{12,44},{16,24},{20,52},{24,0},{28,60},{32,40}... | collective-permute-start | bytes 393224 | tf_op jit(solution)/shard_map/ppermute | solution.py:42
  76.5 2.1 %collective-permute-start.20 = (bf16[512,128]{1,0:T(8,128)(2,1)S(1)}, bf16[512,128]{1,0:T(8,128)(2,1)S(1)}, u32[]{:S(2)}, u32[]{:S(2)}) collective-permute-start(bf16[512,128]{1,0:T(8,128)(2,1)S(1)} %get-tuple-element.80), channel_id=1, source_target_pairs={{0,16},{4,68},{8,24},{12,76},{16,0},{20,84},{24,8},{28,92},{32,48}... | collective-permute-start | bytes 393224 | tf_op jit(solution)/shard_map/ppermute | solution.py:42
  78.6 1.6 %collective-permute-start.21 = (bf16[512,128]{1,0:T(8,128)(2,1)S(1)}, bf16[512,128]{1,0:T(8,128)(2,1)S(1)}, u32[]{:S(2)}, u32[]{:S(2)}) collective-permute-start(bf16[512,128]{1,0:T(8,128)(2,1)S(1)} %get-tuple-element.80), channel_id=1, source_target_pairs={{0,24},{4,100},{8,0},{12,108},{16,8},{20,116},{24,16},{28,124},{32... | collective-permute-start | bytes 393224 | tf_op jit(solution)/shard_map/ppermute | solution.py:42
  80.2 2.7 %within.1.comb_ref = f32[2,1024,1024]{2,1,0:T(8,128)S(1)} custom-call(f32[8,1024]{1,0:T(8,128)S(1)} %copy-done.2, bf16[1024,1024]{1,0:T(8,128)(2,1)S(1)} %get-tuple-element.81.v_ref, bf16[8,3,128,256]{3,2,1,0:T(8,128)(2,1)S(1)} %get-tuple-element.82.st_ref, bf16[1024,1024]{1,0:T(8,128)(2,1)S(1)} %get-tuple-element.83.q_ref, ...), custom_call_target="tpu_custom_call" | custom-call | flops 3000000000 | bytes 10000000 | tf_op jit(solution)/shard_map/within/pallas_call | solution.py:358
  84.0 1.6 %collective-permute-start.22 = (bf16[512,128]{1,0:T(8,128)(2,1)S(1)}, bf16[512,128]{1,0:T(8,128)(2,1)S(1)}, u32[]{:S(2)}, u32[]{:S(2)}) collective-permute-start(bf16[512,128]{1,0:T(8,128)(2,1)S(1)} %get-tuple-element.89), channel_id=1, source_target_pairs={{0,32},{4,12},{8,40},{12,20},{16,48},{20,28},{24,56},{28,4},{32,64... | collective-permute-start | bytes 393224 | tf_op jit(solution)/shard_map/ppermute | solution.py:42
  85.5 2.9 %collective-permute-start.23 = (bf16[512,128]{1,0:T(8,128)(2,1)S(1)}, bf16[512,128]{1,0:T(8,128)(2,1)S(1)}, u32[]{:S(2)}, u32[]{:S(2)}) collective-permute-start(bf16[512,128]{1,0:T(8,128)(2,1)S(1)} %get-tuple-element.90), channel_id=1, source_target_pairs={{0,64},{4,20},{8,72},{12,28},{16,80},{20,4},{24,88},{28,12},{32,96... | collective-permute-start | bytes 393224 | tf_op jit(solution)/shard_map/ppermute | solution.py:42
  90.2 2.6 %collective-permute-done.23.r2 = bf16[512,128]{1,0:T(8,128)(2,1)S(1)} collective-permute-done((bf16[512,128]{1,0:T(8,128)(2,1)S(1)}, bf16[512,128]{1,0:T(8,128)(2,1)S(1)}, u32[]{:S(2)}, u32[]{:S(2)}) %collective-permute-start.23) | collective-permute-done | bytes 131104 | tf_op jit(solution)/shard_map/ppermute | solution.py:42
  93.9 1.5 %collective-permute-done.25.other_ref = f32[512,128]{1,0:T(8,128)S(1)} collective-permute-done((f32[512,128]{1,0:T(8,128)S(1)}, f32[512,128]{1,0:T(8,128)S(1)}, u32[]{:S(2)}, u32[]{:S(2)}) %collective-permute-start.25) | collective-permute-done | bytes 262176 | tf_op jit(solution)/shard_map/ppermute | solution.py:26
  95.4 3.5 %outer.1 = (f32[1024,1024]{1,0:T(8,128)S(1)}, f32[8,128]{1,0:T(8,128)S(1)}) custom-call(f32[8,128]{1,0:T(8,128)S(1)} %get-tuple-element.51.sf, f32[8,1024]{1,0:T(8,128)S(1)} %copy-done.2, f32[512,128]{1,0:T(8,128)S(1)} %get-tuple-element.92.mine_ref, f32[512,128]{1,0:T(8,128)S(1)} %collective-permute-done.25.other_ref, f32[2,1024,1024]{2,1,0:T(8,128)S(1)} %within.1.comb_ref, ...), custom_call_target="tpu_custom_call" | custom-call | tf_op jit(solution)/shard_map/outer/pallas_call | solution.py:495
  99.0 1.6 %collective-permute-start.26 = (f32[8,128]{1,0:T(8,128)S(1)}, f32[8,128]{1,0:T(8,128)S(1)}, u32[]{:S(2)}, u32[]{:S(2)}) collective-permute-start(f32[8,128]{1,0:T(8,128)S(1)} %get-tuple-element.96.s0), channel_id=1, source_target_pairs={{0,1},{1,2},{2,3},{3,0},{4,5},{5,6},{6,7},{7,4},{8,9},{9,10},{10,1... | collective-permute-start | bytes 12296 | tf_op jit(solution)/shard_map/ppermute | solution.py:30
  100.6 2.9 %collective-permute-start.27 = (f32[8,128]{1,0:T(8,128)S(1)}, f32[8,128]{1,0:T(8,128)S(1)}, u32[]{:S(2)}, u32[]{:S(2)}) collective-permute-start(f32[8,128]{1,0:T(8,128)S(1)} %get-tuple-element.96.s0), channel_id=1, source_target_pairs={{0,2},{1,3},{2,0},{3,1},{4,6},{5,7},{6,4},{7,5},{8,10},{9,11},{10,... | collective-permute-start | bytes 12296 | tf_op jit(solution)/shard_map/ppermute | solution.py:30
  103.5 1.3 %collective-permute-start.28 = (f32[8,128]{1,0:T(8,128)S(1)}, f32[8,128]{1,0:T(8,128)S(1)}, u32[]{:S(2)}, u32[]{:S(2)}) collective-permute-start(f32[8,128]{1,0:T(8,128)S(1)} %get-tuple-element.96.s0), channel_id=1, source_target_pairs={{0,3},{1,0},{2,1},{3,2},{4,7},{5,4},{6,5},{7,6},{8,11},{9,8},{10,9... | collective-permute-start | bytes 12296 | tf_op jit(solution)/shard_map/ppermute | solution.py:30
  105.7 1.4 %collective-permute-done.28.s3 = f32[8,128]{1,0:T(8,128)S(1)} collective-permute-done((f32[8,128]{1,0:T(8,128)S(1)}, f32[8,128]{1,0:T(8,128)S(1)}, u32[]{:S(2)}, u32[]{:S(2)}) %collective-permute-start.28) | collective-permute-done | bytes 4128 | tf_op jit(solution)/shard_map/ppermute | solution.py:30
  107.1 1.6 %norm.1 = bf16[1024,1024]{1,0:T(8,128)(2,1)} custom-call(f32[1024,1024]{1,0:T(8,128)S(1)} %get-tuple-element.95.out_ref, f32[8,128]{1,0:T(8,128)S(1)} %get-tuple-element.96.s0, f32[8,128]{1,0:T(8,128)S(1)} %collective-permute-done.26.s1, f32[8,128]{1,0:T(8,128)S(1)} %collective-permute-done.27.s2, f32[8,128]{1,0:T(8,128)S(1)} %collective-permute-done.28.s3, ...), custom_call_target="tpu_custom_call" | custom-call | tf_op jit(solution)/shard_map/norm/pallas_call | solution.py:523
  (93 shorter events, 15.4 us)
Async XLA Ops:
  3.2 1.5 %collective-permute-start = (bf16[208,512]{1,0:T(8,128)(2,1)S(1)}, bf16[208,512]{1,0:T(8,128)(2,1)S(1)}, u32[]{:S(2)}, u32[]{:S(2)}) collective-permute-start(bf16[208,512]{1,0:T(8,128)(2,1)S(1)} %pad_maximum_fusion.2), channel_id=1, source_target_pairs={{0,4},{4,0},{1,5},{5,1},{2,6},{6,2},{3,7},{7,3},{8,12},{12,8},{9,1... | collective-permute-start | bytes 638984 | tf_op jit(solution)/shard_map/ppermute | solution.py:26
  5.0 15.9 %collective-permute-start.1 = (bf16[400,512]{1,0:T(8,128)(2,1)S(1)}, bf16[400,512]{1,0:T(8,128)(2,1)S(1)}, u32[]{:S(2)}, u32[]{:S(2)}) collective-permute-start(bf16[400,512]{1,0:T(8,128)(2,1)S(1)} %pad_maximum_fusion.1), channel_id=1, source_target_pairs={{0,8},{4,36},{8,16},{12,44},{16,24},{20,52},{24,0},{28,60},{32,40}... | collective-permute-start | bytes 1228808 | tf_op jit(solution)/shard_map/ppermute | solution.py:42
  7.0 13.9 %collective-permute-start.2 = (bf16[400,512]{1,0:T(8,128)(2,1)S(1)}, bf16[400,512]{1,0:T(8,128)(2,1)S(1)}, u32[]{:S(2)}, u32[]{:S(2)}) collective-permute-start(bf16[400,512]{1,0:T(8,128)(2,1)S(1)} %pad_maximum_fusion.1), channel_id=1, source_target_pairs={{0,16},{4,68},{8,24},{12,76},{16,0},{20,84},{24,8},{28,92},{32,48}... | collective-permute-start | bytes 1228808 | tf_op jit(solution)/shard_map/ppermute | solution.py:42
  10.6 10.3 %collective-permute-start.3 = (bf16[400,512]{1,0:T(8,128)(2,1)S(1)}, bf16[400,512]{1,0:T(8,128)(2,1)S(1)}, u32[]{:S(2)}, u32[]{:S(2)}) collective-permute-start(bf16[400,512]{1,0:T(8,128)(2,1)S(1)} %pad_maximum_fusion.1), channel_id=1, source_target_pairs={{0,24},{4,100},{8,0},{12,108},{16,8},{20,116},{24,16},{28,124},{32... | collective-permute-start | bytes 1228808 | tf_op jit(solution)/shard_map/ppermute | solution.py:42
  21.1 7.2 %collective-permute-start.6 = (bf16[832,512]{1,0:T(8,128)(2,1)S(1)}, bf16[832,512]{1,0:T(8,128)(2,1)S(1)}, u32[]{:S(2)}, u32[]{:S(2)}) collective-permute-start(bf16[832,512]{1,0:T(8,128)(2,1)S(1)} %get-tuple-element.104.refs_0_), channel_id=1, source_target_pairs={{0,4},{4,0},{1,5},{5,1},{2,6},{6,2},{3,7},{7,3},{8,12},{12,8},{9,1... | collective-permute-start | bytes 2555912 | tf_op jit(solution)/shard_map/ppermute | solution.py:26
  21.3 4.1 %collective-permute-start.7 = (bf16[768,512]{1,0:T(8,128)(2,1)S(1)}, bf16[768,512]{1,0:T(8,128)(2,1)S(1)}, u32[]{:S(2)}, u32[]{:S(2)}) collective-permute-start(bf16[768,512]{1,0:T(8,128)(2,1)S(1)} %pad_maximum_fusion.refs_1_), channel_id=1, source_target_pairs={{0,4},{4,0},{1,5},{5,1},{2,6},{6,2},{3,7},{7,3},{8,12},{12,8},{9,1... | collective-permute-start | bytes 2359304 | tf_op jit(solution)/shard_map/ppermute | solution.py:26
  21.9 13.9 %collective-permute-start.4 = (bf16[832,512]{1,0:T(8,128)(2,1)S(1)}, bf16[832,512]{1,0:T(8,128)(2,1)S(1)}, u32[]{:S(2)}, u32[]{:S(2)}) collective-permute-start(bf16[832,512]{1,0:T(8,128)(2,1)S(1)} %get-tuple-element.104.refs_0_), channel_id=1, source_target_pairs={{0,32},{4,12},{8,40},{12,20},{16,48},{20,28},{24,56},{28,4},{32,64... | collective-permute-start | bytes 2555912 | tf_op jit(solution)/shard_map/ppermute | solution.py:42
  23.4 12.0 %collective-permute-start.5 = (bf16[768,512]{1,0:T(8,128)(2,1)S(1)}, bf16[768,512]{1,0:T(8,128)(2,1)S(1)}, u32[]{:S(2)}, u32[]{:S(2)}) collective-permute-start(bf16[768,512]{1,0:T(8,128)(2,1)S(1)} %pad_maximum_fusion.refs_1_), channel_id=1, source_target_pairs={{0,96},{4,28},{8,104},{12,4},{16,112},{20,12},{24,120},{28,20},{32... | collective-permute-start | bytes 2359304 | tf_op jit(solution)/shard_map/ppermute | solution.py:42
  25.1 19.1 %collective-permute-start.9 = (bf16[768,512]{1,0:T(8,128)(2,1)S(1)}, bf16[768,512]{1,0:T(8,128)(2,1)S(1)}, u32[]{:S(2)}, u32[]{:S(2)}) collective-permute-start(bf16[768,512]{1,0:T(8,128)(2,1)S(1)} %pad_maximum_fusion.refs_1_), channel_id=1, source_target_pairs={{0,32},{4,12},{8,40},{12,20},{16,48},{20,28},{24,56},{28,4},{32,64... | collective-permute-start | bytes 2359304 | tf_op jit(solution)/shard_map/ppermute | solution.py:42
  25.4 19.3 %collective-permute-start.11 = (bf16[832,512]{1,0:T(8,128)(2,1)S(1)}, bf16[832,512]{1,0:T(8,128)(2,1)S(1)}, u32[]{:S(2)}, u32[]{:S(2)}) collective-permute-start(bf16[832,512]{1,0:T(8,128)(2,1)S(1)} %get-tuple-element.104.refs_0_), channel_id=1, source_target_pairs={{0,96},{4,28},{8,104},{12,4},{16,112},{20,12},{24,120},{28,20},{32... | collective-permute-start | bytes 2555912 | tf_op jit(solution)/shard_map/ppermute | solution.py:42
  35.3 17.6 %copy-start.12 = (bf16[768,512]{1,0:T(8,128)(2,1)}, bf16[768,512]{1,0:T(8,128)(2,1)S(1)}, u32[]{:S(2)}) copy-start(bf16[768,512]{1,0:T(8,128)(2,1)S(1)} %collective-permute-done.5.refs_3_) | copy-start | bytes 2359300
  35.8 17.1 %copy-start.7 = (bf16[832,512]{1,0:T(8,128)(2,1)}, bf16[832,512]{1,0:T(8,128)(2,1)S(1)}, u32[]{:S(2)}) copy-start(bf16[832,512]{1,0:T(8,128)(2,1)S(1)} %collective-permute-done.4.refs_0_) | copy-start | bytes 2555908
  35.8 17.1 %collective-permute-start.15 = (bf16[768,512]{1,0:T(8,128)(2,1)S(1)}, bf16[768,512]{1,0:T(8,128)(2,1)S(1)}, u32[]{:S(2)}, u32[]{:S(2)}) collective-permute-start(bf16[768,512]{1,0:T(8,128)(2,1)S(1)} %collective-permute-done.5.refs_3_), channel_id=1, source_target_pairs={{0,96},{4,28},{8,104},{12,4},{16,112},{20,12},{24,120},{28,20},{32... | collective-permute-start | bytes 2359304 | tf_op jit(solution)/shard_map/ppermute | solution.py:42
  38.4 19.6 %collective-permute-start.14 = (bf16[832,512]{1,0:T(8,128)(2,1)S(1)}, bf16[832,512]{1,0:T(8,128)(2,1)S(1)}, u32[]{:S(2)}, u32[]{:S(2)}) collective-permute-start(bf16[832,512]{1,0:T(8,128)(2,1)S(1)} %collective-permute-done.4.refs_0_), channel_id=1, source_target_pairs={{0,32},{4,12},{8,40},{12,20},{16,48},{20,28},{24,56},{28,4},{32,64... | collective-permute-start | bytes 2555912 | tf_op jit(solution)/shard_map/ppermute | solution.py:42
  44.2 14.4 %collective-permute-start.10 = (bf16[768,512]{1,0:T(8,128)(2,1)S(1)}, bf16[768,512]{1,0:T(8,128)(2,1)S(1)}, u32[]{:S(2)}, u32[]{:S(2)}) collective-permute-start(bf16[768,512]{1,0:T(8,128)(2,1)S(1)} %collective-permute-done.9.refs_1_), channel_id=1, source_target_pairs={{0,4},{4,0},{1,5},{5,1},{2,6},{6,2},{3,7},{7,3},{8,12},{12,8},{9,1... | collective-permute-start | bytes 2359304 | tf_op jit(solution)/shard_map/ppermute | solution.py:26
  44.2 16.2 %collective-permute-start.8 = (bf16[832,512]{1,0:T(8,128)(2,1)S(1)}, bf16[832,512]{1,0:T(8,128)(2,1)S(1)}, u32[]{:S(2)}, u32[]{:S(2)}) collective-permute-start(bf16[832,512]{1,0:T(8,128)(2,1)S(1)} %collective-permute-done.4.refs_0_), channel_id=1, source_target_pairs={{0,4},{4,0},{1,5},{5,1},{2,6},{6,2},{3,7},{7,3},{8,12},{12,8},{9,1... | collective-permute-start | bytes 2555912 | tf_op jit(solution)/shard_map/ppermute | solution.py:26
  44.7 15.6 %collective-permute-start.13 = (bf16[768,512]{1,0:T(8,128)(2,1)S(1)}, bf16[768,512]{1,0:T(8,128)(2,1)S(1)}, u32[]{:S(2)}, u32[]{:S(2)}) collective-permute-start(bf16[768,512]{1,0:T(8,128)(2,1)S(1)} %collective-permute-done.5.refs_3_), channel_id=1, source_target_pairs={{0,4},{4,0},{1,5},{5,1},{2,6},{6,2},{3,7},{7,3},{8,12},{12,8},{9,1... | collective-permute-start | bytes 2359304 | tf_op jit(solution)/shard_map/ppermute | solution.py:26
  52.9 7.5 %collective-permute-start.12 = (bf16[832,512]{1,0:T(8,128)(2,1)S(1)}, bf16[832,512]{1,0:T(8,128)(2,1)S(1)}, u32[]{:S(2)}, u32[]{:S(2)}) collective-permute-start(bf16[832,512]{1,0:T(8,128)(2,1)S(1)} %collective-permute-done.11.refs_2_), channel_id=1, source_target_pairs={{0,4},{4,0},{1,5},{5,1},{2,6},{6,2},{3,7},{7,3},{8,12},{12,8},{9,1... | collective-permute-start | bytes 2555912 | tf_op jit(solution)/shard_map/ppermute | solution.py:26
  58.0 9.6 %collective-permute-start.16 = (bf16[832,512]{1,0:T(8,128)(2,1)S(1)}, bf16[832,512]{1,0:T(8,128)(2,1)S(1)}, u32[]{:S(2)}, u32[]{:S(2)}) collective-permute-start(bf16[832,512]{1,0:T(8,128)(2,1)S(1)} %collective-permute-done.14.refs_0_), channel_id=1, source_target_pairs={{0,4},{4,0},{1,5},{5,1},{2,6},{6,2},{3,7},{7,3},{8,12},{12,8},{9,1... | collective-permute-start | bytes 2555912 | tf_op jit(solution)/shard_map/ppermute | solution.py:26
  58.6 9.0 %collective-permute-start.17 = (bf16[768,512]{1,0:T(8,128)(2,1)S(1)}, bf16[768,512]{1,0:T(8,128)(2,1)S(1)}, u32[]{:S(2)}, u32[]{:S(2)}) collective-permute-start(bf16[768,512]{1,0:T(8,128)(2,1)S(1)} %collective-permute-done.15.refs_1_), channel_id=1, source_target_pairs={{0,4},{4,0},{1,5},{5,1},{2,6},{6,2},{3,7},{7,3},{8,12},{12,8},{9,1... | collective-permute-start | bytes 2359304 | tf_op jit(solution)/shard_map/ppermute | solution.py:26
  73.2 1.6 %collective-permute-start.18 = (f32[512,128]{1,0:T(8,128)S(1)}, f32[512,128]{1,0:T(8,128)S(1)}, u32[]{:S(2)}, u32[]{:S(2)}) collective-permute-start(f32[512,128]{1,0:T(8,128)S(1)} %get-tuple-element.77), channel_id=1, source_target_pairs={{0,4},{4,0},{1,5},{5,1},{2,6},{6,2},{3,7},{7,3},{8,12},{12,8},{9,1... | collective-permute-start | bytes 786440 | tf_op jit(solution)/shard_map/ppermute | solution.py:26
  75.0 7.8 %collective-permute-start.19 = (bf16[512,128]{1,0:T(8,128)(2,1)S(1)}, bf16[512,128]{1,0:T(8,128)(2,1)S(1)}, u32[]{:S(2)}, u32[]{:S(2)}) collective-permute-start(bf16[512,128]{1,0:T(8,128)(2,1)S(1)} %get-tuple-element.80), channel_id=1, source_target_pairs={{0,8},{4,36},{8,16},{12,44},{16,24},{20,52},{24,0},{28,60},{32,40}... | collective-permute-start | bytes 393224 | tf_op jit(solution)/shard_map/ppermute | solution.py:42
  76.5 6.5 %collective-permute-start.20 = (bf16[512,128]{1,0:T(8,128)(2,1)S(1)}, bf16[512,128]{1,0:T(8,128)(2,1)S(1)}, u32[]{:S(2)}, u32[]{:S(2)}) collective-permute-start(bf16[512,128]{1,0:T(8,128)(2,1)S(1)} %get-tuple-element.80), channel_id=1, source_target_pairs={{0,16},{4,68},{8,24},{12,76},{16,0},{20,84},{24,8},{28,92},{32,48}... | collective-permute-start | bytes 393224 | tf_op jit(solution)/shard_map/ppermute | solution.py:42
  78.6 5.0 %collective-permute-start.21 = (bf16[512,128]{1,0:T(8,128)(2,1)S(1)}, bf16[512,128]{1,0:T(8,128)(2,1)S(1)}, u32[]{:S(2)}, u32[]{:S(2)}) collective-permute-start(bf16[512,128]{1,0:T(8,128)(2,1)S(1)} %get-tuple-element.80), channel_id=1, source_target_pairs={{0,24},{4,100},{8,0},{12,108},{16,8},{20,116},{24,16},{28,124},{32... | collective-permute-start | bytes 393224 | tf_op jit(solution)/shard_map/ppermute | solution.py:42
  80.2 15.3 %copy-start = (bf16[1024,1024]{1,0:T(8,128)(2,1)S(1)}, bf16[1024,1024]{1,0:T(8,128)(2,1)}, u32[]{:S(2)}) copy-start(bf16[1024,1024]{1,0:T(8,128)(2,1)} %q_ref) | copy-start | bytes 6291460
  84.0 6.2 %collective-permute-start.22 = (bf16[512,128]{1,0:T(8,128)(2,1)S(1)}, bf16[512,128]{1,0:T(8,128)(2,1)S(1)}, u32[]{:S(2)}, u32[]{:S(2)}) collective-permute-start(bf16[512,128]{1,0:T(8,128)(2,1)S(1)} %get-tuple-element.89), channel_id=1, source_target_pairs={{0,32},{4,12},{8,40},{12,20},{16,48},{20,28},{24,56},{28,4},{32,64... | collective-permute-start | bytes 393224 | tf_op jit(solution)/shard_map/ppermute | solution.py:42
  85.5 7.3 %collective-permute-start.23 = (bf16[512,128]{1,0:T(8,128)(2,1)S(1)}, bf16[512,128]{1,0:T(8,128)(2,1)S(1)}, u32[]{:S(2)}, u32[]{:S(2)}) collective-permute-start(bf16[512,128]{1,0:T(8,128)(2,1)S(1)} %get-tuple-element.90), channel_id=1, source_target_pairs={{0,64},{4,20},{8,72},{12,28},{16,80},{20,4},{24,88},{28,12},{32,96... | collective-permute-start | bytes 393224 | tf_op jit(solution)/shard_map/ppermute | solution.py:42
  88.5 5.0 %collective-permute-start.24 = (bf16[512,128]{1,0:T(8,128)(2,1)S(1)}, bf16[512,128]{1,0:T(8,128)(2,1)S(1)}, u32[]{:S(2)}, u32[]{:S(2)}) collective-permute-start(bf16[512,128]{1,0:T(8,128)(2,1)S(1)} %get-tuple-element.91), channel_id=1, source_target_pairs={{0,96},{4,28},{8,104},{12,4},{16,112},{20,12},{24,120},{28,20},{32... | collective-permute-start | bytes 393224 | tf_op jit(solution)/shard_map/ppermute | solution.py:42
  93.6 1.8 %collective-permute-start.25 = (f32[512,128]{1,0:T(8,128)S(1)}, f32[512,128]{1,0:T(8,128)S(1)}, u32[]{:S(2)}, u32[]{:S(2)}) collective-permute-start(f32[512,128]{1,0:T(8,128)S(1)} %get-tuple-element.93), channel_id=1, source_target_pairs={{0,4},{4,0},{1,5},{5,1},{2,6},{6,2},{3,7},{7,3},{8,12},{12,8},{9,1... | collective-permute-start | bytes 786440 | tf_op jit(solution)/shard_map/ppermute | solution.py:26
  99.0 5.9 %collective-permute-start.26 = (f32[8,128]{1,0:T(8,128)S(1)}, f32[8,128]{1,0:T(8,128)S(1)}, u32[]{:S(2)}, u32[]{:S(2)}) collective-permute-start(f32[8,128]{1,0:T(8,128)S(1)} %get-tuple-element.96.s0), channel_id=1, source_target_pairs={{0,1},{1,2},{2,3},{3,0},{4,5},{5,6},{6,7},{7,4},{8,9},{9,10},{10,1... | collective-permute-start | bytes 12296 | tf_op jit(solution)/shard_map/ppermute | solution.py:30
  100.6 5.1 %collective-permute-start.27 = (f32[8,128]{1,0:T(8,128)S(1)}, f32[8,128]{1,0:T(8,128)S(1)}, u32[]{:S(2)}, u32[]{:S(2)}) collective-permute-start(f32[8,128]{1,0:T(8,128)S(1)} %get-tuple-element.96.s0), channel_id=1, source_target_pairs={{0,2},{1,3},{2,0},{3,1},{4,6},{5,7},{6,4},{7,5},{8,10},{9,11},{10,... | collective-permute-start | bytes 12296 | tf_op jit(solution)/shard_map/ppermute | solution.py:30
  103.5 3.6 %collective-permute-start.28 = (f32[8,128]{1,0:T(8,128)S(1)}, f32[8,128]{1,0:T(8,128)S(1)}, u32[]{:S(2)}, u32[]{:S(2)}) collective-permute-start(f32[8,128]{1,0:T(8,128)S(1)} %get-tuple-element.96.s0), channel_id=1, source_target_pairs={{0,3},{1,0},{2,1},{3,2},{4,7},{5,4},{6,5},{7,6},{8,11},{9,8},{10,9... | collective-permute-start | bytes 12296 | tf_op jit(solution)/shard_map/ppermute | solution.py:30
  (14 other events, 63.3 us)

commit v3 on v2

--- a/solution.py
+++ b/solution.py
@@ -70,6 +70,9 @@
 def prep_kernel(doc, ld_ref, fx_ref, dec_ref, sf_ref):
     lane = lax.broadcasted_iota(jnp.int32, (E, E), 1)
     mat = jnp.zeros((E, E), f32)
+    place = lax.broadcasted_iota(jnp.int32, (8, E), 1)
+    start = jnp.ones((8, E), f32)
+    starts = jnp.zeros((8, E), f32)
     surv = []
     for b in range(4):
         total = jnp.sum(ld_ref[:, b * SPAN : (b + 1) * SPAN], axis=1, keepdims=True)
@@ -78,15 +81,16 @@
         tall = jnp.concatenate([decay, jnp.zeros((E - 8, E), f32)], axis=0)
         mat = jnp.where(lane == b, tall, mat)
         surv.append(1.0 - jnp.full((1, E), doc[b], jnp.int32).astype(f32))
+        start = start * surv[b]
+        starts = jnp.where(place == b, start, starts)
+        start = start * decay
     dec_ref[32:40, :] = jnp.concatenate(surv + [jnp.zeros((4, E), f32)], axis=0)
     rows = jnp.transpose(mat)
     f = None
-    sfs = []
     for b in range(4):
         f = surv[b] if b == 0 else f * surv[b]
-        sfs.append(f)
         f = f * rows[b : b + 1, :]
-    sf_ref[...] = jnp.concatenate(sfs + [jnp.zeros((4, E), f32)], axis=0)
+    sf_ref[...] = starts
     high = f.astype(bf16).astype(f32)
     mid = (f - high).astype(bf16).astype(f32)
     low = f - high - mid
@@ -213,58 +217,68 @@
         dst[rows, :] = part
 
 
-def mm_kernel(jobs, tails, plane, x_ref, *refs):
+def mm_kernel(jobs, plane, here, x_ref, *refs):
     n = 2 * len(jobs)
     bufs, refs = refs[:n], refs[n:]
-    src = refs[0].at[plane] if plane is not None else None
-    out = refs[0 if plane is None else 1]
-    wv, sems = refs[-2:]
-    copies = [
-        pltpu.make_async_copy(b.at[: 2 * CHIP, :], wv.at[i], sems.at[i])
-        for i, b in enumerate(bufs)
-    ]
-    if tails:
+    src = None
+    if plane is not None:
+        src = refs[0] if plane < 0 else refs[0].at[plane]
+        refs = refs[1:]
+    out, tails = refs[:2]
+    copies = []
+    if here:
+        wv = bufs
+        for j in range(len(jobs)):
+            tails[j] = bufs[2 * j][2 * CHIP :, :E]
+    else:
+        wv, sems = refs[2:]
+        for i, b in enumerate(bufs):
+            copies.append(
+                pltpu.make_async_copy(b.at[: 2 * CHIP, :], wv.at[i], sems.at[i])
+            )
+        wv = [wv.at[i] for i in range(n)]
         for j in range(len(jobs)):
             copies.append(
                 pltpu.make_async_copy(
-                    bufs[2 * j].at[2 * CHIP :, :E], refs[-3].at[j], sems.at[n + j]
+                    bufs[2 * j].at[2 * CHIP :, :E], tails.at[j], sems.at[n + j]
                 )
             )
     for c in copies:
         c.start()
     for j, (mine, d) in enumerate(jobs):
-        copies[2 * j].wait()
-        copies[2 * j + 1].wait()
+        for c in copies[2 * j : 2 * j + 2]:
+            c.wait()
         if plane is None:
             dst, before = out.at[j], None
         else:
             dst, before = out, (out if j else src)
-        multiply(mine, d, x_ref, wv.at[2 * j], wv.at[2 * j + 1], before, dst)
+        multiply(mine, d, x_ref, wv[2 * j], wv[2 * j + 1], before, dst)
     for c in copies[n:]:
         c.wait()
 
 
-def mm(jobs, x, bufs, tails, plane=None, before=None):
+def mm(jobs, x, bufs, plane=None, before=None, here=False):
     n = 2 * len(jobs)
-    outs = [pltpu.VMEM((ROOM_P, 1024, HALF) if plane is None else (1024, HALF), f32)]
-    if tails:
-        outs.append(pltpu.VMEM((len(jobs), 64, E), bf16))
     extra = [] if before is None else [before]
-    return pl.pallas_call(
-        functools.partial(mm_kernel, jobs, tails, plane),
-        in_specs=[VM] + [HB] * n + [VM] * len(extra),
-        out_specs=[VM] * len(outs),
-        out_shape=outs,
-        scratch_shapes=[
-            pltpu.VMEM((n, 2 * CHIP, HALF), bf16),
-            pltpu.SemaphoreType.DMA((n + len(jobs),)),
+    scratch = [] if here else [
+        pltpu.VMEM((n, 2 * CHIP, HALF), bf16),
+        pltpu.SemaphoreType.DMA((n + len(jobs),)),
+    ]
+    return pl.pallas_call(
+        functools.partial(mm_kernel, jobs, plane, here),
+        in_specs=[VM] + [VM if here else HB] * n + [VM] * len(extra),
+        out_specs=[VM] * 2,
+        out_shape=[
+            pltpu.VMEM((ROOM_P, 1024, HALF) if plane is None else (1024, HALF), f32),
+            pltpu.VMEM((len(jobs), 64, E), bf16),
         ],
-        compiler_params=params(10),
+        scratch_shapes=scratch,
+        compiler_params=params(6 if here else 10),
         cost_estimate=pl.CostEstimate(
             flops=1024 * LINE * HALF * n, transcendentals=0, bytes_accessed=n * 5 * 10**6
         ),
         name="project",
-    )(x, *[hbm(a) for a in bufs], *extra)
+    )(x, *[(vmem if here else hbm)(a) for a in bufs], *extra)
 
 
 def head_col(ld_block):
@@ -276,7 +290,8 @@
     v_ref, keep_ref, give_ref, tail_ref, st_ref, q_ref, w_ref, acc, kd_ref, sems = refs[
         2 * len(jobs) :
     ]
-    tail_ref[...] = bufs[0][2 * CHIP :, :E]
+    tail_ref[0] = bufs[0][2 * CHIP :, :E]
+    tail_ref[1] = bufs[2][2 * CHIP :, :E]
     core = lax.axis_index("core")
     loads = [
         pltpu.make_async_copy(s, t, sems.at[i])
@@ -322,7 +337,7 @@
             pltpu.VMEM((1024, 1024), bf16),
             pltpu.VMEM((HALF, E), f32),
             pltpu.VMEM((HALF, E), f32),
-            pltpu.VMEM((64, E), bf16),
+            pltpu.VMEM((2, 64, E), bf16),
             pltpu.VMEM((8, 3, E, 2 * E), bf16),
             pltpu.VMEM((1024, 1024), bf16),
             pltpu.VMEM((8, 4, SPAN, SPAN), bf16),
@@ -368,19 +383,23 @@
     )(ld, v, st, q, w)
 
 
-def weights_kernel(tails, tail, out_ref):
+def weights_kernel(t_own, t_mine, t_up, t_dn, t_last, out_ref):
     x, z, core = lax.axis_index("x"), lax.axis_index("z"), lax.axis_index("core")
     first = core == 0
-    rows, own = [], []
-    for n in range(4):
-        t = (tail[...] if n == 2 else tails[(0, 1, None, 2)[n]]).astype(f32)
-        for e in range(4):
-            f0 = t[16 * e : 16 * e + 1] + t[16 * e + 1 : 16 * e + 2] + t[16 * e + 2 : 16 * e + 3]
-            at = 16 * e + 8
-            f1 = t[at : at + 1] + t[at + 1 : at + 2] + t[at + 2 : at + 3]
-            if not rows:
-                own = [f0, f1]
-            rows.append(f0 * f1)
+
+    def factors(tiles):
+        out = []
+        for t in tiles:
+            t = t.astype(f32)
+            for e in range(4):
+                r = [t[16 * e + i : 16 * e + i + 1] for i in range(3)]
+                out.append(r[0] + r[1] + r[2])
+        return out
+
+    near = factors((t_own[0], t_mine[0], t_last[0], t_mine[1]))
+    far = factors((t_own[1], t_up[0], t_last[1], t_dn[0]))
+    own = [near[0], far[0]]
+    rows = [near[4 * n + e] * far[4 * e + n] for n in range(4) for e in range(4)]
     g = jnp.concatenate(rows, axis=0)
     n = lax.broadcasted_iota(jnp.int32, (16, E), 0)
     px = jnp.where(first, n // 4, n % 4)
@@ -404,15 +423,15 @@
     out_ref[...] = jnp.where(first, turned[:8], jnp.concatenate([turned[4:8]] * 2, axis=0))
 
 
-def weights(tails, tail):
+def weights(*tails):
     return pl.pallas_call(
         weights_kernel,
-        in_specs=[VM] * 2,
+        in_specs=[VM] * 5,
         out_specs=VM,
         out_shape=pltpu.VMEM((8, E), f32),
         compiler_params=params(4),
         name="weights",
-    )(tails, tail)
+    )(*tails)
 
 
 def one(ref, h, i):
@@ -463,55 +482,62 @@
     )(*args)
 
 
-def outer_kernel(
-    sf, ld_ref, mine_ref, other_ref, comb_ref, q_ref, out_ref, sq_ref
-):
-    first = lax.axis_index("core") == 0
+def outer_kernel(side, sf, ld_ref, state_ref, comb_ref, q_ref, *refs):
+    before, (out_ref, sq_ref) = refs[:-2], refs[-2:]
+    core = lax.axis_index("core")
+    half = core if side == 0 else 1 - core
     pairs = []
-    for h in range(8):
-        r = slice((h % 4) * E, (h % 4 + 1) * E)
-        a, b = mine_ref[r, :], other_ref[r, :]
-        m = jnp.where(first, a, b) if h < 4 else jnp.where(first, b, a)
+    for h in range(4):
+        m = state_ref[h * E : (h + 1) * E, :]
         high = m.astype(bf16)
         pairs.append(jnp.concatenate([high, (m - high.astype(f32)).astype(bf16)], axis=1))
     for b in range(4):
         rows = slice(b * SPAN, (b + 1) * SPAN)
-        col = head_col(ld_ref[:, rows]) * sf[b : b + 1, :8]
+        scale = jnp.exp(block_cum(ld_ref[:, rows])) * sf[:, b : b + 1]
+        scale = jnp.where(half == 0, scale[:4], scale[4:])
+        col = jnp.transpose(jnp.concatenate([scale, scale], axis=0))
         total = None
-        for h in range(8):
-            lanes = slice(h * E, (h + 1) * E)
-            q = q_ref[rows, lanes]
-            o = dot(q, pairs[h])
+        for h in range(4):
+            lanes = pl.ds(pl.multiple_of(half * HALF + h * E, E), E)
+            o = dot(q_ref[rows, lanes], pairs[h])
             o = (o[:, :E] + o[:, E:]) * col[:, h : h + 1]
             o = comb_ref[0, rows, lanes] + o
-            out_ref[rows, lanes] = o
+            out_ref[rows, h * E : (h + 1) * E] = o
             total = o * o if total is None else total + o * o
         for t in range(2):
             tt = jnp.transpose(total[t * E : (t + 1) * E, :])
-            sq_ref[b * 2 + t : b * 2 + t + 1, :] = jnp.sum(tt, axis=0, keepdims=True)
-
-
-def outer(sf, ld, q, mine, other, comb):
-    return pl.pallas_call(
-        outer_kernel,
-        in_specs=[VM] * 6,
+            r = slice(b * 2 + t, b * 2 + t + 1)
+            sq = jnp.sum(tt, axis=0, keepdims=True)
+            sq_ref[r, :] = sq + before[0][r, :] if before else sq
+
+
+def outer(side, sf, ld, state, comb, q, *before):
+    return pl.pallas_call(
+        functools.partial(outer_kernel, side),
+        in_specs=[VM] * (5 + len(before)),
         out_specs=[VM, VM],
-        out_shape=[pltpu.VMEM((1024, 1024), f32), pltpu.VMEM((8, E), f32)],
+        out_shape=[pltpu.VMEM((1024, HALF), f32), pltpu.VMEM((8, E), f32)],
         compiler_params=params(6),
+        cost_estimate=pl.CostEstimate(
+            flops=6 * 10**8, transcendentals=0, bytes_accessed=6 * 10**6
+        ),
         name="outer",
-    )(sf, ld, mine, other, comb, vmem(q))
-
-
-def norm_kernel(out_ref, s0, s1, s2, s3, gain_ref, y_hbm, y_ref, sems):
+    )(sf, ld, state, comb, q, *before)
+
+
+def norm_kernel(mine_ref, other_ref, s0, s1, s2, s3, gain_ref, y_hbm, y_ref, sems):
+    core = lax.axis_index("core")
     total = s0[...] + s1[...] + s2[...] + s3[...]
     scale = lax.rsqrt(total / (SHARD_ATTN_PARTS * E) + 1e-06)
     copies = []
     for t in range(8):
         col = jnp.transpose(jnp.broadcast_to(scale[t : t + 1, :], (E, E)))
         rows = slice(t * E, (t + 1) * E)
-        for h in range(8):
-            lanes = slice(h * E, (h + 1) * E)
-            y_ref[rows, lanes] = (out_ref[rows, lanes] * col * gain_ref[:, lanes]).astype(bf16)
+        for ref, half in ((mine_ref, core), (other_ref, 1 - core)):
+            for h in range(4):
+                lanes = pl.ds(pl.multiple_of(half * HALF + h * E, E), E)
+                y = ref[rows, h * E : (h + 1) * E] * col * gain_ref[:, lanes]
+                y_ref[rows, lanes] = y.astype(bf16)
         c = pltpu.make_async_copy(y_ref.at[rows, :], y_hbm.at[rows, :], sems.at[t])
         c.start()
         copies.append(c)
@@ -519,16 +545,16 @@
         c.wait()
 
 
-def norm(out, sqs, gain):
+def norm(mine, other, sqs, gain):
     return pl.pallas_call(
         norm_kernel,
-        in_specs=[VM] * 6,
+        in_specs=[VM] * 7,
         out_specs=HB,
         out_shape=jax.ShapeDtypeStruct((1024, 1024), bf16),
         scratch_shapes=[pltpu.VMEM((1024, 1024), bf16), pltpu.SemaphoreType.DMA((8,))],
         compiler_params=params(8),
         name="norm",
-    )(out, *sqs, gain)
+    )(mine, other, *sqs, gain)
 
 
 def per_device(inputs, q, k, value_weight, ld, doc_start, gain):
@@ -536,17 +562,15 @@
     first = core == 0
     bar = lax.optimization_barrier
 
-    fx, dec, sf = prep(doc_start, ld)
     my_w = lax.dynamic_slice(value_weight, (0, core * HALF), (CHIP // 2, HALF))
     their_w = lax.dynamic_slice(value_weight, (0, (1 - core) * HALF), (CHIP // 2, HALF))
-    got = swap(jnp.concatenate([their_w, fx], axis=0))
-    recv_w, recv_f = got[: CHIP // 2], got[CHIP // 2 :]
+    recv_w = swap(their_w)
+    fx, dec, sf = prep(doc_start, ld)
     chip_w = jnp.where(
         first,
-        jnp.concatenate([my_w, recv_w], axis=0),
-        jnp.concatenate([recv_w, my_w], axis=0),
+        jnp.concatenate([my_w, recv_w, fx], axis=0),
+        jnp.concatenate([recv_w, my_w, fx], axis=0),
     )
-    chip_w = jnp.concatenate([chip_w, fx[:8], recv_f[:8]], axis=0)
     chip_w, ld, q, k = bar((chip_w, ld, q, k))
     line = [chip_w] + [crossed(chip_w, "z", "x", d, d) for d in (1, 2, 3)]
     w, kd, xv = pre(ld, q, k, inputs)
@@ -557,23 +581,24 @@
     dn_hi = crossed(p_hi, "x", "z", -1, -1)
     up_hi = crossed(p_hi, "x", "z", 1, 1)
     dn_lo = crossed(p_lo, "x", "z", -1, -1)
-    sums = mm(((True, 0), (False, 0)), xv, (p_lo, p_hi, swap(p_lo), swap(p_hi)), False)[0]
+    bufs = (p_lo, p_hi, swap(p_lo), swap(p_hi))
+    sums, t_own = mm(((True, 0), (False, 0)), xv, bufs, here=True)
     up_lo, dn_hi, sums = bar((up_lo, dn_hi, sums))
     op_lo = crossed(up_lo, "x", "z", 1, 1)
     op_hi = crossed(dn_hi, "x", "z", -1, -1)
+    up_lo, up_hi, dn_lo, dn_hi = bar((up_lo, up_hi, dn_lo, dn_hi))
+    swapped = (swap(up_lo), swap(up_hi))
     bufs = (up_lo, up_hi, dn_lo, dn_hi)
-    mine = mm(((True, 1), (True, 3)), xv, bufs, False, 0, sums)[0]
-    bufs = tuple(swap(a) for a in bufs)
-    op_lo, op_hi, mine = bar((op_lo, op_hi, mine))
-    theirs, = mm(((False, 1), (False, 3)), xv, bufs, False, 1, sums)
-    tails = jnp.stack([a[2 * CHIP :, :E] for a in (p_lo, up_lo, dn_lo)])
+    mine, t_mine = mm(((True, 1), (True, 3)), xv, bufs, 0, sums, True)
+    op_lo, op_hi, dn_lo, dn_hi, mine = bar((op_lo, op_hi, dn_lo, dn_hi, mine))
+    theirs, t_up = mm(((False, 1),), xv, swapped, 1, sums, True)
+    theirs, t_dn = mm(((False, 3),), xv, (swap(dn_lo), swap(dn_hi)), -1, theirs, True)
     bufs = [op_lo, op_hi, swap(op_lo), swap(op_hi)]
-    theirs, tails = bar((theirs, tails))
-    v, own, give, tail, st, qv, wv = post(
+    v, own, give, t_last, st, qv, wv = post(
         ((True, 2), (False, 2)), vmem(dec), q, kd, w, mine, theirs, xv, [vmem(a) for a in bufs]
     )
     recv = vmem(swap(give))
-    wt = weights(tails, tail)
+    wt = weights(t_own, t_mine, t_up, t_dn, t_last)
     chip, chip16 = small(chip_kernel, "chip", (wt, own, recv), (f32, bf16))
     got = [vmem(crossed(chip16, "z", "x", d, d)) for d in (1, 2, 3)]
     v, chip = bar((v, chip))
@@ -581,11 +606,12 @@
     *got, comb = bar((*got, comb))
     sent = small(spread_kernel, "spread", (wt, chip, *got), (f32, bf16, bf16, bf16))
     got = [vmem(crossed(sent[d], "x", "z", d, d)) for d in (1, 2, 3)]
-    mine, give = small(enter_kernel, "enter", (wt, sent[0], *got, own, recv), (f32, f32))
-    other = vmem(swap(give))
-    out, sq = outer(vmem(sf), ld, q, mine, other, comb)
+    state, give = small(enter_kernel, "enter", (wt, sent[0], *got, own, recv), (f32, f32))
+    sf, qv = vmem(sf), vmem(q)
+    mine, sq = outer(0, sf, ld, state, comb, qv)
+    other, sq = outer(1, sf, ld, vmem(swap(give)), comb, qv, sq)
     sqs = [sq] + [vmem(ring(sq, "head", d)) for d in (1, 2, 3)]
-    return norm(out, sqs, gain.reshape(1, -1))
+    return norm(mine, other, sqs, gain.reshape(1, -1))
 
 
 def solution(mesh):

time: 109 us -> 102 us (0.936)
  starting transfers between devices: 35 us -> 29.3 us
  waiting for transfers between devices: 26.6 us -> 32.2 us
  local copies, waits for them, and re-layouts: 7.11 us -> 3.35 us
  Pallas kernels: 39.4 us -> 36.6 us
    ppermute x15, waiting for transfers between devices: 20.1 us -> 25.9 us  [crossed(): return lax.ppermute(a, SEQ, pairs)]
    ppermute x15, starting transfers between devices: 26.4 us -> 21.8 us  [crossed(): return lax.ppermute(a, SEQ, pairs)]
    pallas_call x6 -> x8, Pallas kernels: 20.4 us -> 16.8 us  [the longest x4 10.6 us: mm(): pl.pallas_call(functools.partial(mm_kernel, jobs, plane, here), in_specs=...]
    unnamed x36 -> x17, local copies, waits for them, and re-layouts: 4.53 us -> 2.25 us
    ppermute x11, waiting for transfers between devices: 4.17 us -> 2.47 us  [swap(): return lax.ppermute(a, 'core', SWAP)]
    ppermute x3, waiting for transfers between devices: 2.26 us -> 3.84 us  [ring(): return lax.ppermute(a, axis, [(i, (i + step) % 4) for i in range(4)])]
    another operation x2 -> x0, local copies, waits for them, and re-layouts: 1.44 us -> none  [per_device(): tails = jnp.stack([a[2 * CHIP:, :E] for a in (p_lo, up_lo, dn_lo)])]
    ppermute x3, starting transfers between devices: 5.89 us -> 4.69 us  [ring(): return lax.ppermute(a, axis, [(i, (i + step) % 4) for i in range(4)])]
  transfers between devices with their start and end apart: 29 -> 29, of which waited for: 14 -> 17; matrix products, arithmetic and copies ran while one was open for 1% -> 0% of each run, Pallas kernels for 25% -> 25%
where the time goes in v3:
time: 102 us
  Pallas kernels  36.6 us (36%)
  waiting for transfers between devices  32.2 us (32%)
  starting transfers between devices  29.3 us (29%)
  local copies, waits for them, and re-layouts  3.35 us (3%)
    ppermute x15, waiting for transfers between devices, crossed(): return lax.ppermute(a, SEQ, pairs)  25.9 us
    ppermute x15, starting transfers between devices, crossed(): return lax.ppermute(a, SEQ, pairs)  21.8 us
    pallas_call x4, Pallas kernels, mm(): pl.pallas_call(functools.partial(mm_kernel, jobs, plane, here), in_specs=...  10.6 us
    pallas_call x1, Pallas kernels, pre(): pl.pallas_call(pre_kernel, in_specs=[VM, HB, HB, HB], out_specs=[HB, HB,...  9.24 us
    pallas_call x1, Pallas kernels, post(): pl.pallas_call(functools.partial(post_kernel, jobs), in_specs=[VM, HB, HB...  6.53 us
    ppermute x3, starting transfers between devices, ring(): return lax.ppermute(a, axis, [(i, (i + step) % 4) for i in range(4)])  4.69 us
    pallas_call x2, Pallas kernels, outer(): pl.pallas_call(functools.partial(outer_kernel, side), in_specs=[VM] * (5...  4.44 us
    ppermute x3, waiting for transfers between devices, ring(): return lax.ppermute(a, axis, [(i, (i + step) % 4) for i in range(4)])  3.84 us
  transfers between devices with their start and end apart: 29, of which 17 were waited for; matrix products, arithmetic and copies ran while one was open for 0% of the time, Pallas kernels for 25%

profile of v3, /device:TPU:0, one launch (start us, length us, event | category | flops | bytes accessed | tf_op | source)
XLA Modules:
  0.0 102.0 jit_solution(6863907679005915266)
XLA Ops:
  0.0 1.0 %constant_dynamic-slice_fusion.1 = (bf16[192,512]{1,0:T(8,128)(2,1)S(1)}, bf16[192,512]{1,0:T(8,128)(2,1)S(1)}) fusion(bf16[192,1024]{1,0:T(8,128)(2,1)} %param.10, s32[]{:T(128)S(6)} %select_n.15, s32[]{:T(128)S(6)} %select_n.16), kind=kLoop, calls=%fused_computation.11 | loop fusion | bytes 786440 | tf_op jit(solution)/shard_map/dynamic_slice | solution.py:565
  3.4 4.2 %collective-permute-start.3 = (bf16[400,512]{1,0:T(8,128)(2,1)S(1)}, bf16[400,512]{1,0:T(8,128)(2,1)S(1)}, u32[]{:S(2)}, u32[]{:S(2)}) collective-permute-start(bf16[400,512]{1,0:T(8,128)(2,1)S(1)} %fusion), channel_id=1, source_target_pairs={{0,24},{4,100},{8,0},{12,108},{16,8},{20,116},{24,16},{28,124},{32... | collective-permute-start | bytes 1228808 | tf_op jit(solution)/shard_map/ppermute | solution.py:42
  7.6 1.3 %collective-permute-start.1 = (bf16[400,512]{1,0:T(8,128)(2,1)S(1)}, bf16[400,512]{1,0:T(8,128)(2,1)S(1)}, u32[]{:S(2)}, u32[]{:S(2)}) collective-permute-start(bf16[400,512]{1,0:T(8,128)(2,1)S(1)} %fusion), channel_id=1, source_target_pairs={{0,8},{4,36},{8,16},{12,44},{16,24},{20,52},{24,0},{28,60},{32,40}... | collective-permute-start | bytes 1228808 | tf_op jit(solution)/shard_map/ppermute | solution.py:42
  9.6 9.2 %pre.1 = (bf16[8,4,256,256]{3,2,1,0:T(8,128)(2,1)}, bf16[8,4,128,256]{3,2,1,0:T(8,128)(2,1)}, bf16[1024,6144]{1,0:T(8,128)(2,1)S(1)}) custom-call(f32[8,1024]{1,0:T(8,128)S(1)} %copy-done.2, bf16[1024,1024]{1,0:T(8,128)(2,1)} %q_ref.1, bf16[1024,1024]{1,0:T(8,128)(2,1)} %k_hbm, bf16[1024,6144]{1,0:T(8,128)(2,1)} %x_hbm.1), custom_call_target="tpu_custom_call" | custom-call | flops 1000000000 | bytes 10000000 | tf_op jit(solution)/shard_map/pre/pallas_call | solution.py:187
  18.9 2.3 %collective-permute-done.1 = bf16[400,512]{1,0:T(8,128)(2,1)S(1)} collective-permute-done((bf16[400,512]{1,0:T(8,128)(2,1)S(1)}, bf16[400,512]{1,0:T(8,128)(2,1)S(1)}, u32[]{:S(2)}, u32[]{:S(2)}) %collective-permute-start.1) | collective-permute-done | bytes 409632 | tf_op jit(solution)/shard_map/ppermute | solution.py:42
  22.1 1.5 %collective-permute-start.6 = (bf16[832,512]{1,0:T(8,128)(2,1)S(1)}, bf16[832,512]{1,0:T(8,128)(2,1)S(1)}, u32[]{:S(2)}, u32[]{:S(2)}) collective-permute-start(bf16[832,512]{1,0:T(8,128)(2,1)S(1)} %slice_dynamic-update-slice_fusion.2.refs_0_), channel_id=1, source_target_pairs={{0,32},{4,12},{8,40},{12,20},{16,48},{20,28},{24,56},{28,4},{32,64... | collective-permute-start | bytes 2555912 | tf_op jit(solution)/shard_map/ppermute | solution.py:42
  23.6 1.7 %collective-permute-start.7 = (bf16[768,512]{1,0:T(8,128)(2,1)S(1)}, bf16[768,512]{1,0:T(8,128)(2,1)S(1)}, u32[]{:S(2)}, u32[]{:S(2)}) collective-permute-start(bf16[768,512]{1,0:T(8,128)(2,1)S(1)} %pad_maximum_fusion.refs_1_), channel_id=1, source_target_pairs={{0,96},{4,28},{8,104},{12,4},{16,112},{20,12},{24,120},{28,20},{32... | collective-permute-start | bytes 2359304 | tf_op jit(solution)/shard_map/ppermute | solution.py:42
  25.3 1.5 %collective-permute-start.9 = (bf16[832,512]{1,0:T(8,128)(2,1)S(1)}, bf16[832,512]{1,0:T(8,128)(2,1)S(1)}, u32[]{:S(2)}, u32[]{:S(2)}) collective-permute-start(bf16[832,512]{1,0:T(8,128)(2,1)S(1)} %slice_dynamic-update-slice_fusion.2.refs_0_), channel_id=1, source_target_pairs={{0,96},{4,28},{8,104},{12,4},{16,112},{20,12},{24,120},{28,20},{32... | collective-permute-start | bytes 2555912 | tf_op jit(solution)/shard_map/ppermute | solution.py:42
  27.3 3.5 %project.4 = (f32[4,1024,512]{2,1,0:T(8,128)S(1)}, bf16[2,64,128]{2,1,0:T(8,128)(2,1)S(1)}) custom-call(bf16[1024,6144]{1,0:T(8,128)(2,1)S(1)} %get-tuple-element.70.x_ref, bf16[832,512]{1,0:T(8,128)(2,1)S(1)} %slice_dynamic-update-slice_fusion.2.refs_0_, bf16[768,512]{1,0:T(8,128)(2,1)S(1)} %pad_maximum_fusion.refs_1_, ...), custom_call_target="tpu_custom_call" | custom-call | flops 3221225472 | bytes 20000000 | tf_op jit(solution)/shard_map/project/pallas_call | solution.py:267
  30.8 4.7 %collective-permute-done.7.refs_3_ = bf16[768,512]{1,0:T(8,128)(2,1)S(1)} collective-permute-done((bf16[768,512]{1,0:T(8,128)(2,1)S(1)}, bf16[768,512]{1,0:T(8,128)(2,1)S(1)}, u32[]{:S(2)}, u32[]{:S(2)}) %collective-permute-start.7) | collective-permute-done | bytes 786464 | tf_op jit(solution)/shard_map/ppermute | solution.py:42
  36.0 1.1 %collective-permute-start.12 = (bf16[832,512]{1,0:T(8,128)(2,1)S(1)}, bf16[832,512]{1,0:T(8,128)(2,1)S(1)}, u32[]{:S(2)}, u32[]{:S(2)}) collective-permute-start(bf16[832,512]{1,0:T(8,128)(2,1)S(1)} %collective-permute-done.6.refs_0_), channel_id=1, source_target_pairs={{0,32},{4,12},{8,40},{12,20},{16,48},{20,28},{24,56},{28,4},{32,64... | collective-permute-start | bytes 2555912 | tf_op jit(solution)/shard_map/ppermute | solution.py:42
  37.0 2.2 %collective-permute-start.13 = (bf16[768,512]{1,0:T(8,128)(2,1)S(1)}, bf16[768,512]{1,0:T(8,128)(2,1)S(1)}, u32[]{:S(2)}, u32[]{:S(2)}) collective-permute-start(bf16[768,512]{1,0:T(8,128)(2,1)S(1)} %collective-permute-done.7.refs_3_), channel_id=1, source_target_pairs={{0,96},{4,28},{8,104},{12,4},{16,112},{20,12},{24,120},{28,20},{32... | collective-permute-start | bytes 2359304 | tf_op jit(solution)/shard_map/ppermute | solution.py:42
  39.2 5.2 %collective-permute-done.8.refs_1_ = bf16[768,512]{1,0:T(8,128)(2,1)S(1)} collective-permute-done((bf16[768,512]{1,0:T(8,128)(2,1)S(1)}, bf16[768,512]{1,0:T(8,128)(2,1)S(1)}, u32[]{:S(2)}, u32[]{:S(2)}) %collective-permute-start.8) | collective-permute-done | bytes 786464 | tf_op jit(solution)/shard_map/ppermute | solution.py:42
  45.2 3.5 %project.5 = (f32[1024,512]{1,0:T(8,128)S(1)}, bf16[2,64,128]{2,1,0:T(8,128)(2,1)S(1)}) custom-call(bf16[1024,6144]{1,0:T(8,128)(2,1)S(1)} %get-tuple-element.70.x_ref, bf16[832,512]{1,0:T(8,128)(2,1)S(1)} %collective-permute-done.6.refs_0_, bf16[768,512]{1,0:T(8,128)(2,1)S(1)} %collective-permute-done.8.refs_1_, ...), custom_call_target="tpu_custom_call" | custom-call | flops 3221225472 | bytes 20000000 | tf_op jit(solution)/shard_map/project/pallas_call | solution.py:267
  48.7 4.4 %collective-permute-done.13.refs_1_ = bf16[768,512]{1,0:T(8,128)(2,1)S(1)} collective-permute-done((bf16[768,512]{1,0:T(8,128)(2,1)S(1)}, bf16[768,512]{1,0:T(8,128)(2,1)S(1)}, u32[]{:S(2)}, u32[]{:S(2)}) %collective-permute-start.13) | collective-permute-done | bytes 786464 | tf_op jit(solution)/shard_map/ppermute | solution.py:42
  54.6 1.8 %project.6 = (f32[1024,512]{1,0:T(8,128)S(1)}, bf16[1,64,128]{2,1,0:T(8,128)(2,1)S(1)}) custom-call(bf16[1024,6144]{1,0:T(8,128)(2,1)S(1)} %get-tuple-element.70.x_ref, bf16[832,512]{1,0:T(8,128)(2,1)S(1)} %collective-permute-done.10.refs_0_, bf16[768,512]{1,0:T(8,128)(2,1)S(1)} %collective-permute-done.11.refs_1_, ...), custom_call_target="tpu_custom_call" | custom-call | flops 1610612736 | bytes 10000000 | tf_op jit(solution)/shard_map/project/pallas_call | solution.py:267
  57.0 1.8 %project.7 = (f32[1024,512]{1,0:T(8,128)S(1)}, bf16[1,64,128]{2,1,0:T(8,128)(2,1)S(1)}) custom-call(bf16[1024,6144]{1,0:T(8,128)(2,1)S(1)} %get-tuple-element.70.x_ref, bf16[832,512]{1,0:T(8,128)(2,1)S(1)} %collective-permute-done.14.refs_0_, bf16[768,512]{1,0:T(8,128)(2,1)S(1)} %collective-permute-done.15.refs_1_, f32[1024,512]{1,0:T(8,128)S(1)} %get-tuple-element.91.refs_2_), custom_call_target="tpu_custom_call" | custom-call | flops 1610612736 | bytes 10000000 | tf_op jit(solution)/shard_map/project/pallas_call | solution.py:267
  59.4 6.5 %post.1 = (bf16[1024,1024]{1,0:T(8,128)(2,1)S(1)}, f32[512,128]{1,0:T(8,128)S(1)}, f32[512,128]{1,0:T(8,128)S(1)}, bf16[2,64,128]{2,1,0:T(8,128)(2,1)S(1)}, bf16...) custom-call(f32[40,128]{1,0:T(8,128)S(1)} %get-tuple-element.93.dec, ...), custom_call_target="tpu_custom_call" | custom-call | tf_op jit(solution)/shard_map/post/pallas_call | solution.py:332
  66.2 1.3 %collective-permute-done.18.recv_ref = f32[512,128]{1,0:T(8,128)S(1)} collective-permute-done((f32[512,128]{1,0:T(8,128)S(1)}, f32[512,128]{1,0:T(8,128)S(1)}, u32[]{:S(2)}, u32[]{:S(2)}) %collective-permute-start.18) | collective-permute-done | bytes 262176 | tf_op jit(solution)/shard_map/ppermute | solution.py:26
  67.7 1.7 %collective-permute-start.21 = (bf16[512,128]{1,0:T(8,128)(2,1)S(1)}, bf16[512,128]{1,0:T(8,128)(2,1)S(1)}, u32[]{:S(2)}, u32[]{:S(2)}) collective-permute-start(bf16[512,128]{1,0:T(8,128)(2,1)S(1)} %get-tuple-element.106), channel_id=1, source_target_pairs={{0,24},{4,100},{8,0},{12,108},{16,8},{20,116},{24,16},{28,124},{32... | collective-permute-start | bytes 393224 | tf_op jit(solution)/shard_map/ppermute | solution.py:42
  70.7 2.6 %within.1.comb_ref = f32[2,1024,1024]{2,1,0:T(8,128)S(1)} custom-call(f32[8,1024]{1,0:T(8,128)S(1)} %copy-done.3, bf16[1024,1024]{1,0:T(8,128)(2,1)S(1)} %get-tuple-element.107.v_ref, bf16[8,3,128,256]{3,2,1,0:T(8,128)(2,1)S(1)} %get-tuple-element.108.st_ref, bf16[1024,1024]{1,0:T(8,128)(2,1)S(1)} %get-tuple-element.109.q_ref, ...), custom_call_target="tpu_custom_call" | custom-call | flops 3000000000 | bytes 10000000 | tf_op jit(solution)/shard_map/within/pallas_call | solution.py:373
  73.3 2.7 %collective-permute-done.20.r2 = bf16[512,128]{1,0:T(8,128)(2,1)S(1)} collective-permute-done((bf16[512,128]{1,0:T(8,128)(2,1)S(1)}, bf16[512,128]{1,0:T(8,128)(2,1)S(1)}, u32[]{:S(2)}, u32[]{:S(2)}) %collective-permute-start.20) | collective-permute-done | bytes 131104 | tf_op jit(solution)/shard_map/ppermute | solution.py:42
  76.0 1.3 %collective-permute-done.19.r1 = bf16[512,128]{1,0:T(8,128)(2,1)S(1)} collective-permute-done((bf16[512,128]{1,0:T(8,128)(2,1)S(1)}, bf16[512,128]{1,0:T(8,128)(2,1)S(1)}, u32[]{:S(2)}, u32[]{:S(2)}) %collective-permute-start.19) | collective-permute-done | bytes 131104 | tf_op jit(solution)/shard_map/ppermute | solution.py:42
  78.4 3.4 %collective-permute-start.23 = (bf16[512,128]{1,0:T(8,128)(2,1)S(1)}, bf16[512,128]{1,0:T(8,128)(2,1)S(1)}, u32[]{:S(2)}, u32[]{:S(2)}) collective-permute-start(bf16[512,128]{1,0:T(8,128)(2,1)S(1)} %get-tuple-element.116), channel_id=1, source_target_pairs={{0,64},{4,20},{8,72},{12,28},{16,80},{20,4},{24,88},{28,12},{32,96... | collective-permute-start | bytes 393224 | tf_op jit(solution)/shard_map/ppermute | solution.py:42
  82.6 1.4 %collective-permute-done.22.r1 = bf16[512,128]{1,0:T(8,128)(2,1)S(1)} collective-permute-done((bf16[512,128]{1,0:T(8,128)(2,1)S(1)}, bf16[512,128]{1,0:T(8,128)(2,1)S(1)}, u32[]{:S(2)}, u32[]{:S(2)}) %collective-permute-start.22) | collective-permute-done | bytes 131104 | tf_op jit(solution)/shard_map/ppermute | solution.py:42
  83.9 2.2 %collective-permute-done.23.r2 = bf16[512,128]{1,0:T(8,128)(2,1)S(1)} collective-permute-done((bf16[512,128]{1,0:T(8,128)(2,1)S(1)}, bf16[512,128]{1,0:T(8,128)(2,1)S(1)}, u32[]{:S(2)}, u32[]{:S(2)}) %collective-permute-start.23) | collective-permute-done | bytes 131104 | tf_op jit(solution)/shard_map/ppermute | solution.py:42
  87.3 2.2 %outer.2 = (f32[1024,512]{1,0:T(8,128)S(1)}, f32[8,128]{1,0:T(8,128)S(1)}) custom-call(f32[8,128]{1,0:T(8,128)S(1)} %get-tuple-element.65.sf, f32[8,1024]{1,0:T(8,128)S(1)} %copy-done.3, f32[512,128]{1,0:T(8,128)S(1)} %get-tuple-element.118.state_ref, f32[2,1024,1024]{2,1,0:T(8,128)S(1)} %within.1.comb_ref, bf16[1024,1024]{1,0:T(8,128)(2,1)S(1)} %copy-done), custom_call_target="tpu_custom_call" | custom-call | flops 600000000 | bytes 6000000 | tf_op jit(solution)/shard_map/outer/pallas_call | solution.py:515
  89.5 2.2 %outer.3 = (f32[1024,512]{1,0:T(8,128)S(1)}, f32[8,128]{1,0:T(8,128)S(1)}) custom-call(f32[8,128]{1,0:T(8,128)S(1)} %get-tuple-element.65.sf, f32[8,1024]{1,0:T(8,128)S(1)} %copy-done.3, f32[512,128]{1,0:T(8,128)S(1)} %collective-permute-done.25.state_ref, f32[2,1024,1024]{2,1,0:T(8,128)S(1)} %within.1.comb_ref, bf16[1024,1024]{1,0:T(8,128)(2,1)S(1)} %copy-done, ...), custom_call_target="tpu_custom_call" | custom-call | flops 600000000 | bytes 6000000 | tf_op jit(solution)/shard_map/outer/pallas_call | solution.py:515
  91.7 3.1 %collective-permute-start.28 = (f32[8,128]{1,0:T(8,128)S(1)}, f32[8,128]{1,0:T(8,128)S(1)}, u32[]{:S(2)}, u32[]{:S(2)}) collective-permute-start(f32[8,128]{1,0:T(8,128)S(1)} %get-tuple-element.124.s0), channel_id=1, source_target_pairs={{0,3},{1,0},{2,1},{3,2},{4,7},{5,4},{6,5},{7,6},{8,11},{9,8},{10,9... | collective-permute-start | bytes 12296 | tf_op jit(solution)/shard_map/ppermute | solution.py:30
  95.4 1.0 collective-permute-start.26
  96.4 3.5 %collective-permute-done.27.s2 = f32[8,128]{1,0:T(8,128)S(1)} collective-permute-done((f32[8,128]{1,0:T(8,128)S(1)}, f32[8,128]{1,0:T(8,128)S(1)}, u32[]{:S(2)}, u32[]{:S(2)}) %collective-permute-start.27) | collective-permute-done | bytes 4128 | tf_op jit(solution)/shard_map/ppermute | solution.py:30
  100.3 1.6 %norm.1 = bf16[1024,1024]{1,0:T(8,128)(2,1)} custom-call(f32[1024,512]{1,0:T(8,128)S(1)} %get-tuple-element.120.mine_ref, f32[1024,512]{1,0:T(8,128)S(1)} %get-tuple-element.123.other_ref, f32[8,128]{1,0:T(8,128)S(1)} %get-tuple-element.124.s0, f32[8,128]{1,0:T(8,128)S(1)} %collective-permute-done.26.s1, f32[8,128]{1,0:T(8,128)S(1)} %collective-permute-done.27.s2, ...), custom_call_target="tpu_custom_call" | custom-call | tf_op jit(solution)/shard_map/norm/pallas_call | solution.py:549
  (64 shorter events, 14.0 us)
Async XLA Ops:
  1.1 2.2 %collective-permute-start = (bf16[192,512]{1,0:T(8,128)(2,1)S(1)}, bf16[192,512]{1,0:T(8,128)(2,1)S(1)}, u32[]{:S(2)}, u32[]{:S(2)}) collective-permute-start(bf16[192,512]{1,0:T(8,128)(2,1)S(1)} %get-tuple-element.126), channel_id=1, source_target_pairs={{0,4},{4,0},{1,5},{5,1},{2,6},{6,2},{3,7},{7,3},{8,12},{12,8},{9,1... | collective-permute-start | bytes 589832 | tf_op jit(solution)/shard_map/ppermute | solution.py:26
  3.4 15.5 %collective-permute-start.3 = (bf16[400,512]{1,0:T(8,128)(2,1)S(1)}, bf16[400,512]{1,0:T(8,128)(2,1)S(1)}, u32[]{:S(2)}, u32[]{:S(2)}) collective-permute-start(bf16[400,512]{1,0:T(8,128)(2,1)S(1)} %fusion), channel_id=1, source_target_pairs={{0,24},{4,100},{8,0},{12,108},{16,8},{20,116},{24,16},{28,124},{32... | collective-permute-start | bytes 1228808 | tf_op jit(solution)/shard_map/ppermute | solution.py:42
  7.6 11.3 %collective-permute-start.2 = (bf16[400,512]{1,0:T(8,128)(2,1)S(1)}, bf16[400,512]{1,0:T(8,128)(2,1)S(1)}, u32[]{:S(2)}, u32[]{:S(2)}) collective-permute-start(bf16[400,512]{1,0:T(8,128)(2,1)S(1)} %fusion), channel_id=1, source_target_pairs={{0,16},{4,68},{8,24},{12,76},{16,0},{20,84},{24,8},{28,92},{32,48}... | collective-permute-start | bytes 1228808 | tf_op jit(solution)/shard_map/ppermute | solution.py:42
  7.6 13.6 %collective-permute-start.1 = (bf16[400,512]{1,0:T(8,128)(2,1)S(1)}, bf16[400,512]{1,0:T(8,128)(2,1)S(1)}, u32[]{:S(2)}, u32[]{:S(2)}) collective-permute-start(bf16[400,512]{1,0:T(8,128)(2,1)S(1)} %fusion), channel_id=1, source_target_pairs={{0,8},{4,36},{8,16},{12,44},{16,24},{20,52},{24,0},{28,60},{32,40}... | collective-permute-start | bytes 1228808 | tf_op jit(solution)/shard_map/ppermute | solution.py:42
  21.3 5.6 %collective-permute-start.5 = (bf16[768,512]{1,0:T(8,128)(2,1)S(1)}, bf16[768,512]{1,0:T(8,128)(2,1)S(1)}, u32[]{:S(2)}, u32[]{:S(2)}) collective-permute-start(bf16[768,512]{1,0:T(8,128)(2,1)S(1)} %pad_maximum_fusion.refs_1_), channel_id=1, source_target_pairs={{0,4},{4,0},{1,5},{5,1},{2,6},{6,2},{3,7},{7,3},{8,12},{12,8},{9,1... | collective-permute-start | bytes 2359304 | tf_op jit(solution)/shard_map/ppermute | solution.py:26
  21.5 5.8 %collective-permute-start.4 = (bf16[832,512]{1,0:T(8,128)(2,1)S(1)}, bf16[832,512]{1,0:T(8,128)(2,1)S(1)}, u32[]{:S(2)}, u32[]{:S(2)}) collective-permute-start(bf16[832,512]{1,0:T(8,128)(2,1)S(1)} %slice_dynamic-update-slice_fusion.2.refs_0_), channel_id=1, source_target_pairs={{0,4},{4,0},{1,5},{5,1},{2,6},{6,2},{3,7},{7,3},{8,12},{12,8},{9,1... | collective-permute-start | bytes 2555912 | tf_op jit(solution)/shard_map/ppermute | solution.py:26
  22.1 13.9 %collective-permute-start.6 = (bf16[832,512]{1,0:T(8,128)(2,1)S(1)}, bf16[832,512]{1,0:T(8,128)(2,1)S(1)}, u32[]{:S(2)}, u32[]{:S(2)}) collective-permute-start(bf16[832,512]{1,0:T(8,128)(2,1)S(1)} %slice_dynamic-update-slice_fusion.2.refs_0_), channel_id=1, source_target_pairs={{0,32},{4,12},{8,40},{12,20},{16,48},{20,28},{24,56},{28,4},{32,64... | collective-permute-start | bytes 2555912 | tf_op jit(solution)/shard_map/ppermute | solution.py:42
  23.6 12.0 %collective-permute-start.7 = (bf16[768,512]{1,0:T(8,128)(2,1)S(1)}, bf16[768,512]{1,0:T(8,128)(2,1)S(1)}, u32[]{:S(2)}, u32[]{:S(2)}) collective-permute-start(bf16[768,512]{1,0:T(8,128)(2,1)S(1)} %pad_maximum_fusion.refs_1_), channel_id=1, source_target_pairs={{0,96},{4,28},{8,104},{12,4},{16,112},{20,12},{24,120},{28,20},{32... | collective-permute-start | bytes 2359304 | tf_op jit(solution)/shard_map/ppermute | solution.py:42
  25.3 19.4 %collective-permute-start.9 = (bf16[832,512]{1,0:T(8,128)(2,1)S(1)}, bf16[832,512]{1,0:T(8,128)(2,1)S(1)}, u32[]{:S(2)}, u32[]{:S(2)}) collective-permute-start(bf16[832,512]{1,0:T(8,128)(2,1)S(1)} %slice_dynamic-update-slice_fusion.2.refs_0_), channel_id=1, source_target_pairs={{0,96},{4,28},{8,104},{12,4},{16,112},{20,12},{24,120},{28,20},{32... | collective-permute-start | bytes 2555912 | tf_op jit(solution)/shard_map/ppermute | solution.py:42
  26.9 17.5 %collective-permute-start.8 = (bf16[768,512]{1,0:T(8,128)(2,1)S(1)}, bf16[768,512]{1,0:T(8,128)(2,1)S(1)}, u32[]{:S(2)}, u32[]{:S(2)}) collective-permute-start(bf16[768,512]{1,0:T(8,128)(2,1)S(1)} %pad_maximum_fusion.refs_1_), channel_id=1, source_target_pairs={{0,32},{4,12},{8,40},{12,20},{16,48},{20,28},{24,56},{28,4},{32,64... | collective-permute-start | bytes 2359304 | tf_op jit(solution)/shard_map/ppermute | solution.py:42
  36.0 17.6 %collective-permute-start.12 = (bf16[832,512]{1,0:T(8,128)(2,1)S(1)}, bf16[832,512]{1,0:T(8,128)(2,1)S(1)}, u32[]{:S(2)}, u32[]{:S(2)}) collective-permute-start(bf16[832,512]{1,0:T(8,128)(2,1)S(1)} %collective-permute-done.6.refs_0_), channel_id=1, source_target_pairs={{0,32},{4,12},{8,40},{12,20},{16,48},{20,28},{24,56},{28,4},{32,64... | collective-permute-start | bytes 2555912 | tf_op jit(solution)/shard_map/ppermute | solution.py:42
  37.0 16.1 %collective-permute-start.13 = (bf16[768,512]{1,0:T(8,128)(2,1)S(1)}, bf16[768,512]{1,0:T(8,128)(2,1)S(1)}, u32[]{:S(2)}, u32[]{:S(2)}) collective-permute-start(bf16[768,512]{1,0:T(8,128)(2,1)S(1)} %collective-permute-done.7.refs_3_), channel_id=1, source_target_pairs={{0,96},{4,28},{8,104},{12,4},{16,112},{20,12},{24,120},{28,20},{32... | collective-permute-start | bytes 2359304 | tf_op jit(solution)/shard_map/ppermute | solution.py:42
  44.7 9.4 %collective-permute-start.11 = (bf16[768,512]{1,0:T(8,128)(2,1)S(1)}, bf16[768,512]{1,0:T(8,128)(2,1)S(1)}, u32[]{:S(2)}, u32[]{:S(2)}) collective-permute-start(bf16[768,512]{1,0:T(8,128)(2,1)S(1)} %collective-permute-done.8.refs_1_), channel_id=1, source_target_pairs={{0,4},{4,0},{1,5},{5,1},{2,6},{6,2},{3,7},{7,3},{8,12},{12,8},{9,1... | collective-permute-start | bytes 2359304 | tf_op jit(solution)/shard_map/ppermute | solution.py:26
  44.7 9.9 %collective-permute-start.10 = (bf16[832,512]{1,0:T(8,128)(2,1)S(1)}, bf16[832,512]{1,0:T(8,128)(2,1)S(1)}, u32[]{:S(2)}, u32[]{:S(2)}) collective-permute-start(bf16[832,512]{1,0:T(8,128)(2,1)S(1)} %collective-permute-done.6.refs_0_), channel_id=1, source_target_pairs={{0,4},{4,0},{1,5},{5,1},{2,6},{6,2},{3,7},{7,3},{8,12},{12,8},{9,1... | collective-permute-start | bytes 2555912 | tf_op jit(solution)/shard_map/ppermute | solution.py:26
  53.5 3.5 %collective-permute-start.14 = (bf16[832,512]{1,0:T(8,128)(2,1)S(1)}, bf16[832,512]{1,0:T(8,128)(2,1)S(1)}, u32[]{:S(2)}, u32[]{:S(2)}) collective-permute-start(bf16[832,512]{1,0:T(8,128)(2,1)S(1)} %collective-permute-done.9.refs_2_), channel_id=1, source_target_pairs={{0,4},{4,0},{1,5},{5,1},{2,6},{6,2},{3,7},{7,3},{8,12},{12,8},{9,1... | collective-permute-start | bytes 2555912 | tf_op jit(solution)/shard_map/ppermute | solution.py:26
  53.5 3.5 %collective-permute-start.15 = (bf16[768,512]{1,0:T(8,128)(2,1)S(1)}, bf16[768,512]{1,0:T(8,128)(2,1)S(1)}, u32[]{:S(2)}, u32[]{:S(2)}) collective-permute-start(bf16[768,512]{1,0:T(8,128)(2,1)S(1)} %collective-permute-done.7.refs_3_), channel_id=1, source_target_pairs={{0,4},{4,0},{1,5},{5,1},{2,6},{6,2},{3,7},{7,3},{8,12},{12,8},{9,1... | collective-permute-start | bytes 2359304 | tf_op jit(solution)/shard_map/ppermute | solution.py:26
  54.0 5.3 %collective-permute-start.16 = (bf16[832,512]{1,0:T(8,128)(2,1)S(1)}, bf16[832,512]{1,0:T(8,128)(2,1)S(1)}, u32[]{:S(2)}, u32[]{:S(2)}) collective-permute-start(bf16[832,512]{1,0:T(8,128)(2,1)S(1)} %collective-permute-done.12.refs_0_), channel_id=1, source_target_pairs={{0,4},{4,0},{1,5},{5,1},{2,6},{6,2},{3,7},{7,3},{8,12},{12,8},{9,1... | collective-permute-start | bytes 2555912 | tf_op jit(solution)/shard_map/ppermute | solution.py:26
  54.0 5.3 %collective-permute-start.17 = (bf16[768,512]{1,0:T(8,128)(2,1)S(1)}, bf16[768,512]{1,0:T(8,128)(2,1)S(1)}, u32[]{:S(2)}, u32[]{:S(2)}) collective-permute-start(bf16[768,512]{1,0:T(8,128)(2,1)S(1)} %collective-permute-done.13.refs_1_), channel_id=1, source_target_pairs={{0,4},{4,0},{1,5},{5,1},{2,6},{6,2},{3,7},{7,3},{8,12},{12,8},{9,1... | collective-permute-start | bytes 2359304 | tf_op jit(solution)/shard_map/ppermute | solution.py:26
  59.4 11.3 %copy-start.3 = (f32[8,1024]{1,0:T(8,128)S(1)}, f32[8,1024]{1,0:T(8,128)}, u32[]{:S(2)}) copy-start(f32[8,1024]{1,0:T(8,128)} %ld_ref.5) | copy-start | bytes 98308
  65.9 1.6 %collective-permute-start.18 = (f32[512,128]{1,0:T(8,128)S(1)}, f32[512,128]{1,0:T(8,128)S(1)}, u32[]{:S(2)}, u32[]{:S(2)}) collective-permute-start(f32[512,128]{1,0:T(8,128)S(1)} %get-tuple-element.103), channel_id=1, source_target_pairs={{0,4},{4,0},{1,5},{5,1},{2,6},{6,2},{3,7},{7,3},{8,12},{12,8},{9,1... | collective-permute-start | bytes 786440 | tf_op jit(solution)/shard_map/ppermute | solution.py:26
  67.7 5.6 %collective-permute-start.21 = (bf16[512,128]{1,0:T(8,128)(2,1)S(1)}, bf16[512,128]{1,0:T(8,128)(2,1)S(1)}, u32[]{:S(2)}, u32[]{:S(2)}) collective-permute-start(bf16[512,128]{1,0:T(8,128)(2,1)S(1)} %get-tuple-element.106), channel_id=1, source_target_pairs={{0,24},{4,100},{8,0},{12,108},{16,8},{20,116},{24,16},{28,124},{32... | collective-permute-start | bytes 393224 | tf_op jit(solution)/shard_map/ppermute | solution.py:42
  69.4 6.6 %collective-permute-start.20 = (bf16[512,128]{1,0:T(8,128)(2,1)S(1)}, bf16[512,128]{1,0:T(8,128)(2,1)S(1)}, u32[]{:S(2)}, u32[]{:S(2)}) collective-permute-start(bf16[512,128]{1,0:T(8,128)(2,1)S(1)} %get-tuple-element.106), channel_id=1, source_target_pairs={{0,16},{4,68},{8,24},{12,76},{16,0},{20,84},{24,8},{28,92},{32,48}... | collective-permute-start | bytes 393224 | tf_op jit(solution)/shard_map/ppermute | solution.py:42
  69.8 7.5 %collective-permute-start.19 = (bf16[512,128]{1,0:T(8,128)(2,1)S(1)}, bf16[512,128]{1,0:T(8,128)(2,1)S(1)}, u32[]{:S(2)}, u32[]{:S(2)}) collective-permute-start(bf16[512,128]{1,0:T(8,128)(2,1)S(1)} %get-tuple-element.106), channel_id=1, source_target_pairs={{0,8},{4,36},{8,16},{12,44},{16,24},{20,52},{24,0},{28,60},{32,40}... | collective-permute-start | bytes 393224 | tf_op jit(solution)/shard_map/ppermute | solution.py:42
  70.7 16.6 %copy-start = (bf16[1024,1024]{1,0:T(8,128)(2,1)S(1)}, bf16[1024,1024]{1,0:T(8,128)(2,1)}, u32[]{:S(2)}) copy-start(bf16[1024,1024]{1,0:T(8,128)(2,1)} %q_ref.1) | copy-start | bytes 6291460
  77.7 6.2 %collective-permute-start.22 = (bf16[512,128]{1,0:T(8,128)(2,1)S(1)}, bf16[512,128]{1,0:T(8,128)(2,1)S(1)}, u32[]{:S(2)}, u32[]{:S(2)}) collective-permute-start(bf16[512,128]{1,0:T(8,128)(2,1)S(1)} %get-tuple-element.115), channel_id=1, source_target_pairs={{0,32},{4,12},{8,40},{12,20},{16,48},{20,28},{24,56},{28,4},{32,64... | collective-permute-start | bytes 393224 | tf_op jit(solution)/shard_map/ppermute | solution.py:42
  78.4 7.7 %collective-permute-start.23 = (bf16[512,128]{1,0:T(8,128)(2,1)S(1)}, bf16[512,128]{1,0:T(8,128)(2,1)S(1)}, u32[]{:S(2)}, u32[]{:S(2)}) collective-permute-start(bf16[512,128]{1,0:T(8,128)(2,1)S(1)} %get-tuple-element.116), channel_id=1, source_target_pairs={{0,64},{4,20},{8,72},{12,28},{16,80},{20,4},{24,88},{28,12},{32,96... | collective-permute-start | bytes 393224 | tf_op jit(solution)/shard_map/ppermute | solution.py:42
  81.8 5.0 %collective-permute-start.24 = (bf16[512,128]{1,0:T(8,128)(2,1)S(1)}, bf16[512,128]{1,0:T(8,128)(2,1)S(1)}, u32[]{:S(2)}, u32[]{:S(2)}) collective-permute-start(bf16[512,128]{1,0:T(8,128)(2,1)S(1)} %get-tuple-element.117), channel_id=1, source_target_pairs={{0,96},{4,28},{8,104},{12,4},{16,112},{20,12},{24,120},{28,20},{32... | collective-permute-start | bytes 393224 | tf_op jit(solution)/shard_map/ppermute | solution.py:42
  86.9 2.5 %collective-permute-start.25 = (f32[512,128]{1,0:T(8,128)S(1)}, f32[512,128]{1,0:T(8,128)S(1)}, u32[]{:S(2)}, u32[]{:S(2)}) collective-permute-start(f32[512,128]{1,0:T(8,128)S(1)} %get-tuple-element.121), channel_id=1, source_target_pairs={{0,4},{4,0},{1,5},{5,1},{2,6},{6,2},{3,7},{7,3},{8,12},{12,8},{9,1... | collective-permute-start | bytes 786440 | tf_op jit(solution)/shard_map/ppermute | solution.py:26
  89.5 10.8 %copy-start.4 = (f32[1024]{0:T(1024)S(1)}, f32[1024]{0:T(1024)}, u32[]{:S(2)}) copy-start(f32[1024]{0:T(1024)} %param.13) | copy-start | bytes 12292
  91.7 4.7 %collective-permute-start.28 = (f32[8,128]{1,0:T(8,128)S(1)}, f32[8,128]{1,0:T(8,128)S(1)}, u32[]{:S(2)}, u32[]{:S(2)}) collective-permute-start(f32[8,128]{1,0:T(8,128)S(1)} %get-tuple-element.124.s0), channel_id=1, source_target_pairs={{0,3},{1,0},{2,1},{3,2},{4,7},{5,4},{6,5},{7,6},{8,11},{9,8},{10,9... | collective-permute-start | bytes 12296 | tf_op jit(solution)/shard_map/ppermute | solution.py:30
  94.8 5.1 %collective-permute-start.27 = (f32[8,128]{1,0:T(8,128)S(1)}, f32[8,128]{1,0:T(8,128)S(1)}, u32[]{:S(2)}, u32[]{:S(2)}) collective-permute-start(f32[8,128]{1,0:T(8,128)S(1)} %get-tuple-element.124.s0), channel_id=1, source_target_pairs={{0,2},{1,3},{2,0},{3,1},{4,6},{5,7},{6,4},{7,5},{8,10},{9,11},{10,... | collective-permute-start | bytes 12296 | tf_op jit(solution)/shard_map/ppermute | solution.py:30
  95.4 4.8 %collective-permute-start.26 = (f32[8,128]{1,0:T(8,128)S(1)}, f32[8,128]{1,0:T(8,128)S(1)}, u32[]{:S(2)}, u32[]{:S(2)}) collective-permute-start(f32[8,128]{1,0:T(8,128)S(1)} %get-tuple-element.124.s0), channel_id=1, source_target_pairs={{0,1},{1,2},{2,3},{3,0},{4,5},{5,6},{6,7},{7,4},{8,9},{9,10},{10,1... | collective-permute-start | bytes 12296 | tf_op jit(solution)/shard_map/ppermute | solution.py:30
  (3 other events, 2.2 us)

commit v4 on v3

--- a/solution.py
+++ b/solution.py
@@ -285,13 +285,9 @@
     return jnp.transpose(jnp.exp(block_cum(ld_block)))
 
 
-def post_kernel(jobs, dec, q_hbm, kd_hbm, w_hbm, mine_ref, their_ref, x_ref, *refs):
-    bufs = refs[: 2 * len(jobs)]
-    v_ref, keep_ref, give_ref, tail_ref, st_ref, q_ref, w_ref, acc, kd_ref, sems = refs[
-        2 * len(jobs) :
-    ]
-    tail_ref[0] = bufs[0][2 * CHIP :, :E]
-    tail_ref[1] = bufs[2][2 * CHIP :, :E]
+def post_kernel(job, dec, q_hbm, kd_hbm, w_hbm, mine_ref, their_ref, x_ref, lo, hi, *refs):
+    v_ref, keep_ref, give_ref, tail_ref, st_ref, q_ref, w_ref, acc, kd_ref, sems = refs
+    tail_ref[0] = lo[2 * CHIP :, :E]
     core = lax.axis_index("core")
     loads = [
         pltpu.make_async_copy(s, t, sems.at[i])
@@ -299,9 +295,7 @@
     ]
     for c in loads:
         c.start()
-    for j, (mine, d) in enumerate(jobs):
-        src, half = (mine_ref, core) if mine else (their_ref, 1 - core)
-        multiply(mine, d, x_ref, bufs[2 * j], bufs[2 * j + 1], src, acc.at[half])
+    multiply(*job, x_ref, lo, hi, their_ref, acc)
     loads[0].wait()
     states = [None] * 8
     for b in range(4):
@@ -309,7 +303,7 @@
         for h in range(8):
             lanes = slice(h * E, (h + 1) * E)
             part = slice((h % 4) * E, (h % 4 + 1) * E)
-            v = acc[h // 4, rows, part].astype(bf16)
+            v = jnp.where(core == h // 4, mine_ref[rows, part], acc[rows, part]).astype(bf16)
             v_ref[rows, lanes] = v
             state = states[h]
             if b > 0:
@@ -328,22 +322,22 @@
         c.wait()
 
 
-def post(jobs, dec, q, kd, w, mine, theirs, x, bufs):
-    return pl.pallas_call(
-        functools.partial(post_kernel, jobs),
+def post(job, dec, q, kd, w, mine, theirs, x, bufs):
+    return pl.pallas_call(
+        functools.partial(post_kernel, job),
         in_specs=[VM, HB, HB, HB] + [VM] * (3 + len(bufs)),
         out_specs=[VM] * 7,
         out_shape=[
             pltpu.VMEM((1024, 1024), bf16),
             pltpu.VMEM((HALF, E), f32),
             pltpu.VMEM((HALF, E), f32),
-            pltpu.VMEM((2, 64, E), bf16),
+            pltpu.VMEM((1, 64, E), bf16),
             pltpu.VMEM((8, 3, E, 2 * E), bf16),
             pltpu.VMEM((1024, 1024), bf16),
             pltpu.VMEM((8, 4, SPAN, SPAN), bf16),
         ],
         scratch_shapes=[
-            pltpu.VMEM((2, 1024, HALF), f32),
+            pltpu.VMEM((1024, HALF), f32),
             pltpu.VMEM((8, 4, E, SPAN), bf16),
             pltpu.SemaphoreType.DMA((3,)),
         ],
@@ -383,7 +377,7 @@
     )(ld, v, st, q, w)
 
 
-def weights_kernel(t_own, t_mine, t_up, t_dn, t_last, out_ref):
+def weights_kernel(t_own, t_mine, t_op, t_up, t_last, t_dn, out_ref):
     x, z, core = lax.axis_index("x"), lax.axis_index("z"), lax.axis_index("core")
     first = core == 0
 
@@ -396,8 +390,8 @@
                 out.append(r[0] + r[1] + r[2])
         return out
 
-    near = factors((t_own[0], t_mine[0], t_last[0], t_mine[1]))
-    far = factors((t_own[1], t_up[0], t_last[1], t_dn[0]))
+    near = factors((t_own[0], t_mine[0], t_op[0], t_mine[1]))
+    far = factors((t_own[1], t_up[0], t_last[0], t_dn[0]))
     own = [near[0], far[0]]
     rows = [near[4 * n + e] * far[4 * e + n] for n in range(4) for e in range(4)]
     g = jnp.concatenate(rows, axis=0)
@@ -426,7 +420,7 @@
 def weights(*tails):
     return pl.pallas_call(
         weights_kernel,
-        in_specs=[VM] * 5,
+        in_specs=[VM] * 6,
         out_specs=VM,
         out_shape=pltpu.VMEM((8, E), f32),
         compiler_params=params(4),
@@ -571,17 +565,24 @@
         jnp.concatenate([my_w, recv_w, fx], axis=0),
         jnp.concatenate([recv_w, my_w, fx], axis=0),
     )
-    chip_w, ld, q, k = bar((chip_w, ld, q, k))
-    line = [chip_w] + [crossed(chip_w, "z", "x", d, d) for d in (1, 2, 3)]
-    w, kd, xv = pre(ld, q, k, inputs)
-    line, w = bar((tuple(line), w))
-    p_lo = jnp.concatenate([a[:CHIP] for a in line[:2]] + [a[CHIP:] for a in line], axis=0)
-    p_hi = jnp.concatenate([a[:CHIP] for a in line[2:]], axis=0)
+    rows = CHIP // 2
+    up = crossed(chip_w, "z", "x", 1, 1)
+    dn = crossed(chip_w, "z", "x", -1, -1)
+    far_a = crossed(up[:rows], "z", "x", 1, 1)
+    far_b = crossed(dn[rows:], "z", "x", -1, -1)
+    chip_w, up, dn, far_a, far_b, ld, q, k = bar((chip_w, up, dn, far_a, far_b, ld, q, k))
+    p_lo = jnp.concatenate(
+        [chip_w[:CHIP], up[:CHIP], chip_w[CHIP:], up[CHIP:], far_b[rows:], dn[CHIP:]], axis=0
+    )
+    p_hi = jnp.concatenate([far_a, far_b[:rows], dn[:CHIP]], axis=0)
     up_lo = crossed(p_lo, "x", "z", 1, 1)
     dn_hi = crossed(p_hi, "x", "z", -1, -1)
     up_hi = crossed(p_hi, "x", "z", 1, 1)
     dn_lo = crossed(p_lo, "x", "z", -1, -1)
-    bufs = (p_lo, p_hi, swap(p_lo), swap(p_hi))
+    s_lo, s_hi = swap(p_lo), swap(p_hi)
+    s_lo, s_hi, ld, q, k = bar((s_lo, s_hi, ld, q, k))
+    w, kd, xv = pre(ld, q, k, inputs)
+    bufs = (p_lo, p_hi, s_lo, s_hi)
     sums, t_own = mm(((True, 0), (False, 0)), xv, bufs, here=True)
     up_lo, dn_hi, sums = bar((up_lo, dn_hi, sums))
     op_lo = crossed(up_lo, "x", "z", 1, 1)
@@ -593,12 +594,13 @@
     op_lo, op_hi, dn_lo, dn_hi, mine = bar((op_lo, op_hi, dn_lo, dn_hi, mine))
     theirs, t_up = mm(((False, 1),), xv, swapped, 1, sums, True)
     theirs, t_dn = mm(((False, 3),), xv, (swap(dn_lo), swap(dn_hi)), -1, theirs, True)
-    bufs = [op_lo, op_hi, swap(op_lo), swap(op_hi)]
+    mine, t_op = mm(((True, 2),), xv, (op_lo, op_hi), -1, mine, True)
+    bufs = [swap(op_lo), swap(op_hi)]
     v, own, give, t_last, st, qv, wv = post(
-        ((True, 2), (False, 2)), vmem(dec), q, kd, w, mine, theirs, xv, [vmem(a) for a in bufs]
+        (False, 2), vmem(dec), q, kd, w, mine, theirs, xv, [vmem(a) for a in bufs]
     )
     recv = vmem(swap(give))
-    wt = weights(t_own, t_mine, t_up, t_dn, t_last)
+    wt = weights(t_own, t_mine, t_op, t_up, t_last, t_dn)
     chip, chip16 = small(chip_kernel, "chip", (wt, own, recv), (f32, bf16))
     got = [vmem(crossed(chip16, "z", "x", d, d)) for d in (1, 2, 3)]
     v, chip = bar((v, chip))

time: 102 us -> 102 us (level)
  starting transfers between devices: 29.3 us -> 33.5 us
  waiting for transfers between devices: 32.2 us -> 29.3 us
  Pallas kernels: 36.6 us -> 35.5 us
    ppermute x15 -> x16, starting transfers between devices: 21.8 us -> 24.9 us  [crossed(): return lax.ppermute(a, SEQ, pairs)]
    pallas_call x2, Pallas kernels: 6.68 us -> 3.67 us  [the longest x1 3.52 us: post(): pl.pallas_call(functools.partial(post_kernel, job), in_specs=[VM, HB, HB,...]
    pallas_call x4 -> x5, Pallas kernels: 10.6 us -> 12.4 us  [mm(): pl.pallas_call(functools.partial(mm_kernel, jobs, plane, here), in_specs=...]
    ppermute x3, waiting for transfers between devices: 3.84 us -> 2.26 us  [ring(): return lax.ppermute(a, axis, [(i, (i + step) % 4) for i in range(4)])]
    ppermute x3, starting transfers between devices: 4.69 us -> 5.89 us  [ring(): return lax.ppermute(a, axis, [(i, (i + step) % 4) for i in range(4)])]
    ppermute x11, waiting for transfers between devices: 2.47 us -> 1.4 us  [swap(): return lax.ppermute(a, 'core', SWAP)]
    unnamed x17 -> x15, local copies, waits for them, and re-layouts: 2.25 us -> 1.49 us
    ppermute x15 -> x16, waiting for transfers between devices: 25.9 us -> 25.6 us  [crossed(): return lax.ppermute(a, SEQ, pairs)]
  transfers between devices with their start and end apart: 29 -> 30, of which waited for: 17 -> 14; matrix products, arithmetic and copies ran while one was open for 0% -> 0% of each run, Pallas kernels for 25% -> 27%
where the time goes in v4:
time: 102 us
  Pallas kernels  35.5 us (35%)
  starting transfers between devices  33.5 us (33%)
  waiting for transfers between devices  29.3 us (29%)
  local copies, waits for them, and re-layouts  2.61 us (3%)
    ppermute x16, waiting for transfers between devices, crossed(): return lax.ppermute(a, SEQ, pairs)  25.6 us
    ppermute x16, starting transfers between devices, crossed(): return lax.ppermute(a, SEQ, pairs)  24.9 us
    pallas_call x5, Pallas kernels, mm(): pl.pallas_call(functools.partial(mm_kernel, jobs, plane, here), in_specs=...  12.4 us
    pallas_call x1, Pallas kernels, pre(): pl.pallas_call(pre_kernel, in_specs=[VM, HB, HB, HB], out_specs=[HB, HB,...  9.24 us
    ppermute x3, starting transfers between devices, ring(): return lax.ppermute(a, axis, [(i, (i + step) % 4) for i in range(4)])  5.89 us
    pallas_call x2, Pallas kernels, outer(): pl.pallas_call(functools.partial(outer_kernel, side), in_specs=[VM] * (5...  4.44 us
    pallas_call x1, Pallas kernels, post(): pl.pallas_call(functools.partial(post_kernel, job), in_specs=[VM, HB, HB,...  3.52 us
    ppermute x11, starting transfers between devices, swap(): return lax.ppermute(a, 'core', SWAP)  2.66 us
  transfers between devices with their start and end apart: 30, of which 14 were waited for; matrix products, arithmetic and copies ran while one was open for 0% of the time, Pallas kernels for 27%

profile of v4, /device:TPU:0, one launch (start us, length us, event | category | flops | bytes accessed | tf_op | source)
XLA Modules:
  0.0 101.5 jit_solution(1952288943420259177)
XLA Ops:
  0.0 1.0 %constant_dynamic-slice_fusion.1 = (bf16[192,512]{1,0:T(8,128)(2,1)S(1)}, bf16[192,512]{1,0:T(8,128)(2,1)S(1)}) fusion(bf16[192,1024]{1,0:T(8,128)(2,1)} %param.10, s32[]{:T(128)S(6)} %select_n.15, s32[]{:T(128)S(6)} %select_n.16), kind=kLoop, calls=%fused_computation.11 | loop fusion | bytes 786440 | tf_op jit(solution)/shard_map/dynamic_slice | solution.py:559
  3.4 4.2 %collective-permute-start.2 = (bf16[400,512]{1,0:T(8,128)(2,1)S(1)}, bf16[400,512]{1,0:T(8,128)(2,1)S(1)}, u32[]{:S(2)}, u32[]{:S(2)}) collective-permute-start(bf16[400,512]{1,0:T(8,128)(2,1)S(1)} %fusion), channel_id=1, source_target_pairs={{0,24},{4,100},{8,0},{12,108},{16,8},{20,116},{24,16},{28,124},{32... | collective-permute-start | bytes 1228808 | tf_op jit(solution)/shard_map/ppermute | solution.py:42
  7.6 5.5 %collective-permute-done.2 = bf16[400,512]{1,0:T(8,128)(2,1)S(1)} collective-permute-done((bf16[400,512]{1,0:T(8,128)(2,1)S(1)}, bf16[400,512]{1,0:T(8,128)(2,1)S(1)}, u32[]{:S(2)}, u32[]{:S(2)}) %collective-permute-start.2) | collective-permute-done | bytes 409632 | tf_op jit(solution)/shard_map/ppermute | solution.py:42
  13.1 3.8 %collective-permute-start.4 = (bf16[208,512]{1,0:T(8,128)(2,1)S(1)}, bf16[208,512]{1,0:T(8,128)(2,1)S(1)}, u32[]{:S(2)}, u32[]{:S(2)}) collective-permute-start(bf16[208,512]{1,0:T(8,128)(2,1)S(1)} %slice.41), channel_id=1, source_target_pairs={{0,24},{4,100},{8,0},{12,108},{16,8},{20,116},{24,16},{28,124},{32... | collective-permute-start | bytes 638984 | tf_op jit(solution)/shard_map/ppermute | solution.py:42
  17.0 6.9 %collective-permute-done.3 = bf16[192,512]{1,0:T(8,128)(2,1)S(1)} collective-permute-done((bf16[192,512]{1,0:T(8,128)(2,1)S(1)}, bf16[192,512]{1,0:T(8,128)(2,1)S(1)}, u32[]{:S(2)}, u32[]{:S(2)}) %collective-permute-start.3) | collective-permute-done | bytes 196640 | tf_op jit(solution)/shard_map/ppermute | solution.py:42
  24.7 1.5 %collective-permute-start.7 = (bf16[832,512]{1,0:T(8,128)(2,1)S(1)}, bf16[832,512]{1,0:T(8,128)(2,1)S(1)}, u32[]{:S(2)}, u32[]{:S(2)}) collective-permute-start(bf16[832,512]{1,0:T(8,128)(2,1)S(1)} %slice_dynamic-update-slice_fusion.2.refs_0_), channel_id=1, source_target_pairs={{0,32},{4,12},{8,40},{12,20},{16,48},{20,28},{24,56},{28,4},{32,64... | collective-permute-start | bytes 2555912 | tf_op jit(solution)/shard_map/ppermute | solution.py:42
  26.2 1.7 %collective-permute-start.8 = (bf16[768,512]{1,0:T(8,128)(2,1)S(1)}, bf16[768,512]{1,0:T(8,128)(2,1)S(1)}, u32[]{:S(2)}, u32[]{:S(2)}) collective-permute-start(bf16[768,512]{1,0:T(8,128)(2,1)S(1)} %pad_maximum_fusion.refs_1_), channel_id=1, source_target_pairs={{0,96},{4,28},{8,104},{12,4},{16,112},{20,12},{24,120},{28,20},{32... | collective-permute-start | bytes 2359304 | tf_op jit(solution)/shard_map/ppermute | solution.py:42
  28.0 1.5 %collective-permute-start.10 = (bf16[832,512]{1,0:T(8,128)(2,1)S(1)}, bf16[832,512]{1,0:T(8,128)(2,1)S(1)}, u32[]{:S(2)}, u32[]{:S(2)}) collective-permute-start(bf16[832,512]{1,0:T(8,128)(2,1)S(1)} %slice_dynamic-update-slice_fusion.2.refs_0_), channel_id=1, source_target_pairs={{0,96},{4,28},{8,104},{12,4},{16,112},{20,12},{24,120},{28,20},{32... | collective-permute-start | bytes 2555912 | tf_op jit(solution)/shard_map/ppermute | solution.py:42
  30.0 9.2 %pre.1 = (bf16[8,4,256,256]{3,2,1,0:T(8,128)(2,1)}, bf16[8,4,128,256]{3,2,1,0:T(8,128)(2,1)}, bf16[1024,6144]{1,0:T(8,128)(2,1)S(1)}) custom-call(f32[8,1024]{1,0:T(8,128)S(1)} %copy-done.2, bf16[1024,1024]{1,0:T(8,128)(2,1)} %q_ref.1, bf16[1024,1024]{1,0:T(8,128)(2,1)} %k_hbm, bf16[1024,6144]{1,0:T(8,128)(2,1)} %x_hbm.1), custom_call_target="tpu_custom_call" | custom-call | flops 1000000000 | bytes 10000000 | tf_op jit(solution)/shard_map/pre/pallas_call | solution.py:187
  39.3 3.5 %project.5 = (f32[4,1024,512]{2,1,0:T(8,128)S(1)}, bf16[2,64,128]{2,1,0:T(8,128)(2,1)S(1)}) custom-call(bf16[1024,6144]{1,0:T(8,128)(2,1)S(1)} %get-tuple-element.84.x_ref, bf16[832,512]{1,0:T(8,128)(2,1)S(1)} %slice_dynamic-update-slice_fusion.2.refs_0_, bf16[768,512]{1,0:T(8,128)(2,1)S(1)} %pad_maximum_fusion.refs_1_, ...), custom_call_target="tpu_custom_call" | custom-call | flops 3221225472 | bytes 20000000 | tf_op jit(solution)/shard_map/project/pallas_call | solution.py:267
  43.1 3.0 %collective-permute-start.12 = (bf16[768,512]{1,0:T(8,128)(2,1)S(1)}, bf16[768,512]{1,0:T(8,128)(2,1)S(1)}, u32[]{:S(2)}, u32[]{:S(2)}) collective-permute-start(bf16[768,512]{1,0:T(8,128)(2,1)S(1)} %collective-permute-done.8.refs_3_), channel_id=1, source_target_pairs={{0,96},{4,28},{8,104},{12,4},{16,112},{20,12},{24,120},{28,20},{32... | collective-permute-start | bytes 2359304 | tf_op jit(solution)/shard_map/ppermute | solution.py:42
  47.9 3.5 %project.6 = (f32[1024,512]{1,0:T(8,128)S(1)}, bf16[2,64,128]{2,1,0:T(8,128)(2,1)S(1)}) custom-call(bf16[1024,6144]{1,0:T(8,128)(2,1)S(1)} %get-tuple-element.84.x_ref, bf16[832,512]{1,0:T(8,128)(2,1)S(1)} %collective-permute-done.7.refs_0_, bf16[768,512]{1,0:T(8,128)(2,1)S(1)} %collective-permute-done.9.refs_1_, ...), custom_call_target="tpu_custom_call" | custom-call | flops 3221225472 | bytes 20000000 | tf_op jit(solution)/shard_map/project/pallas_call | solution.py:267
  51.3 4.4 %collective-permute-done.12.refs_1_ = bf16[768,512]{1,0:T(8,128)(2,1)S(1)} collective-permute-done((bf16[768,512]{1,0:T(8,128)(2,1)S(1)}, bf16[768,512]{1,0:T(8,128)(2,1)S(1)}, u32[]{:S(2)}, u32[]{:S(2)}) %collective-permute-start.12) | collective-permute-done | bytes 786464 | tf_op jit(solution)/shard_map/ppermute | solution.py:42
  57.8 1.8 %project.7 = (f32[1024,512]{1,0:T(8,128)S(1)}, bf16[1,64,128]{2,1,0:T(8,128)(2,1)S(1)}) custom-call(bf16[1024,6144]{1,0:T(8,128)(2,1)S(1)} %get-tuple-element.84.x_ref, bf16[832,512]{1,0:T(8,128)(2,1)S(1)} %collective-permute-done.11.refs_0_, bf16[768,512]{1,0:T(8,128)(2,1)S(1)} %collective-permute-done.12.refs_1_, f32[1024,512]{1,0:T(8,128)S(1)} %get-tuple-element.100.refs_2_), custom_call_target="tpu_custom_call" | custom-call | flops 1610612736 | bytes 10000000 | tf_op jit(solution)/shard_map/project/pallas_call | solution.py:267
  59.6 1.8 %project.8 = (f32[1024,512]{1,0:T(8,128)S(1)}, bf16[1,64,128]{2,1,0:T(8,128)(2,1)S(1)}) custom-call(bf16[1024,6144]{1,0:T(8,128)(2,1)S(1)} %get-tuple-element.84.x_ref, bf16[832,512]{1,0:T(8,128)(2,1)S(1)} %collective-permute-done.13.refs_0_, bf16[768,512]{1,0:T(8,128)(2,1)S(1)} %collective-permute-done.14.refs_1_, ...), custom_call_target="tpu_custom_call" | custom-call | flops 1610612736 | bytes 10000000 | tf_op jit(solution)/shard_map/project/pallas_call | solution.py:267
  61.5 1.8 %project.9 = (f32[1024,512]{1,0:T(8,128)S(1)}, bf16[1,64,128]{2,1,0:T(8,128)(2,1)S(1)}) custom-call(bf16[1024,6144]{1,0:T(8,128)(2,1)S(1)} %get-tuple-element.84.x_ref, bf16[832,512]{1,0:T(8,128)(2,1)S(1)} %collective-permute-done.15.refs_0_, bf16[768,512]{1,0:T(8,128)(2,1)S(1)} %collective-permute-done.16.refs_1_, f32[1024,512]{1,0:T(8,128)S(1)} %get-tuple-element.109.refs_2_), custom_call_target="tpu_custom_call" | custom-call | flops 1610612736 | bytes 10000000 | tf_op jit(solution)/shard_map/project/pallas_call | solution.py:267
  63.3 3.5 %post.1 = (bf16[1024,1024]{1,0:T(8,128)(2,1)S(1)}, f32[512,128]{1,0:T(8,128)S(1)}, f32[512,128]{1,0:T(8,128)S(1)}, bf16[1,64,128]{2,1,0:T(8,128)(2,1)S(1)}, bf16...) custom-call(f32[40,128]{1,0:T(8,128)S(1)} %get-tuple-element.103.dec, ...), custom_call_target="tpu_custom_call" | custom-call | tf_op jit(solution)/shard_map/post/pallas_call | solution.py:326
  67.1 1.4 %collective-permute-done.19.recv_ref = f32[512,128]{1,0:T(8,128)S(1)} collective-permute-done((f32[512,128]{1,0:T(8,128)S(1)}, f32[512,128]{1,0:T(8,128)S(1)}, u32[]{:S(2)}, u32[]{:S(2)}) %collective-permute-start.19) | collective-permute-done | bytes 262176 | tf_op jit(solution)/shard_map/ppermute | solution.py:26
  68.7 1.9 %collective-permute-start.21 = (bf16[512,128]{1,0:T(8,128)(2,1)S(1)}, bf16[512,128]{1,0:T(8,128)(2,1)S(1)}, u32[]{:S(2)}, u32[]{:S(2)}) collective-permute-start(bf16[512,128]{1,0:T(8,128)(2,1)S(1)} %get-tuple-element.118), channel_id=1, source_target_pairs={{0,16},{4,68},{8,24},{12,76},{16,0},{20,84},{24,8},{28,92},{32,48}... | collective-permute-start | bytes 393224 | tf_op jit(solution)/shard_map/ppermute | solution.py:42
  70.6 1.3 %collective-permute-start.22 = (bf16[512,128]{1,0:T(8,128)(2,1)S(1)}, bf16[512,128]{1,0:T(8,128)(2,1)S(1)}, u32[]{:S(2)}, u32[]{:S(2)}) collective-permute-start(bf16[512,128]{1,0:T(8,128)(2,1)S(1)} %get-tuple-element.118), channel_id=1, source_target_pairs={{0,24},{4,100},{8,0},{12,108},{16,8},{20,116},{24,16},{28,124},{32... | collective-permute-start | bytes 393224 | tf_op jit(solution)/shard_map/ppermute | solution.py:42
  72.0 2.6 %within.1.comb_ref = f32[2,1024,1024]{2,1,0:T(8,128)S(1)} custom-call(f32[8,1024]{1,0:T(8,128)S(1)} %copy-done.2, bf16[1024,1024]{1,0:T(8,128)(2,1)S(1)} %get-tuple-element.119.v_ref, bf16[8,3,128,256]{3,2,1,0:T(8,128)(2,1)S(1)} %get-tuple-element.120.st_ref, bf16[1024,1024]{1,0:T(8,128)(2,1)S(1)} %get-tuple-element.121.q_ref, ...), custom_call_target="tpu_custom_call" | custom-call | flops 3000000000 | bytes 10000000 | tf_op jit(solution)/shard_map/within/pallas_call | solution.py:367
  74.6 1.7 %collective-permute-done.20.r1 = bf16[512,128]{1,0:T(8,128)(2,1)S(1)} collective-permute-done((bf16[512,128]{1,0:T(8,128)(2,1)S(1)}, bf16[512,128]{1,0:T(8,128)(2,1)S(1)}, u32[]{:S(2)}, u32[]{:S(2)}) %collective-permute-start.20) | collective-permute-done | bytes 131104 | tf_op jit(solution)/shard_map/ppermute | solution.py:42
  78.2 3.5 %collective-permute-start.24 = (bf16[512,128]{1,0:T(8,128)(2,1)S(1)}, bf16[512,128]{1,0:T(8,128)(2,1)S(1)}, u32[]{:S(2)}, u32[]{:S(2)}) collective-permute-start(bf16[512,128]{1,0:T(8,128)(2,1)S(1)} %get-tuple-element.128), channel_id=1, source_target_pairs={{0,64},{4,20},{8,72},{12,28},{16,80},{20,4},{24,88},{28,12},{32,96... | collective-permute-start | bytes 393224 | tf_op jit(solution)/shard_map/ppermute | solution.py:42
  82.6 1.2 %collective-permute-done.23.r1 = bf16[512,128]{1,0:T(8,128)(2,1)S(1)} collective-permute-done((bf16[512,128]{1,0:T(8,128)(2,1)S(1)}, bf16[512,128]{1,0:T(8,128)(2,1)S(1)}, u32[]{:S(2)}, u32[]{:S(2)}) %collective-permute-start.23) | collective-permute-done | bytes 131104 | tf_op jit(solution)/shard_map/ppermute | solution.py:42
  83.8 2.2 %collective-permute-done.24.r2 = bf16[512,128]{1,0:T(8,128)(2,1)S(1)} collective-permute-done((bf16[512,128]{1,0:T(8,128)(2,1)S(1)}, bf16[512,128]{1,0:T(8,128)(2,1)S(1)}, u32[]{:S(2)}, u32[]{:S(2)}) %collective-permute-start.24) | collective-permute-done | bytes 131104 | tf_op jit(solution)/shard_map/ppermute | solution.py:42
  87.1 2.2 %outer.2 = (f32[1024,512]{1,0:T(8,128)S(1)}, f32[8,128]{1,0:T(8,128)S(1)}) custom-call(f32[8,128]{1,0:T(8,128)S(1)} %get-tuple-element.71.sf, f32[8,1024]{1,0:T(8,128)S(1)} %copy-done.2, f32[512,128]{1,0:T(8,128)S(1)} %get-tuple-element.130.state_ref, f32[2,1024,1024]{2,1,0:T(8,128)S(1)} %within.1.comb_ref, bf16[1024,1024]{1,0:T(8,128)(2,1)S(1)} %copy-done), custom_call_target="tpu_custom_call" | custom-call | flops 600000000 | bytes 6000000 | tf_op jit(solution)/shard_map/outer/pallas_call | solution.py:509
  89.4 2.2 %outer.3 = (f32[1024,512]{1,0:T(8,128)S(1)}, f32[8,128]{1,0:T(8,128)S(1)}) custom-call(f32[8,128]{1,0:T(8,128)S(1)} %get-tuple-element.71.sf, f32[8,1024]{1,0:T(8,128)S(1)} %copy-done.2, f32[512,128]{1,0:T(8,128)S(1)} %collective-permute-done.26.state_ref, f32[2,1024,1024]{2,1,0:T(8,128)S(1)} %within.1.comb_ref, bf16[1024,1024]{1,0:T(8,128)(2,1)S(1)} %copy-done, ...), custom_call_target="tpu_custom_call" | custom-call | flops 600000000 | bytes 6000000 | tf_op jit(solution)/shard_map/outer/pallas_call | solution.py:509
  91.6 1.6 %collective-permute-start.27 = (f32[8,128]{1,0:T(8,128)S(1)}, f32[8,128]{1,0:T(8,128)S(1)}, u32[]{:S(2)}, u32[]{:S(2)}) collective-permute-start(f32[8,128]{1,0:T(8,128)S(1)} %get-tuple-element.136.s0), channel_id=1, source_target_pairs={{0,1},{1,2},{2,3},{3,0},{4,5},{5,6},{6,7},{7,4},{8,9},{9,10},{10,1... | collective-permute-start | bytes 12296 | tf_op jit(solution)/shard_map/ppermute | solution.py:30
  93.2 2.9 %collective-permute-start.28 = (f32[8,128]{1,0:T(8,128)S(1)}, f32[8,128]{1,0:T(8,128)S(1)}, u32[]{:S(2)}, u32[]{:S(2)}) collective-permute-start(f32[8,128]{1,0:T(8,128)S(1)} %get-tuple-element.136.s0), channel_id=1, source_target_pairs={{0,2},{1,3},{2,0},{3,1},{4,6},{5,7},{6,4},{7,5},{8,10},{9,11},{10,... | collective-permute-start | bytes 12296 | tf_op jit(solution)/shard_map/ppermute | solution.py:30
  96.1 1.3 %collective-permute-start.29 = (f32[8,128]{1,0:T(8,128)S(1)}, f32[8,128]{1,0:T(8,128)S(1)}, u32[]{:S(2)}, u32[]{:S(2)}) collective-permute-start(f32[8,128]{1,0:T(8,128)S(1)} %get-tuple-element.136.s0), channel_id=1, source_target_pairs={{0,3},{1,0},{2,1},{3,2},{4,7},{5,4},{6,5},{7,6},{8,11},{9,8},{10,9... | collective-permute-start | bytes 12296 | tf_op jit(solution)/shard_map/ppermute | solution.py:30
  98.4 1.4 %collective-permute-done.29.s3 = f32[8,128]{1,0:T(8,128)S(1)} collective-permute-done((f32[8,128]{1,0:T(8,128)S(1)}, f32[8,128]{1,0:T(8,128)S(1)}, u32[]{:S(2)}, u32[]{:S(2)}) %collective-permute-start.29) | collective-permute-done | bytes 4128 | tf_op jit(solution)/shard_map/ppermute | solution.py:30
  99.8 1.6 %norm.1 = bf16[1024,1024]{1,0:T(8,128)(2,1)} custom-call(f32[1024,512]{1,0:T(8,128)S(1)} %get-tuple-element.132.mine_ref, f32[1024,512]{1,0:T(8,128)S(1)} %get-tuple-element.135.other_ref, f32[8,128]{1,0:T(8,128)S(1)} %get-tuple-element.136.s0, f32[8,128]{1,0:T(8,128)S(1)} %collective-permute-done.27.s1, f32[8,128]{1,0:T(8,128)S(1)} %collective-permute-done.28.s2, ...), custom_call_target="tpu_custom_call" | custom-call | tf_op jit(solution)/shard_map/norm/pallas_call | solution.py:543
  (67 shorter events, 13.2 us)
Async XLA Ops:
  1.1 2.2 %collective-permute-start = (bf16[192,512]{1,0:T(8,128)(2,1)S(1)}, bf16[192,512]{1,0:T(8,128)(2,1)S(1)}, u32[]{:S(2)}, u32[]{:S(2)}) collective-permute-start(bf16[192,512]{1,0:T(8,128)(2,1)S(1)} %get-tuple-element.138), channel_id=1, source_target_pairs={{0,4},{4,0},{1,5},{5,1},{2,6},{6,2},{3,7},{7,3},{8,12},{12,8},{9,1... | collective-permute-start | bytes 589832 | tf_op jit(solution)/shard_map/ppermute | solution.py:26
  3.4 9.7 %collective-permute-start.2 = (bf16[400,512]{1,0:T(8,128)(2,1)S(1)}, bf16[400,512]{1,0:T(8,128)(2,1)S(1)}, u32[]{:S(2)}, u32[]{:S(2)}) collective-permute-start(bf16[400,512]{1,0:T(8,128)(2,1)S(1)} %fusion), channel_id=1, source_target_pairs={{0,24},{4,100},{8,0},{12,108},{16,8},{20,116},{24,16},{28,124},{32... | collective-permute-start | bytes 1228808 | tf_op jit(solution)/shard_map/ppermute | solution.py:42
  7.6 9.3 %collective-permute-start.1 = (bf16[400,512]{1,0:T(8,128)(2,1)S(1)}, bf16[400,512]{1,0:T(8,128)(2,1)S(1)}, u32[]{:S(2)}, u32[]{:S(2)}) collective-permute-start(bf16[400,512]{1,0:T(8,128)(2,1)S(1)} %fusion), channel_id=1, source_target_pairs={{0,8},{4,36},{8,16},{12,44},{16,24},{20,52},{24,0},{28,60},{32,40}... | collective-permute-start | bytes 1228808 | tf_op jit(solution)/shard_map/ppermute | solution.py:42
  13.1 10.7 %collective-permute-start.4 = (bf16[208,512]{1,0:T(8,128)(2,1)S(1)}, bf16[208,512]{1,0:T(8,128)(2,1)S(1)}, u32[]{:S(2)}, u32[]{:S(2)}) collective-permute-start(bf16[208,512]{1,0:T(8,128)(2,1)S(1)} %slice.41), channel_id=1, source_target_pairs={{0,24},{4,100},{8,0},{12,108},{16,8},{20,116},{24,16},{28,124},{32... | collective-permute-start | bytes 638984 | tf_op jit(solution)/shard_map/ppermute | solution.py:42
  16.9 13.1 %copy-start.2 = (f32[8,1024]{1,0:T(8,128)S(1)}, f32[8,1024]{1,0:T(8,128)}, u32[]{:S(2)}) copy-start(f32[8,1024]{1,0:T(8,128)} %ld_ref.5) | copy-start | bytes 98308
  16.9 7.0 %collective-permute-start.3 = (bf16[192,512]{1,0:T(8,128)(2,1)S(1)}, bf16[192,512]{1,0:T(8,128)(2,1)S(1)}, u32[]{:S(2)}, u32[]{:S(2)}) collective-permute-start(bf16[192,512]{1,0:T(8,128)(2,1)S(1)} %slice.40), channel_id=1, source_target_pairs={{0,8},{4,36},{8,16},{12,44},{16,24},{20,52},{24,0},{28,60},{32,40}... | collective-permute-start | bytes 589832 | tf_op jit(solution)/shard_map/ppermute | solution.py:42
  24.0 5.6 %collective-permute-start.6 = (bf16[768,512]{1,0:T(8,128)(2,1)S(1)}, bf16[768,512]{1,0:T(8,128)(2,1)S(1)}, u32[]{:S(2)}, u32[]{:S(2)}) collective-permute-start(bf16[768,512]{1,0:T(8,128)(2,1)S(1)} %pad_maximum_fusion.refs_1_), channel_id=1, source_target_pairs={{0,4},{4,0},{1,5},{5,1},{2,6},{6,2},{3,7},{7,3},{8,12},{12,8},{9,1... | collective-permute-start | bytes 2359304 | tf_op jit(solution)/shard_map/ppermute | solution.py:26
  24.2 5.8 %collective-permute-start.5 = (bf16[832,512]{1,0:T(8,128)(2,1)S(1)}, bf16[832,512]{1,0:T(8,128)(2,1)S(1)}, u32[]{:S(2)}, u32[]{:S(2)}) collective-permute-start(bf16[832,512]{1,0:T(8,128)(2,1)S(1)} %slice_dynamic-update-slice_fusion.2.refs_0_), channel_id=1, source_target_pairs={{0,4},{4,0},{1,5},{5,1},{2,6},{6,2},{3,7},{7,3},{8,12},{12,8},{9,1... | collective-permute-start | bytes 2555912 | tf_op jit(solution)/shard_map/ppermute | solution.py:26
  24.7 18.0 %collective-permute-start.7 = (bf16[832,512]{1,0:T(8,128)(2,1)S(1)}, bf16[832,512]{1,0:T(8,128)(2,1)S(1)}, u32[]{:S(2)}, u32[]{:S(2)}) collective-permute-start(bf16[832,512]{1,0:T(8,128)(2,1)S(1)} %slice_dynamic-update-slice_fusion.2.refs_0_), channel_id=1, source_target_pairs={{0,32},{4,12},{8,40},{12,20},{16,48},{20,28},{24,56},{28,4},{32,64... | collective-permute-start | bytes 2555912 | tf_op jit(solution)/shard_map/ppermute | solution.py:42
  26.2 16.5 %collective-permute-start.8 = (bf16[768,512]{1,0:T(8,128)(2,1)S(1)}, bf16[768,512]{1,0:T(8,128)(2,1)S(1)}, u32[]{:S(2)}, u32[]{:S(2)}) collective-permute-start(bf16[768,512]{1,0:T(8,128)(2,1)S(1)} %pad_maximum_fusion.refs_1_), channel_id=1, source_target_pairs={{0,96},{4,28},{8,104},{12,4},{16,112},{20,12},{24,120},{28,20},{32... | collective-permute-start | bytes 2359304 | tf_op jit(solution)/shard_map/ppermute | solution.py:42
  28.0 19.4 %collective-permute-start.10 = (bf16[832,512]{1,0:T(8,128)(2,1)S(1)}, bf16[832,512]{1,0:T(8,128)(2,1)S(1)}, u32[]{:S(2)}, u32[]{:S(2)}) collective-permute-start(bf16[832,512]{1,0:T(8,128)(2,1)S(1)} %slice_dynamic-update-slice_fusion.2.refs_0_), channel_id=1, source_target_pairs={{0,96},{4,28},{8,104},{12,4},{16,112},{20,12},{24,120},{28,20},{32... | collective-permute-start | bytes 2555912 | tf_op jit(solution)/shard_map/ppermute | solution.py:42
  29.5 17.5 %collective-permute-start.9 = (bf16[768,512]{1,0:T(8,128)(2,1)S(1)}, bf16[768,512]{1,0:T(8,128)(2,1)S(1)}, u32[]{:S(2)}, u32[]{:S(2)}) collective-permute-start(bf16[768,512]{1,0:T(8,128)(2,1)S(1)} %pad_maximum_fusion.refs_1_), channel_id=1, source_target_pairs={{0,32},{4,12},{8,40},{12,20},{16,48},{20,28},{24,56},{28,4},{32,64... | collective-permute-start | bytes 2359304 | tf_op jit(solution)/shard_map/ppermute | solution.py:42
  42.8 14.0 %collective-permute-start.11 = (bf16[832,512]{1,0:T(8,128)(2,1)S(1)}, bf16[832,512]{1,0:T(8,128)(2,1)S(1)}, u32[]{:S(2)}, u32[]{:S(2)}) collective-permute-start(bf16[832,512]{1,0:T(8,128)(2,1)S(1)} %collective-permute-done.7.refs_0_), channel_id=1, source_target_pairs={{0,32},{4,12},{8,40},{12,20},{16,48},{20,28},{24,56},{28,4},{32,64... | collective-permute-start | bytes 2555912 | tf_op jit(solution)/shard_map/ppermute | solution.py:42
  43.1 12.7 %collective-permute-start.12 = (bf16[768,512]{1,0:T(8,128)(2,1)S(1)}, bf16[768,512]{1,0:T(8,128)(2,1)S(1)}, u32[]{:S(2)}, u32[]{:S(2)}) collective-permute-start(bf16[768,512]{1,0:T(8,128)(2,1)S(1)} %collective-permute-done.8.refs_3_), channel_id=1, source_target_pairs={{0,96},{4,28},{8,104},{12,4},{16,112},{20,12},{24,120},{28,20},{32... | collective-permute-start | bytes 2359304 | tf_op jit(solution)/shard_map/ppermute | solution.py:42
  47.4 9.9 %collective-permute-start.14 = (bf16[768,512]{1,0:T(8,128)(2,1)S(1)}, bf16[768,512]{1,0:T(8,128)(2,1)S(1)}, u32[]{:S(2)}, u32[]{:S(2)}) collective-permute-start(bf16[768,512]{1,0:T(8,128)(2,1)S(1)} %collective-permute-done.9.refs_1_), channel_id=1, source_target_pairs={{0,4},{4,0},{1,5},{5,1},{2,6},{6,2},{3,7},{7,3},{8,12},{12,8},{9,1... | collective-permute-start | bytes 2359304 | tf_op jit(solution)/shard_map/ppermute | solution.py:26
  47.4 12.3 %collective-permute-start.13 = (bf16[832,512]{1,0:T(8,128)(2,1)S(1)}, bf16[832,512]{1,0:T(8,128)(2,1)S(1)}, u32[]{:S(2)}, u32[]{:S(2)}) collective-permute-start(bf16[832,512]{1,0:T(8,128)(2,1)S(1)} %collective-permute-done.7.refs_0_), channel_id=1, source_target_pairs={{0,4},{4,0},{1,5},{5,1},{2,6},{6,2},{3,7},{7,3},{8,12},{12,8},{9,1... | collective-permute-start | bytes 2555912 | tf_op jit(solution)/shard_map/ppermute | solution.py:26
  56.7 4.7 %collective-permute-start.15 = (bf16[832,512]{1,0:T(8,128)(2,1)S(1)}, bf16[832,512]{1,0:T(8,128)(2,1)S(1)}, u32[]{:S(2)}, u32[]{:S(2)}) collective-permute-start(bf16[832,512]{1,0:T(8,128)(2,1)S(1)} %collective-permute-done.10.refs_2_), channel_id=1, source_target_pairs={{0,4},{4,0},{1,5},{5,1},{2,6},{6,2},{3,7},{7,3},{8,12},{12,8},{9,1... | collective-permute-start | bytes 2555912 | tf_op jit(solution)/shard_map/ppermute | solution.py:26
  56.7 4.7 %collective-permute-start.16 = (bf16[768,512]{1,0:T(8,128)(2,1)S(1)}, bf16[768,512]{1,0:T(8,128)(2,1)S(1)}, u32[]{:S(2)}, u32[]{:S(2)}) collective-permute-start(bf16[768,512]{1,0:T(8,128)(2,1)S(1)} %collective-permute-done.8.refs_3_), channel_id=1, source_target_pairs={{0,4},{4,0},{1,5},{5,1},{2,6},{6,2},{3,7},{7,3},{8,12},{12,8},{9,1... | collective-permute-start | bytes 2359304 | tf_op jit(solution)/shard_map/ppermute | solution.py:26
  57.2 6.1 %collective-permute-start.17 = (bf16[832,512]{1,0:T(8,128)(2,1)S(1)}, bf16[832,512]{1,0:T(8,128)(2,1)S(1)}, u32[]{:S(2)}, u32[]{:S(2)}) collective-permute-start(bf16[832,512]{1,0:T(8,128)(2,1)S(1)} %collective-permute-done.11.refs_0_), channel_id=1, source_target_pairs={{0,4},{4,0},{1,5},{5,1},{2,6},{6,2},{3,7},{7,3},{8,12},{12,8},{9,1... | collective-permute-start | bytes 2555912 | tf_op jit(solution)/shard_map/ppermute | solution.py:26
  57.2 6.1 %collective-permute-start.18 = (bf16[768,512]{1,0:T(8,128)(2,1)S(1)}, bf16[768,512]{1,0:T(8,128)(2,1)S(1)}, u32[]{:S(2)}, u32[]{:S(2)}) collective-permute-start(bf16[768,512]{1,0:T(8,128)(2,1)S(1)} %collective-permute-done.12.refs_1_), channel_id=1, source_target_pairs={{0,4},{4,0},{1,5},{5,1},{2,6},{6,2},{3,7},{7,3},{8,12},{12,8},{9,1... | collective-permute-start | bytes 2359304 | tf_op jit(solution)/shard_map/ppermute | solution.py:26
  66.9 1.6 %collective-permute-start.19 = (f32[512,128]{1,0:T(8,128)S(1)}, f32[512,128]{1,0:T(8,128)S(1)}, u32[]{:S(2)}, u32[]{:S(2)}) collective-permute-start(f32[512,128]{1,0:T(8,128)S(1)} %get-tuple-element.115), channel_id=1, source_target_pairs={{0,4},{4,0},{1,5},{5,1},{2,6},{6,2},{3,7},{7,3},{8,12},{12,8},{9,1... | collective-permute-start | bytes 786440 | tf_op jit(solution)/shard_map/ppermute | solution.py:26
  68.6 7.7 %collective-permute-start.20 = (bf16[512,128]{1,0:T(8,128)(2,1)S(1)}, bf16[512,128]{1,0:T(8,128)(2,1)S(1)}, u32[]{:S(2)}, u32[]{:S(2)}) collective-permute-start(bf16[512,128]{1,0:T(8,128)(2,1)S(1)} %get-tuple-element.118), channel_id=1, source_target_pairs={{0,8},{4,36},{8,16},{12,44},{16,24},{20,52},{24,0},{28,60},{32,40}... | collective-permute-start | bytes 393224 | tf_op jit(solution)/shard_map/ppermute | solution.py:42
  68.7 7.6 %collective-permute-start.21 = (bf16[512,128]{1,0:T(8,128)(2,1)S(1)}, bf16[512,128]{1,0:T(8,128)(2,1)S(1)}, u32[]{:S(2)}, u32[]{:S(2)}) collective-permute-start(bf16[512,128]{1,0:T(8,128)(2,1)S(1)} %get-tuple-element.118), channel_id=1, source_target_pairs={{0,16},{4,68},{8,24},{12,76},{16,0},{20,84},{24,8},{28,92},{32,48}... | collective-permute-start | bytes 393224 | tf_op jit(solution)/shard_map/ppermute | solution.py:42
  70.6 6.6 %collective-permute-start.22 = (bf16[512,128]{1,0:T(8,128)(2,1)S(1)}, bf16[512,128]{1,0:T(8,128)(2,1)S(1)}, u32[]{:S(2)}, u32[]{:S(2)}) collective-permute-start(bf16[512,128]{1,0:T(8,128)(2,1)S(1)} %get-tuple-element.118), channel_id=1, source_target_pairs={{0,24},{4,100},{8,0},{12,108},{16,8},{20,116},{24,16},{28,124},{32... | collective-permute-start | bytes 393224 | tf_op jit(solution)/shard_map/ppermute | solution.py:42
  71.9 15.2 %copy-start = (bf16[1024,1024]{1,0:T(8,128)(2,1)S(1)}, bf16[1024,1024]{1,0:T(8,128)(2,1)}, u32[]{:S(2)}) copy-start(bf16[1024,1024]{1,0:T(8,128)(2,1)} %q_ref.1) | copy-start | bytes 6291460
  77.6 6.2 %collective-permute-start.23 = (bf16[512,128]{1,0:T(8,128)(2,1)S(1)}, bf16[512,128]{1,0:T(8,128)(2,1)S(1)}, u32[]{:S(2)}, u32[]{:S(2)}) collective-permute-start(bf16[512,128]{1,0:T(8,128)(2,1)S(1)} %get-tuple-element.127), channel_id=1, source_target_pairs={{0,32},{4,12},{8,40},{12,20},{16,48},{20,28},{24,56},{28,4},{32,64... | collective-permute-start | bytes 393224 | tf_op jit(solution)/shard_map/ppermute | solution.py:42
  78.2 7.8 %collective-permute-start.24 = (bf16[512,128]{1,0:T(8,128)(2,1)S(1)}, bf16[512,128]{1,0:T(8,128)(2,1)S(1)}, u32[]{:S(2)}, u32[]{:S(2)}) collective-permute-start(bf16[512,128]{1,0:T(8,128)(2,1)S(1)} %get-tuple-element.128), channel_id=1, source_target_pairs={{0,64},{4,20},{8,72},{12,28},{16,80},{20,4},{24,88},{28,12},{32,96... | collective-permute-start | bytes 393224 | tf_op jit(solution)/shard_map/ppermute | solution.py:42
  81.7 5.0 %collective-permute-start.25 = (bf16[512,128]{1,0:T(8,128)(2,1)S(1)}, bf16[512,128]{1,0:T(8,128)(2,1)S(1)}, u32[]{:S(2)}, u32[]{:S(2)}) collective-permute-start(bf16[512,128]{1,0:T(8,128)(2,1)S(1)} %get-tuple-element.129), channel_id=1, source_target_pairs={{0,96},{4,28},{8,104},{12,4},{16,112},{20,12},{24,120},{28,20},{32... | collective-permute-start | bytes 393224 | tf_op jit(solution)/shard_map/ppermute | solution.py:42
  86.8 2.5 %collective-permute-start.26 = (f32[512,128]{1,0:T(8,128)S(1)}, f32[512,128]{1,0:T(8,128)S(1)}, u32[]{:S(2)}, u32[]{:S(2)}) collective-permute-start(f32[512,128]{1,0:T(8,128)S(1)} %get-tuple-element.133), channel_id=1, source_target_pairs={{0,4},{4,0},{1,5},{5,1},{2,6},{6,2},{3,7},{7,3},{8,12},{12,8},{9,1... | collective-permute-start | bytes 786440 | tf_op jit(solution)/shard_map/ppermute | solution.py:26
  91.6 5.9 %collective-permute-start.27 = (f32[8,128]{1,0:T(8,128)S(1)}, f32[8,128]{1,0:T(8,128)S(1)}, u32[]{:S(2)}, u32[]{:S(2)}) collective-permute-start(f32[8,128]{1,0:T(8,128)S(1)} %get-tuple-element.136.s0), channel_id=1, source_target_pairs={{0,1},{1,2},{2,3},{3,0},{4,5},{5,6},{6,7},{7,4},{8,9},{9,10},{10,1... | collective-permute-start | bytes 12296 | tf_op jit(solution)/shard_map/ppermute | solution.py:30
  93.2 5.1 %collective-permute-start.28 = (f32[8,128]{1,0:T(8,128)S(1)}, f32[8,128]{1,0:T(8,128)S(1)}, u32[]{:S(2)}, u32[]{:S(2)}) collective-permute-start(f32[8,128]{1,0:T(8,128)S(1)} %get-tuple-element.136.s0), channel_id=1, source_target_pairs={{0,2},{1,3},{2,0},{3,1},{4,6},{5,7},{6,4},{7,5},{8,10},{9,11},{10,... | collective-permute-start | bytes 12296 | tf_op jit(solution)/shard_map/ppermute | solution.py:30
  96.1 3.6 %collective-permute-start.29 = (f32[8,128]{1,0:T(8,128)S(1)}, f32[8,128]{1,0:T(8,128)S(1)}, u32[]{:S(2)}, u32[]{:S(2)}) collective-permute-start(f32[8,128]{1,0:T(8,128)S(1)} %get-tuple-element.136.s0), channel_id=1, source_target_pairs={{0,3},{1,0},{2,1},{3,2},{4,7},{5,4},{6,5},{7,6},{8,11},{9,8},{10,9... | collective-permute-start | bytes 12296 | tf_op jit(solution)/shard_map/ppermute | solution.py:30
  (3 other events, 11.8 us)

commit v5 on v4

--- a/solution.py
+++ b/solution.py
@@ -565,24 +565,17 @@
         jnp.concatenate([my_w, recv_w, fx], axis=0),
         jnp.concatenate([recv_w, my_w, fx], axis=0),
     )
-    rows = CHIP // 2
-    up = crossed(chip_w, "z", "x", 1, 1)
-    dn = crossed(chip_w, "z", "x", -1, -1)
-    far_a = crossed(up[:rows], "z", "x", 1, 1)
-    far_b = crossed(dn[rows:], "z", "x", -1, -1)
-    chip_w, up, dn, far_a, far_b, ld, q, k = bar((chip_w, up, dn, far_a, far_b, ld, q, k))
-    p_lo = jnp.concatenate(
-        [chip_w[:CHIP], up[:CHIP], chip_w[CHIP:], up[CHIP:], far_b[rows:], dn[CHIP:]], axis=0
-    )
-    p_hi = jnp.concatenate([far_a, far_b[:rows], dn[:CHIP]], axis=0)
+    chip_w, ld, q, k = bar((chip_w, ld, q, k))
+    line = [chip_w] + [crossed(chip_w, "z", "x", d, d) for d in (1, 2, 3)]
+    w, kd, xv = pre(ld, q, k, inputs)
+    line, w = bar((tuple(line), w))
+    p_lo = jnp.concatenate([a[:CHIP] for a in line[:2]] + [a[CHIP:] for a in line], axis=0)
+    p_hi = jnp.concatenate([a[:CHIP] for a in line[2:]], axis=0)
     up_lo = crossed(p_lo, "x", "z", 1, 1)
     dn_hi = crossed(p_hi, "x", "z", -1, -1)
     up_hi = crossed(p_hi, "x", "z", 1, 1)
     dn_lo = crossed(p_lo, "x", "z", -1, -1)
-    s_lo, s_hi = swap(p_lo), swap(p_hi)
-    s_lo, s_hi, ld, q, k = bar((s_lo, s_hi, ld, q, k))
-    w, kd, xv = pre(ld, q, k, inputs)
-    bufs = (p_lo, p_hi, s_lo, s_hi)
+    bufs = (p_lo, p_hi, swap(p_lo), swap(p_hi))
     sums, t_own = mm(((True, 0), (False, 0)), xv, bufs, here=True)
     up_lo, dn_hi, sums = bar((up_lo, dn_hi, sums))
     op_lo = crossed(up_lo, "x", "z", 1, 1)
@@ -591,10 +584,11 @@
     swapped = (swap(up_lo), swap(up_hi))
     bufs = (up_lo, up_hi, dn_lo, dn_hi)
     mine, t_mine = mm(((True, 1), (True, 3)), xv, bufs, 0, sums, True)
-    op_lo, op_hi, dn_lo, dn_hi, mine = bar((op_lo, op_hi, dn_lo, dn_hi, mine))
+    dn_lo, dn_hi, mine = bar((dn_lo, dn_hi, mine))
+    op_lo, op_hi, done = bar((op_lo, op_hi, mine))
     theirs, t_up = mm(((False, 1),), xv, swapped, 1, sums, True)
     theirs, t_dn = mm(((False, 3),), xv, (swap(dn_lo), swap(dn_hi)), -1, theirs, True)
-    mine, t_op = mm(((True, 2),), xv, (op_lo, op_hi), -1, mine, True)
+    mine, t_op = mm(((True, 2),), xv, (op_lo, op_hi), -1, done, True)
     bufs = [swap(op_lo), swap(op_hi)]
     v, own, give, t_last, st, qv, wv = post(
         (False, 2), vmem(dec), q, kd, w, mine, theirs, xv, [vmem(a) for a in bufs]

time: 102 us -> 97.6 us (0.957)
  waiting for transfers between devices: 29.3 us -> 25.3 us
    ppermute x16 -> x15, waiting for transfers between devices: 25.6 us -> 21.7 us  [crossed(): return lax.ppermute(a, SEQ, pairs)]
    unnamed x15 -> x17, local copies, waits for them, and re-layouts: 1.49 us -> 2.25 us
    ppermute x16 -> x15, starting transfers between devices: 24.9 us -> 24.3 us  [crossed(): return lax.ppermute(a, SEQ, pairs)]
  transfers between devices with their start and end apart: 30 -> 29, of which waited for: 14 -> 14; matrix products, arithmetic and copies ran while one was open for 0% -> 0% of each run, Pallas kernels for 27% -> 28%
where the time goes in v5:
time: 97.6 us; the launch traced here: 97.4 us
  Pallas kernels  35.5 us (36%)
  starting transfers between devices  32.5 us (33%)
  waiting for transfers between devices  25.3 us (26%)
  local copies, waits for them, and re-layouts  3.35 us (3%)
    ppermute x15, starting transfers between devices, crossed(): return lax.ppermute(a, SEQ, pairs)  24.3 us
    ppermute x15, waiting for transfers between devices, crossed(): return lax.ppermute(a, SEQ, pairs)  21.7 us
    pallas_call x5, Pallas kernels, mm(): pl.pallas_call(functools.partial(mm_kernel, jobs, plane, here), in_specs=...  12.4 us
    pallas_call x1, Pallas kernels, pre(): pl.pallas_call(pre_kernel, in_specs=[VM, HB, HB, HB], out_specs=[HB, HB,...  9.24 us
    ppermute x3, starting transfers between devices, ring(): return lax.ppermute(a, axis, [(i, (i + step) % 4) for i in range(4)])  5.89 us
    pallas_call x2, Pallas kernels, outer(): pl.pallas_call(functools.partial(outer_kernel, side), in_specs=[VM] * (5...  4.45 us
    pallas_call x1, Pallas kernels, post(): pl.pallas_call(functools.partial(post_kernel, job), in_specs=[VM, HB, HB,...  3.52 us
    pallas_call x1, Pallas kernels, within(): pl.pallas_call(within_kernel, in_specs=[VM] * 5, out_specs=VM, out_shape=...  2.65 us
  transfers between devices with their start and end apart: 29, of which 14 were waited for; matrix products, arithmetic and copies ran while one was open for 0% of the time, Pallas kernels for 28%

profile of v5, /device:TPU:0, one launch (start us, length us, event | category | flops | bytes accessed | tf_op | source)
XLA Modules:
  0.0 97.4 jit_solution(677545274385215460)
XLA Ops:
  0.0 1.0 %constant_dynamic-slice_fusion.1 = (bf16[192,512]{1,0:T(8,128)(2,1)S(1)}, bf16[192,512]{1,0:T(8,128)(2,1)S(1)}) fusion(bf16[192,1024]{1,0:T(8,128)(2,1)} %param.10, s32[]{:T(128)S(6)} %select_n.15, s32[]{:T(128)S(6)} %select_n.16), kind=kLoop, calls=%fused_computation.11 | loop fusion | bytes 786440 | tf_op jit(solution)/shard_map/dynamic_slice | solution.py:559
  3.4 2.1 %collective-permute-start.1 = (bf16[400,512]{1,0:T(8,128)(2,1)S(1)}, bf16[400,512]{1,0:T(8,128)(2,1)S(1)}, u32[]{:S(2)}, u32[]{:S(2)}) collective-permute-start(bf16[400,512]{1,0:T(8,128)(2,1)S(1)} %fusion), channel_id=1, source_target_pairs={{0,8},{4,36},{8,16},{12,44},{16,24},{20,52},{24,0},{28,60},{32,40}... | collective-permute-start | bytes 1228808 | tf_op jit(solution)/shard_map/ppermute | solution.py:42
  5.5 3.6 %collective-permute-start.2 = (bf16[400,512]{1,0:T(8,128)(2,1)S(1)}, bf16[400,512]{1,0:T(8,128)(2,1)S(1)}, u32[]{:S(2)}, u32[]{:S(2)}) collective-permute-start(bf16[400,512]{1,0:T(8,128)(2,1)S(1)} %fusion), channel_id=1, source_target_pairs={{0,16},{4,68},{8,24},{12,76},{16,0},{20,84},{24,8},{28,92},{32,48}... | collective-permute-start | bytes 1228808 | tf_op jit(solution)/shard_map/ppermute | solution.py:42
  10.8 9.2 %pre.1 = (bf16[8,4,256,256]{3,2,1,0:T(8,128)(2,1)}, bf16[8,4,128,256]{3,2,1,0:T(8,128)(2,1)}, bf16[1024,6144]{1,0:T(8,128)(2,1)S(1)}) custom-call(f32[8,1024]{1,0:T(8,128)S(1)} %copy-done.2, bf16[1024,1024]{1,0:T(8,128)(2,1)} %q_ref.1, bf16[1024,1024]{1,0:T(8,128)(2,1)} %k_hbm, bf16[1024,6144]{1,0:T(8,128)(2,1)} %x_hbm.1), custom_call_target="tpu_custom_call" | custom-call | flops 1000000000 | bytes 10000000 | tf_op jit(solution)/shard_map/pre/pallas_call | solution.py:187
  21.0 1.5 %collective-permute-start.6 = (bf16[832,512]{1,0:T(8,128)(2,1)S(1)}, bf16[832,512]{1,0:T(8,128)(2,1)S(1)}, u32[]{:S(2)}, u32[]{:S(2)}) collective-permute-start(bf16[832,512]{1,0:T(8,128)(2,1)S(1)} %slice_dynamic-update-slice_fusion.2.refs_0_), channel_id=1, source_target_pairs={{0,32},{4,12},{8,40},{12,20},{16,48},{20,28},{24,56},{28,4},{32,64... | collective-permute-start | bytes 2555912 | tf_op jit(solution)/shard_map/ppermute | solution.py:42
  22.5 1.7 %collective-permute-start.7 = (bf16[768,512]{1,0:T(8,128)(2,1)S(1)}, bf16[768,512]{1,0:T(8,128)(2,1)S(1)}, u32[]{:S(2)}, u32[]{:S(2)}) collective-permute-start(bf16[768,512]{1,0:T(8,128)(2,1)S(1)} %pad_maximum_fusion.refs_1_), channel_id=1, source_target_pairs={{0,96},{4,28},{8,104},{12,4},{16,112},{20,12},{24,120},{28,20},{32... | collective-permute-start | bytes 2359304 | tf_op jit(solution)/shard_map/ppermute | solution.py:42
  24.3 1.5 %collective-permute-start.9 = (bf16[832,512]{1,0:T(8,128)(2,1)S(1)}, bf16[832,512]{1,0:T(8,128)(2,1)S(1)}, u32[]{:S(2)}, u32[]{:S(2)}) collective-permute-start(bf16[832,512]{1,0:T(8,128)(2,1)S(1)} %slice_dynamic-update-slice_fusion.2.refs_0_), channel_id=1, source_target_pairs={{0,96},{4,28},{8,104},{12,4},{16,112},{20,12},{24,120},{28,20},{32... | collective-permute-start | bytes 2555912 | tf_op jit(solution)/shard_map/ppermute | solution.py:42
  26.3 3.5 %project.5 = (f32[4,1024,512]{2,1,0:T(8,128)S(1)}, bf16[2,64,128]{2,1,0:T(8,128)(2,1)S(1)}) custom-call(bf16[1024,6144]{1,0:T(8,128)(2,1)S(1)} %get-tuple-element.73.x_ref, bf16[832,512]{1,0:T(8,128)(2,1)S(1)} %slice_dynamic-update-slice_fusion.2.refs_0_, bf16[768,512]{1,0:T(8,128)(2,1)S(1)} %pad_maximum_fusion.refs_1_, ...), custom_call_target="tpu_custom_call" | custom-call | flops 3221225472 | bytes 20000000 | tf_op jit(solution)/shard_map/project/pallas_call | solution.py:267
  29.8 4.7 %collective-permute-done.7.refs_3_ = bf16[768,512]{1,0:T(8,128)(2,1)S(1)} collective-permute-done((bf16[768,512]{1,0:T(8,128)(2,1)S(1)}, bf16[768,512]{1,0:T(8,128)(2,1)S(1)}, u32[]{:S(2)}, u32[]{:S(2)}) %collective-permute-start.7) | collective-permute-done | bytes 786464 | tf_op jit(solution)/shard_map/ppermute | solution.py:42
  34.9 2.5 %collective-permute-start.11 = (bf16[768,512]{1,0:T(8,128)(2,1)S(1)}, bf16[768,512]{1,0:T(8,128)(2,1)S(1)}, u32[]{:S(2)}, u32[]{:S(2)}) collective-permute-start(bf16[768,512]{1,0:T(8,128)(2,1)S(1)} %collective-permute-done.7.refs_3_), channel_id=1, source_target_pairs={{0,96},{4,28},{8,104},{12,4},{16,112},{20,12},{24,120},{28,20},{32... | collective-permute-start | bytes 2359304 | tf_op jit(solution)/shard_map/ppermute | solution.py:42
  37.5 5.9 %collective-permute-done.8.refs_1_ = bf16[768,512]{1,0:T(8,128)(2,1)S(1)} collective-permute-done((bf16[768,512]{1,0:T(8,128)(2,1)S(1)}, bf16[768,512]{1,0:T(8,128)(2,1)S(1)}, u32[]{:S(2)}, u32[]{:S(2)}) %collective-permute-start.8) | collective-permute-done | bytes 786464 | tf_op jit(solution)/shard_map/ppermute | solution.py:42
  44.2 3.5 %project.6 = (f32[1024,512]{1,0:T(8,128)S(1)}, bf16[2,64,128]{2,1,0:T(8,128)(2,1)S(1)}) custom-call(bf16[1024,6144]{1,0:T(8,128)(2,1)S(1)} %get-tuple-element.73.x_ref, bf16[832,512]{1,0:T(8,128)(2,1)S(1)} %collective-permute-done.6.refs_0_, bf16[768,512]{1,0:T(8,128)(2,1)S(1)} %collective-permute-done.8.refs_1_, ...), custom_call_target="tpu_custom_call" | custom-call | flops 3221225472 | bytes 20000000 | tf_op jit(solution)/shard_map/project/pallas_call | solution.py:267
  47.7 4.3 %collective-permute-done.11.refs_1_ = bf16[768,512]{1,0:T(8,128)(2,1)S(1)} collective-permute-done((bf16[768,512]{1,0:T(8,128)(2,1)S(1)}, bf16[768,512]{1,0:T(8,128)(2,1)S(1)}, u32[]{:S(2)}, u32[]{:S(2)}) %collective-permute-start.11) | collective-permute-done | bytes 786464 | tf_op jit(solution)/shard_map/ppermute | solution.py:42
  53.0 1.8 %project.7 = (f32[1024,512]{1,0:T(8,128)S(1)}, bf16[1,64,128]{2,1,0:T(8,128)(2,1)S(1)}) custom-call(bf16[1024,6144]{1,0:T(8,128)(2,1)S(1)} %get-tuple-element.73.x_ref, bf16[832,512]{1,0:T(8,128)(2,1)S(1)} %collective-permute-done.10.refs_0_, bf16[768,512]{1,0:T(8,128)(2,1)S(1)} %collective-permute-done.11.refs_1_, f32[1024,512]{1,0:T(8,128)S(1)} %get-tuple-element.94.refs_2_), custom_call_target="tpu_custom_call" | custom-call | flops 1610612736 | bytes 10000000 | tf_op jit(solution)/shard_map/project/pallas_call | solution.py:267
  54.9 1.8 %project.8 = (f32[1024,512]{1,0:T(8,128)S(1)}, bf16[1,64,128]{2,1,0:T(8,128)(2,1)S(1)}) custom-call(bf16[1024,6144]{1,0:T(8,128)(2,1)S(1)} %get-tuple-element.73.x_ref, bf16[832,512]{1,0:T(8,128)(2,1)S(1)} %collective-permute-done.12.refs_0_, bf16[768,512]{1,0:T(8,128)(2,1)S(1)} %collective-permute-done.13.refs_1_, ...), custom_call_target="tpu_custom_call" | custom-call | flops 1610612736 | bytes 10000000 | tf_op jit(solution)/shard_map/project/pallas_call | solution.py:267
  56.7 1.8 %project.9 = (f32[1024,512]{1,0:T(8,128)S(1)}, bf16[1,64,128]{2,1,0:T(8,128)(2,1)S(1)}) custom-call(bf16[1024,6144]{1,0:T(8,128)(2,1)S(1)} %get-tuple-element.73.x_ref, bf16[832,512]{1,0:T(8,128)(2,1)S(1)} %collective-permute-done.14.refs_0_, bf16[768,512]{1,0:T(8,128)(2,1)S(1)} %collective-permute-done.15.refs_1_, f32[1024,512]{1,0:T(8,128)S(1)} %get-tuple-element.103.refs_2_), custom_call_target="tpu_custom_call" | custom-call | flops 1610612736 | bytes 10000000 | tf_op jit(solution)/shard_map/project/pallas_call | solution.py:267
  58.6 3.5 %post.1 = (bf16[1024,1024]{1,0:T(8,128)(2,1)S(1)}, f32[512,128]{1,0:T(8,128)S(1)}, f32[512,128]{1,0:T(8,128)S(1)}, bf16[1,64,128]{2,1,0:T(8,128)(2,1)S(1)}, bf16...) custom-call(f32[40,128]{1,0:T(8,128)S(1)} %get-tuple-element.97.dec, ...), custom_call_target="tpu_custom_call" | custom-call | tf_op jit(solution)/shard_map/post/pallas_call | solution.py:326
  62.4 1.3 %collective-permute-done.18.recv_ref = f32[512,128]{1,0:T(8,128)S(1)} collective-permute-done((f32[512,128]{1,0:T(8,128)S(1)}, f32[512,128]{1,0:T(8,128)S(1)}, u32[]{:S(2)}, u32[]{:S(2)}) %collective-permute-start.18) | collective-permute-done | bytes 262176 | tf_op jit(solution)/shard_map/ppermute | solution.py:26
  63.9 1.1 %collective-permute-start.19 = (bf16[512,128]{1,0:T(8,128)(2,1)S(1)}, bf16[512,128]{1,0:T(8,128)(2,1)S(1)}, u32[]{:S(2)}, u32[]{:S(2)}) collective-permute-start(bf16[512,128]{1,0:T(8,128)(2,1)S(1)} %get-tuple-element.112), channel_id=1, source_target_pairs={{0,8},{4,36},{8,16},{12,44},{16,24},{20,52},{24,0},{28,60},{32,40}... | collective-permute-start | bytes 393224 | tf_op jit(solution)/shard_map/ppermute | solution.py:42
  65.0 2.8 %collective-permute-start.20 = (bf16[512,128]{1,0:T(8,128)(2,1)S(1)}, bf16[512,128]{1,0:T(8,128)(2,1)S(1)}, u32[]{:S(2)}, u32[]{:S(2)}) collective-permute-start(bf16[512,128]{1,0:T(8,128)(2,1)S(1)} %get-tuple-element.112), channel_id=1, source_target_pairs={{0,16},{4,68},{8,24},{12,76},{16,0},{20,84},{24,8},{28,92},{32,48}... | collective-permute-start | bytes 393224 | tf_op jit(solution)/shard_map/ppermute | solution.py:42
  68.8 2.6 %within.1.comb_ref = f32[2,1024,1024]{2,1,0:T(8,128)S(1)} custom-call(f32[8,1024]{1,0:T(8,128)S(1)} %copy-done.3, bf16[1024,1024]{1,0:T(8,128)(2,1)S(1)} %get-tuple-element.113.v_ref, bf16[8,3,128,256]{3,2,1,0:T(8,128)(2,1)S(1)} %get-tuple-element.114.st_ref, bf16[1024,1024]{1,0:T(8,128)(2,1)S(1)} %get-tuple-element.115.q_ref, ...), custom_call_target="tpu_custom_call" | custom-call | flops 3000000000 | bytes 10000000 | tf_op jit(solution)/shard_map/within/pallas_call | solution.py:367
  73.2 1.1 %collective-permute-start.22 = (bf16[512,128]{1,0:T(8,128)(2,1)S(1)}, bf16[512,128]{1,0:T(8,128)(2,1)S(1)}, u32[]{:S(2)}, u32[]{:S(2)}) collective-permute-start(bf16[512,128]{1,0:T(8,128)(2,1)S(1)} %get-tuple-element.121), channel_id=1, source_target_pairs={{0,32},{4,12},{8,40},{12,20},{16,48},{20,28},{24,56},{28,4},{32,64... | collective-permute-start | bytes 393224 | tf_op jit(solution)/shard_map/ppermute | solution.py:42
  74.2 3.3 %collective-permute-start.23 = (bf16[512,128]{1,0:T(8,128)(2,1)S(1)}, bf16[512,128]{1,0:T(8,128)(2,1)S(1)}, u32[]{:S(2)}, u32[]{:S(2)}) collective-permute-start(bf16[512,128]{1,0:T(8,128)(2,1)S(1)} %get-tuple-element.122), channel_id=1, source_target_pairs={{0,64},{4,20},{8,72},{12,28},{16,80},{20,4},{24,88},{28,12},{32,96... | collective-permute-start | bytes 393224 | tf_op jit(solution)/shard_map/ppermute | solution.py:42
  78.1 1.3 %collective-permute-done.22.r1 = bf16[512,128]{1,0:T(8,128)(2,1)S(1)} collective-permute-done((bf16[512,128]{1,0:T(8,128)(2,1)S(1)}, bf16[512,128]{1,0:T(8,128)(2,1)S(1)}, u32[]{:S(2)}, u32[]{:S(2)}) %collective-permute-start.22) | collective-permute-done | bytes 131104 | tf_op jit(solution)/shard_map/ppermute | solution.py:42
  79.4 2.4 %collective-permute-done.23.r2 = bf16[512,128]{1,0:T(8,128)(2,1)S(1)} collective-permute-done((bf16[512,128]{1,0:T(8,128)(2,1)S(1)}, bf16[512,128]{1,0:T(8,128)(2,1)S(1)}, u32[]{:S(2)}, u32[]{:S(2)}) %collective-permute-start.23) | collective-permute-done | bytes 131104 | tf_op jit(solution)/shard_map/ppermute | solution.py:42
  82.9 2.2 %outer.2 = (f32[1024,512]{1,0:T(8,128)S(1)}, f32[8,128]{1,0:T(8,128)S(1)}) custom-call(f32[8,128]{1,0:T(8,128)S(1)} %get-tuple-element.68.sf, f32[8,1024]{1,0:T(8,128)S(1)} %copy-done.3, f32[512,128]{1,0:T(8,128)S(1)} %get-tuple-element.124.state_ref, f32[2,1024,1024]{2,1,0:T(8,128)S(1)} %within.1.comb_ref, bf16[1024,1024]{1,0:T(8,128)(2,1)S(1)} %copy-done), custom_call_target="tpu_custom_call" | custom-call | flops 600000000 | bytes 6000000 | tf_op jit(solution)/shard_map/outer/pallas_call | solution.py:509
  85.2 2.2 %outer.3 = (f32[1024,512]{1,0:T(8,128)S(1)}, f32[8,128]{1,0:T(8,128)S(1)}) custom-call(f32[8,128]{1,0:T(8,128)S(1)} %get-tuple-element.68.sf, f32[8,1024]{1,0:T(8,128)S(1)} %copy-done.3, f32[512,128]{1,0:T(8,128)S(1)} %collective-permute-done.25.state_ref, f32[2,1024,1024]{2,1,0:T(8,128)S(1)} %within.1.comb_ref, bf16[1024,1024]{1,0:T(8,128)(2,1)S(1)} %copy-done, ...), custom_call_target="tpu_custom_call" | custom-call | flops 600000000 | bytes 6000000 | tf_op jit(solution)/shard_map/outer/pallas_call | solution.py:509
  87.4 1.6 %collective-permute-start.26 = (f32[8,128]{1,0:T(8,128)S(1)}, f32[8,128]{1,0:T(8,128)S(1)}, u32[]{:S(2)}, u32[]{:S(2)}) collective-permute-start(f32[8,128]{1,0:T(8,128)S(1)} %get-tuple-element.130.s0), channel_id=1, source_target_pairs={{0,1},{1,2},{2,3},{3,0},{4,5},{5,6},{6,7},{7,4},{8,9},{9,10},{10,1... | collective-permute-start | bytes 12296 | tf_op jit(solution)/shard_map/ppermute | solution.py:30
  89.1 2.9 %collective-permute-start.27 = (f32[8,128]{1,0:T(8,128)S(1)}, f32[8,128]{1,0:T(8,128)S(1)}, u32[]{:S(2)}, u32[]{:S(2)}) collective-permute-start(f32[8,128]{1,0:T(8,128)S(1)} %get-tuple-element.130.s0), channel_id=1, source_target_pairs={{0,2},{1,3},{2,0},{3,1},{4,6},{5,7},{6,4},{7,5},{8,10},{9,11},{10,... | collective-permute-start | bytes 12296 | tf_op jit(solution)/shard_map/ppermute | solution.py:30
  92.0 1.3 %collective-permute-start.28 = (f32[8,128]{1,0:T(8,128)S(1)}, f32[8,128]{1,0:T(8,128)S(1)}, u32[]{:S(2)}, u32[]{:S(2)}) collective-permute-start(f32[8,128]{1,0:T(8,128)S(1)} %get-tuple-element.130.s0), channel_id=1, source_target_pairs={{0,3},{1,0},{2,1},{3,2},{4,7},{5,4},{6,5},{7,6},{8,11},{9,8},{10,9... | collective-permute-start | bytes 12296 | tf_op jit(solution)/shard_map/ppermute | solution.py:30
  94.2 1.4 %collective-permute-done.28.s3 = f32[8,128]{1,0:T(8,128)S(1)} collective-permute-done((f32[8,128]{1,0:T(8,128)S(1)}, f32[8,128]{1,0:T(8,128)S(1)}, u32[]{:S(2)}, u32[]{:S(2)}) %collective-permute-start.28) | collective-permute-done | bytes 4128 | tf_op jit(solution)/shard_map/ppermute | solution.py:30
  95.6 1.6 %norm.1 = bf16[1024,1024]{1,0:T(8,128)(2,1)} custom-call(f32[1024,512]{1,0:T(8,128)S(1)} %get-tuple-element.126.mine_ref, f32[1024,512]{1,0:T(8,128)S(1)} %get-tuple-element.129.other_ref, f32[8,128]{1,0:T(8,128)S(1)} %get-tuple-element.130.s0, f32[8,128]{1,0:T(8,128)S(1)} %collective-permute-done.26.s1, f32[8,128]{1,0:T(8,128)S(1)} %collective-permute-done.27.s2, ...), custom_call_target="tpu_custom_call" | custom-call | tf_op jit(solution)/shard_map/norm/pallas_call | solution.py:543
  (65 shorter events, 13.4 us)
Async XLA Ops:
  1.1 2.2 %collective-permute-start = (bf16[192,512]{1,0:T(8,128)(2,1)S(1)}, bf16[192,512]{1,0:T(8,128)(2,1)S(1)}, u32[]{:S(2)}, u32[]{:S(2)}) collective-permute-start(bf16[192,512]{1,0:T(8,128)(2,1)S(1)} %get-tuple-element.132), channel_id=1, source_target_pairs={{0,4},{4,0},{1,5},{5,1},{2,6},{6,2},{3,7},{7,3},{8,12},{12,8},{9,1... | collective-permute-start | bytes 589832 | tf_op jit(solution)/shard_map/ppermute | solution.py:26
  3.4 16.7 %collective-permute-start.1 = (bf16[400,512]{1,0:T(8,128)(2,1)S(1)}, bf16[400,512]{1,0:T(8,128)(2,1)S(1)}, u32[]{:S(2)}, u32[]{:S(2)}) collective-permute-start(bf16[400,512]{1,0:T(8,128)(2,1)S(1)} %fusion), channel_id=1, source_target_pairs={{0,8},{4,36},{8,16},{12,44},{16,24},{20,52},{24,0},{28,60},{32,40}... | collective-permute-start | bytes 1228808 | tf_op jit(solution)/shard_map/ppermute | solution.py:42
  5.5 14.6 %collective-permute-start.2 = (bf16[400,512]{1,0:T(8,128)(2,1)S(1)}, bf16[400,512]{1,0:T(8,128)(2,1)S(1)}, u32[]{:S(2)}, u32[]{:S(2)}) collective-permute-start(bf16[400,512]{1,0:T(8,128)(2,1)S(1)} %fusion), channel_id=1, source_target_pairs={{0,16},{4,68},{8,24},{12,76},{16,0},{20,84},{24,8},{28,92},{32,48}... | collective-permute-start | bytes 1228808 | tf_op jit(solution)/shard_map/ppermute | solution.py:42
  9.1 11.0 %collective-permute-start.3 = (bf16[400,512]{1,0:T(8,128)(2,1)S(1)}, bf16[400,512]{1,0:T(8,128)(2,1)S(1)}, u32[]{:S(2)}, u32[]{:S(2)}) collective-permute-start(bf16[400,512]{1,0:T(8,128)(2,1)S(1)} %fusion), channel_id=1, source_target_pairs={{0,24},{4,100},{8,0},{12,108},{16,8},{20,116},{24,16},{28,124},{32... | collective-permute-start | bytes 1228808 | tf_op jit(solution)/shard_map/ppermute | solution.py:42
  20.2 5.6 %collective-permute-start.5 = (bf16[768,512]{1,0:T(8,128)(2,1)S(1)}, bf16[768,512]{1,0:T(8,128)(2,1)S(1)}, u32[]{:S(2)}, u32[]{:S(2)}) collective-permute-start(bf16[768,512]{1,0:T(8,128)(2,1)S(1)} %pad_maximum_fusion.refs_1_), channel_id=1, source_target_pairs={{0,4},{4,0},{1,5},{5,1},{2,6},{6,2},{3,7},{7,3},{8,12},{12,8},{9,1... | collective-permute-start | bytes 2359304 | tf_op jit(solution)/shard_map/ppermute | solution.py:26
  20.5 5.8 %collective-permute-start.4 = (bf16[832,512]{1,0:T(8,128)(2,1)S(1)}, bf16[832,512]{1,0:T(8,128)(2,1)S(1)}, u32[]{:S(2)}, u32[]{:S(2)}) collective-permute-start(bf16[832,512]{1,0:T(8,128)(2,1)S(1)} %slice_dynamic-update-slice_fusion.2.refs_0_), channel_id=1, source_target_pairs={{0,4},{4,0},{1,5},{5,1},{2,6},{6,2},{3,7},{7,3},{8,12},{12,8},{9,1... | collective-permute-start | bytes 2555912 | tf_op jit(solution)/shard_map/ppermute | solution.py:26
  21.0 13.9 %collective-permute-start.6 = (bf16[832,512]{1,0:T(8,128)(2,1)S(1)}, bf16[832,512]{1,0:T(8,128)(2,1)S(1)}, u32[]{:S(2)}, u32[]{:S(2)}) collective-permute-start(bf16[832,512]{1,0:T(8,128)(2,1)S(1)} %slice_dynamic-update-slice_fusion.2.refs_0_), channel_id=1, source_target_pairs={{0,32},{4,12},{8,40},{12,20},{16,48},{20,28},{24,56},{28,4},{32,64... | collective-permute-start | bytes 2555912 | tf_op jit(solution)/shard_map/ppermute | solution.py:42
  22.5 12.0 %collective-permute-start.7 = (bf16[768,512]{1,0:T(8,128)(2,1)S(1)}, bf16[768,512]{1,0:T(8,128)(2,1)S(1)}, u32[]{:S(2)}, u32[]{:S(2)}) collective-permute-start(bf16[768,512]{1,0:T(8,128)(2,1)S(1)} %pad_maximum_fusion.refs_1_), channel_id=1, source_target_pairs={{0,96},{4,28},{8,104},{12,4},{16,112},{20,12},{24,120},{28,20},{32... | collective-permute-start | bytes 2359304 | tf_op jit(solution)/shard_map/ppermute | solution.py:42
  24.3 19.4 %collective-permute-start.9 = (bf16[832,512]{1,0:T(8,128)(2,1)S(1)}, bf16[832,512]{1,0:T(8,128)(2,1)S(1)}, u32[]{:S(2)}, u32[]{:S(2)}) collective-permute-start(bf16[832,512]{1,0:T(8,128)(2,1)S(1)} %slice_dynamic-update-slice_fusion.2.refs_0_), channel_id=1, source_target_pairs={{0,96},{4,28},{8,104},{12,4},{16,112},{20,12},{24,120},{28,20},{32... | collective-permute-start | bytes 2555912 | tf_op jit(solution)/shard_map/ppermute | solution.py:42
  25.8 17.5 %collective-permute-start.8 = (bf16[768,512]{1,0:T(8,128)(2,1)S(1)}, bf16[768,512]{1,0:T(8,128)(2,1)S(1)}, u32[]{:S(2)}, u32[]{:S(2)}) collective-permute-start(bf16[768,512]{1,0:T(8,128)(2,1)S(1)} %pad_maximum_fusion.refs_1_), channel_id=1, source_target_pairs={{0,32},{4,12},{8,40},{12,20},{16,48},{20,28},{24,56},{28,4},{32,64... | collective-permute-start | bytes 2359304 | tf_op jit(solution)/shard_map/ppermute | solution.py:42
  34.9 17.1 %collective-permute-start.11 = (bf16[768,512]{1,0:T(8,128)(2,1)S(1)}, bf16[768,512]{1,0:T(8,128)(2,1)S(1)}, u32[]{:S(2)}, u32[]{:S(2)}) collective-permute-start(bf16[768,512]{1,0:T(8,128)(2,1)S(1)} %collective-permute-done.7.refs_3_), channel_id=1, source_target_pairs={{0,96},{4,28},{8,104},{12,4},{16,112},{20,12},{24,120},{28,20},{32... | collective-permute-start | bytes 2359304 | tf_op jit(solution)/shard_map/ppermute | solution.py:42
  37.5 15.0 %collective-permute-start.10 = (bf16[832,512]{1,0:T(8,128)(2,1)S(1)}, bf16[832,512]{1,0:T(8,128)(2,1)S(1)}, u32[]{:S(2)}, u32[]{:S(2)}) collective-permute-start(bf16[832,512]{1,0:T(8,128)(2,1)S(1)} %collective-permute-done.6.refs_0_), channel_id=1, source_target_pairs={{0,32},{4,12},{8,40},{12,20},{16,48},{20,28},{24,56},{28,4},{32,64... | collective-permute-start | bytes 2555912 | tf_op jit(solution)/shard_map/ppermute | solution.py:42
  43.6 8.9 %collective-permute-start.13 = (bf16[768,512]{1,0:T(8,128)(2,1)S(1)}, bf16[768,512]{1,0:T(8,128)(2,1)S(1)}, u32[]{:S(2)}, u32[]{:S(2)}) collective-permute-start(bf16[768,512]{1,0:T(8,128)(2,1)S(1)} %collective-permute-done.8.refs_1_), channel_id=1, source_target_pairs={{0,4},{4,0},{1,5},{5,1},{2,6},{6,2},{3,7},{7,3},{8,12},{12,8},{9,1... | collective-permute-start | bytes 2359304 | tf_op jit(solution)/shard_map/ppermute | solution.py:26
  43.6 11.2 %collective-permute-start.12 = (bf16[832,512]{1,0:T(8,128)(2,1)S(1)}, bf16[832,512]{1,0:T(8,128)(2,1)S(1)}, u32[]{:S(2)}, u32[]{:S(2)}) collective-permute-start(bf16[832,512]{1,0:T(8,128)(2,1)S(1)} %collective-permute-done.6.refs_0_), channel_id=1, source_target_pairs={{0,4},{4,0},{1,5},{5,1},{2,6},{6,2},{3,7},{7,3},{8,12},{12,8},{9,1... | collective-permute-start | bytes 2555912 | tf_op jit(solution)/shard_map/ppermute | solution.py:26
  47.6 9.1 %collective-permute-start.14 = (bf16[832,512]{1,0:T(8,128)(2,1)S(1)}, bf16[832,512]{1,0:T(8,128)(2,1)S(1)}, u32[]{:S(2)}, u32[]{:S(2)}) collective-permute-start(bf16[832,512]{1,0:T(8,128)(2,1)S(1)} %collective-permute-done.9.refs_2_), channel_id=1, source_target_pairs={{0,4},{4,0},{1,5},{5,1},{2,6},{6,2},{3,7},{7,3},{8,12},{12,8},{9,1... | collective-permute-start | bytes 2555912 | tf_op jit(solution)/shard_map/ppermute | solution.py:26
  52.1 4.6 %collective-permute-start.15 = (bf16[768,512]{1,0:T(8,128)(2,1)S(1)}, bf16[768,512]{1,0:T(8,128)(2,1)S(1)}, u32[]{:S(2)}, u32[]{:S(2)}) collective-permute-start(bf16[768,512]{1,0:T(8,128)(2,1)S(1)} %collective-permute-done.7.refs_3_), channel_id=1, source_target_pairs={{0,4},{4,0},{1,5},{5,1},{2,6},{6,2},{3,7},{7,3},{8,12},{12,8},{9,1... | collective-permute-start | bytes 2359304 | tf_op jit(solution)/shard_map/ppermute | solution.py:26
  52.5 6.1 %collective-permute-start.16 = (bf16[832,512]{1,0:T(8,128)(2,1)S(1)}, bf16[832,512]{1,0:T(8,128)(2,1)S(1)}, u32[]{:S(2)}, u32[]{:S(2)}) collective-permute-start(bf16[832,512]{1,0:T(8,128)(2,1)S(1)} %collective-permute-done.10.refs_0_), channel_id=1, source_target_pairs={{0,4},{4,0},{1,5},{5,1},{2,6},{6,2},{3,7},{7,3},{8,12},{12,8},{9,1... | collective-permute-start | bytes 2555912 | tf_op jit(solution)/shard_map/ppermute | solution.py:26
  52.6 6.0 %collective-permute-start.17 = (bf16[768,512]{1,0:T(8,128)(2,1)S(1)}, bf16[768,512]{1,0:T(8,128)(2,1)S(1)}, u32[]{:S(2)}, u32[]{:S(2)}) collective-permute-start(bf16[768,512]{1,0:T(8,128)(2,1)S(1)} %collective-permute-done.11.refs_1_), channel_id=1, source_target_pairs={{0,4},{4,0},{1,5},{5,1},{2,6},{6,2},{3,7},{7,3},{8,12},{12,8},{9,1... | collective-permute-start | bytes 2359304 | tf_op jit(solution)/shard_map/ppermute | solution.py:26
  58.6 10.3 %copy-start.3 = (f32[8,1024]{1,0:T(8,128)S(1)}, f32[8,1024]{1,0:T(8,128)}, u32[]{:S(2)}) copy-start(f32[8,1024]{1,0:T(8,128)} %ld_ref.5) | copy-start | bytes 98308
  62.1 1.6 %collective-permute-start.18 = (f32[512,128]{1,0:T(8,128)S(1)}, f32[512,128]{1,0:T(8,128)S(1)}, u32[]{:S(2)}, u32[]{:S(2)}) collective-permute-start(f32[512,128]{1,0:T(8,128)S(1)} %get-tuple-element.109), channel_id=1, source_target_pairs={{0,4},{4,0},{1,5},{5,1},{2,6},{6,2},{3,7},{7,3},{8,12},{12,8},{9,1... | collective-permute-start | bytes 786440 | tf_op jit(solution)/shard_map/ppermute | solution.py:26
  63.9 7.6 %collective-permute-start.19 = (bf16[512,128]{1,0:T(8,128)(2,1)S(1)}, bf16[512,128]{1,0:T(8,128)(2,1)S(1)}, u32[]{:S(2)}, u32[]{:S(2)}) collective-permute-start(bf16[512,128]{1,0:T(8,128)(2,1)S(1)} %get-tuple-element.112), channel_id=1, source_target_pairs={{0,8},{4,36},{8,16},{12,44},{16,24},{20,52},{24,0},{28,60},{32,40}... | collective-permute-start | bytes 393224 | tf_op jit(solution)/shard_map/ppermute | solution.py:42
  65.0 7.2 %collective-permute-start.20 = (bf16[512,128]{1,0:T(8,128)(2,1)S(1)}, bf16[512,128]{1,0:T(8,128)(2,1)S(1)}, u32[]{:S(2)}, u32[]{:S(2)}) collective-permute-start(bf16[512,128]{1,0:T(8,128)(2,1)S(1)} %get-tuple-element.112), channel_id=1, source_target_pairs={{0,16},{4,68},{8,24},{12,76},{16,0},{20,84},{24,8},{28,92},{32,48}... | collective-permute-start | bytes 393224 | tf_op jit(solution)/shard_map/ppermute | solution.py:42
  67.8 5.0 %collective-permute-start.21 = (bf16[512,128]{1,0:T(8,128)(2,1)S(1)}, bf16[512,128]{1,0:T(8,128)(2,1)S(1)}, u32[]{:S(2)}, u32[]{:S(2)}) collective-permute-start(bf16[512,128]{1,0:T(8,128)(2,1)S(1)} %get-tuple-element.112), channel_id=1, source_target_pairs={{0,24},{4,100},{8,0},{12,108},{16,8},{20,116},{24,16},{28,124},{32... | collective-permute-start | bytes 393224 | tf_op jit(solution)/shard_map/ppermute | solution.py:42
  68.8 14.1 %copy-start = (bf16[1024,1024]{1,0:T(8,128)(2,1)S(1)}, bf16[1024,1024]{1,0:T(8,128)(2,1)}, u32[]{:S(2)}) copy-start(bf16[1024,1024]{1,0:T(8,128)(2,1)} %q_ref.1) | copy-start | bytes 6291460
  73.2 6.2 %collective-permute-start.22 = (bf16[512,128]{1,0:T(8,128)(2,1)S(1)}, bf16[512,128]{1,0:T(8,128)(2,1)S(1)}, u32[]{:S(2)}, u32[]{:S(2)}) collective-permute-start(bf16[512,128]{1,0:T(8,128)(2,1)S(1)} %get-tuple-element.121), channel_id=1, source_target_pairs={{0,32},{4,12},{8,40},{12,20},{16,48},{20,28},{24,56},{28,4},{32,64... | collective-permute-start | bytes 393224 | tf_op jit(solution)/shard_map/ppermute | solution.py:42
  74.2 7.6 %collective-permute-start.23 = (bf16[512,128]{1,0:T(8,128)(2,1)S(1)}, bf16[512,128]{1,0:T(8,128)(2,1)S(1)}, u32[]{:S(2)}, u32[]{:S(2)}) collective-permute-start(bf16[512,128]{1,0:T(8,128)(2,1)S(1)} %get-tuple-element.122), channel_id=1, source_target_pairs={{0,64},{4,20},{8,72},{12,28},{16,80},{20,4},{24,88},{28,12},{32,96... | collective-permute-start | bytes 393224 | tf_op jit(solution)/shard_map/ppermute | solution.py:42
  77.5 5.0 %collective-permute-start.24 = (bf16[512,128]{1,0:T(8,128)(2,1)S(1)}, bf16[512,128]{1,0:T(8,128)(2,1)S(1)}, u32[]{:S(2)}, u32[]{:S(2)}) collective-permute-start(bf16[512,128]{1,0:T(8,128)(2,1)S(1)} %get-tuple-element.123), channel_id=1, source_target_pairs={{0,96},{4,28},{8,104},{12,4},{16,112},{20,12},{24,120},{28,20},{32... | collective-permute-start | bytes 393224 | tf_op jit(solution)/shard_map/ppermute | solution.py:42
  82.6 2.5 %collective-permute-start.25 = (f32[512,128]{1,0:T(8,128)S(1)}, f32[512,128]{1,0:T(8,128)S(1)}, u32[]{:S(2)}, u32[]{:S(2)}) collective-permute-start(f32[512,128]{1,0:T(8,128)S(1)} %get-tuple-element.127), channel_id=1, source_target_pairs={{0,4},{4,0},{1,5},{5,1},{2,6},{6,2},{3,7},{7,3},{8,12},{12,8},{9,1... | collective-permute-start | bytes 786440 | tf_op jit(solution)/shard_map/ppermute | solution.py:26
  85.2 10.4 %copy-start.4 = (f32[1024]{0:T(1024)S(1)}, f32[1024]{0:T(1024)}, u32[]{:S(2)}) copy-start(f32[1024]{0:T(1024)} %param.13) | copy-start | bytes 12292
  87.4 5.9 %collective-permute-start.26 = (f32[8,128]{1,0:T(8,128)S(1)}, f32[8,128]{1,0:T(8,128)S(1)}, u32[]{:S(2)}, u32[]{:S(2)}) collective-permute-start(f32[8,128]{1,0:T(8,128)S(1)} %get-tuple-element.130.s0), channel_id=1, source_target_pairs={{0,1},{1,2},{2,3},{3,0},{4,5},{5,6},{6,7},{7,4},{8,9},{9,10},{10,1... | collective-permute-start | bytes 12296 | tf_op jit(solution)/shard_map/ppermute | solution.py:30
  89.1 5.1 %collective-permute-start.27 = (f32[8,128]{1,0:T(8,128)S(1)}, f32[8,128]{1,0:T(8,128)S(1)}, u32[]{:S(2)}, u32[]{:S(2)}) collective-permute-start(f32[8,128]{1,0:T(8,128)S(1)} %get-tuple-element.130.s0), channel_id=1, source_target_pairs={{0,2},{1,3},{2,0},{3,1},{4,6},{5,7},{6,4},{7,5},{8,10},{9,11},{10,... | collective-permute-start | bytes 12296 | tf_op jit(solution)/shard_map/ppermute | solution.py:30
  92.0 3.6 %collective-permute-start.28 = (f32[8,128]{1,0:T(8,128)S(1)}, f32[8,128]{1,0:T(8,128)S(1)}, u32[]{:S(2)}, u32[]{:S(2)}) collective-permute-start(f32[8,128]{1,0:T(8,128)S(1)} %get-tuple-element.130.s0), channel_id=1, source_target_pairs={{0,3},{1,0},{2,1},{3,2},{4,7},{5,4},{6,5},{7,6},{8,11},{9,8},{10,9... | collective-permute-start | bytes 12296 | tf_op jit(solution)/shard_map/ppermute | solution.py:30
  (3 other events, 2.2 us)

commit v6 on v5

--- a/solution.py
+++ b/solution.py
@@ -67,7 +67,15 @@
     return pltpu.CompilerParams(vmem_limit_bytes=mib * MIB)
 
 
-def prep_kernel(doc, ld_ref, fx_ref, dec_ref, sf_ref):
+def prep_kernel(doc_hbm, ld_hbm, fx_ref, dec_ref, sf_ref, doc, ld_ref, sems):
+    loads = [
+        pltpu.make_async_copy(doc_hbm, doc, sems.at[0]),
+        pltpu.make_async_copy(ld_hbm, ld_ref, sems.at[1]),
+    ]
+    for c in loads:
+        c.start()
+    for c in loads:
+        c.wait()
     lane = lax.broadcasted_iota(jnp.int32, (E, E), 1)
     mat = jnp.zeros((E, E), f32)
     place = lax.broadcasted_iota(jnp.int32, (8, E), 1)
@@ -102,21 +110,29 @@
 def prep(doc, ld):
     return pl.pallas_call(
         prep_kernel,
-        in_specs=[pl.BlockSpec(memory_space=pltpu.SMEM), VM],
+        in_specs=[HB, HB],
         out_specs=[VM] * 3,
         out_shape=[
             pltpu.VMEM((16, HALF), bf16),
             jax.ShapeDtypeStruct((40, E), f32),
             jax.ShapeDtypeStruct((8, E), f32),
         ],
+        scratch_shapes=[
+            pltpu.SMEM(doc.shape, jnp.int32),
+            pltpu.VMEM(ld.shape, f32),
+            pltpu.SemaphoreType.DMA((2,)),
+        ],
         compiler_params=params(4),
         name="prep",
-    )(doc, ld)
+    )(hbm(doc), hbm(ld))
 
 
 def pre_kernel(
-    ld_ref, q_hbm, k_hbm, x_hbm, w_hbm, kd_hbm, x_ref, q_ref, k_ref, w_ref, kd_ref, sems, xsems
+    ld_hbm, q_hbm, k_hbm, x_hbm, w_hbm, kd_hbm, x_ref, q_ref, k_ref, w_ref, kd_ref, ld_ref, *sems
 ):
+    sems, xsems = sems
+    decays = pltpu.make_async_copy(ld_hbm, ld_ref, xsems.at[8])
+    decays.start()
     half = SPAN // 2
     low = lax.broadcasted_iota(jnp.int32, (half, half), 0) >= lax.broadcasted_iota(
         jnp.int32, (half, half), 1
@@ -146,6 +162,7 @@
         )
         inputs[r].start()
     w_ref[:, :, :half, half:] = jnp.zeros((8, 4, half, half), bf16)
+    decays.wait()
     cums = [block_cum(ld_ref[:, b * SPAN : (b + 1) * SPAN]) for b in range(4)]
 
     def one_head(h, carry):
@@ -186,16 +203,17 @@
     shapes = ((8, 4, SPAN, SPAN), (8, 4, E, SPAN))
     return pl.pallas_call(
         pre_kernel,
-        in_specs=[VM, HB, HB, HB],
+        in_specs=[HB] * 4,
         out_specs=[HB, HB, VM],
         out_shape=[pltpu.HBM(s, bf16) for s in shapes] + [pltpu.VMEM(x.shape, bf16)],
         scratch_shapes=[pltpu.VMEM((1024, 1024), bf16)] * 2
         + [pltpu.VMEM(s, bf16) for s in shapes]
-        + [pltpu.SemaphoreType.DMA((4, 8)), pltpu.SemaphoreType.DMA((8,))],
+        + [pltpu.VMEM(ld.shape, f32)]
+        + [pltpu.SemaphoreType.DMA((4, 8)), pltpu.SemaphoreType.DMA((9,))],
         compiler_params=params(14),
         cost_estimate=pl.CostEstimate(flops=10**9, transcendentals=2 * 10**6, bytes_accessed=10**7),
         name="pre",
-    )(ld, hbm(q), hbm(k), hbm(x))
+    )(hbm(ld), hbm(q), hbm(k), hbm(x))
 
 
 def multiply(mine, d, x_ref, lo, hi, src, dst):

time: 97.6 us -> 95.8 us (0.982)
  local copies, waits for them, and re-layouts: 3.35 us -> 1.19 us
    unnamed x17 -> x11, local copies, waits for them, and re-layouts: 2.25 us -> 0.08 us
  transfers between devices with their start and end apart: 29 -> 29, of which waited for: 14 -> 16; matrix products, arithmetic and copies ran while one was open for 0% -> 0% of each run, Pallas kernels for 28% -> 29%
where the time goes in v6:
time: 95.8 us; the launch traced here: 95.7 us
  Pallas kernels  35.5 us (37%)
  starting transfers between devices  33.1 us (35%)
  waiting for transfers between devices  25.2 us (26%)
  local copies, waits for them, and re-layouts  1.19 us (1%)
    ppermute x15, starting transfers between devices, crossed(): return lax.ppermute(a, SEQ, pairs)  24.9 us
    ppermute x15, waiting for transfers between devices, crossed(): return lax.ppermute(a, SEQ, pairs)  21.1 us
    pallas_call x5, Pallas kernels, mm(): pl.pallas_call(functools.partial(mm_kernel, jobs, plane, here), in_specs=...  12.4 us
    pallas_call x1, Pallas kernels, pre(): pl.pallas_call(pre_kernel, in_specs=[HB] * 4, out_specs=[HB, HB, VM], out...  9.04 us
    ppermute x3, starting transfers between devices, ring(): return lax.ppermute(a, axis, [(i, (i + step) % 4) for i in range(4)])  5.89 us
    pallas_call x2, Pallas kernels, outer(): pl.pallas_call(functools.partial(outer_kernel, side), in_specs=[VM] * (5...  4.45 us
    pallas_call x1, Pallas kernels, post(): pl.pallas_call(functools.partial(post_kernel, job), in_specs=[VM, HB, HB,...  3.52 us
    pallas_call x1, Pallas kernels, within(): pl.pallas_call(within_kernel, in_specs=[VM] * 5, out_specs=VM, out_shape=...  2.65 us
  transfers between devices with their start and end apart: 29, of which 16 were waited for; matrix products, arithmetic and copies ran while one was open for 0% of the time, Pallas kernels for 29%

profile of v6, /device:TPU:0, one launch (start us, length us, event | category | flops | bytes accessed | tf_op | source)
XLA Modules:
  0.0 95.7 jit_solution(13239556401394312223)
XLA Ops:
  0.0 1.0 %constant_dynamic-slice_fusion.1 = (bf16[192,512]{1,0:T(8,128)(2,1)S(1)}, bf16[192,512]{1,0:T(8,128)(2,1)S(1)}) fusion(bf16[192,1024]{1,0:T(8,128)(2,1)} %param.10, s32[]{:T(128)S(6)} %select_n.15, s32[]{:T(128)S(6)} %select_n.16), kind=kLoop, calls=%fused_computation.11 | loop fusion | bytes 786440 | tf_op jit(solution)/shard_map/dynamic_slice | solution.py:577
  2.7 2.1 %collective-permute-start.1 = (bf16[400,512]{1,0:T(8,128)(2,1)S(1)}, bf16[400,512]{1,0:T(8,128)(2,1)S(1)}, u32[]{:S(2)}, u32[]{:S(2)}) collective-permute-start(bf16[400,512]{1,0:T(8,128)(2,1)S(1)} %fusion), channel_id=1, source_target_pairs={{0,8},{4,36},{8,16},{12,44},{16,24},{20,52},{24,0},{28,60},{32,40}... | collective-permute-start | bytes 1228808 | tf_op jit(solution)/shard_map/ppermute | solution.py:42
  4.8 3.6 %collective-permute-start.2 = (bf16[400,512]{1,0:T(8,128)(2,1)S(1)}, bf16[400,512]{1,0:T(8,128)(2,1)S(1)}, u32[]{:S(2)}, u32[]{:S(2)}) collective-permute-start(bf16[400,512]{1,0:T(8,128)(2,1)S(1)} %fusion), channel_id=1, source_target_pairs={{0,16},{4,68},{8,24},{12,76},{16,0},{20,84},{24,8},{28,92},{32,48}... | collective-permute-start | bytes 1228808 | tf_op jit(solution)/shard_map/ppermute | solution.py:42
  9.4 9.0 %pre.1 = (bf16[8,4,256,256]{3,2,1,0:T(8,128)(2,1)}, bf16[8,4,128,256]{3,2,1,0:T(8,128)(2,1)}, bf16[1024,6144]{1,0:T(8,128)(2,1)S(1)}) custom-call(f32[8,1024]{1,0:T(8,128)} %ld_ref.2, bf16[1024,1024]{1,0:T(8,128)(2,1)} %q_ref.1, bf16[1024,1024]{1,0:T(8,128)(2,1)} %k_hbm, bf16[1024,6144]{1,0:T(8,128)(2,1)} %x_hbm.1), custom_call_target="tpu_custom_call" | custom-call | flops 1000000000 | bytes 10000000 | tf_op jit(solution)/shard_map/pre/pallas_call | solution.py:204
  19.6 1.5 %collective-permute-start.6 = (bf16[832,512]{1,0:T(8,128)(2,1)S(1)}, bf16[832,512]{1,0:T(8,128)(2,1)S(1)}, u32[]{:S(2)}, u32[]{:S(2)}) collective-permute-start(bf16[832,512]{1,0:T(8,128)(2,1)S(1)} %slice_dynamic-update-slice_fusion.2.refs_0_), channel_id=1, source_target_pairs={{0,32},{4,12},{8,40},{12,20},{16,48},{20,28},{24,56},{28,4},{32,64... | collective-permute-start | bytes 2555912 | tf_op jit(solution)/shard_map/ppermute | solution.py:42
  21.1 1.7 %collective-permute-start.7 = (bf16[768,512]{1,0:T(8,128)(2,1)S(1)}, bf16[768,512]{1,0:T(8,128)(2,1)S(1)}, u32[]{:S(2)}, u32[]{:S(2)}) collective-permute-start(bf16[768,512]{1,0:T(8,128)(2,1)S(1)} %pad_maximum_fusion.refs_1_), channel_id=1, source_target_pairs={{0,96},{4,28},{8,104},{12,4},{16,112},{20,12},{24,120},{28,20},{32... | collective-permute-start | bytes 2359304 | tf_op jit(solution)/shard_map/ppermute | solution.py:42
  22.8 1.5 %collective-permute-start.9 = (bf16[832,512]{1,0:T(8,128)(2,1)S(1)}, bf16[832,512]{1,0:T(8,128)(2,1)S(1)}, u32[]{:S(2)}, u32[]{:S(2)}) collective-permute-start(bf16[832,512]{1,0:T(8,128)(2,1)S(1)} %slice_dynamic-update-slice_fusion.2.refs_0_), channel_id=1, source_target_pairs={{0,96},{4,28},{8,104},{12,4},{16,112},{20,12},{24,120},{28,20},{32... | collective-permute-start | bytes 2555912 | tf_op jit(solution)/shard_map/ppermute | solution.py:42
  24.9 3.5 %project.5 = (f32[4,1024,512]{2,1,0:T(8,128)S(1)}, bf16[2,64,128]{2,1,0:T(8,128)(2,1)S(1)}) custom-call(bf16[1024,6144]{1,0:T(8,128)(2,1)S(1)} %get-tuple-element.73.x_ref, bf16[832,512]{1,0:T(8,128)(2,1)S(1)} %slice_dynamic-update-slice_fusion.2.refs_0_, bf16[768,512]{1,0:T(8,128)(2,1)S(1)} %pad_maximum_fusion.refs_1_, ...), custom_call_target="tpu_custom_call" | custom-call | flops 3221225472 | bytes 20000000 | tf_op jit(solution)/shard_map/project/pallas_call | solution.py:285
  28.3 4.7 %collective-permute-done.7.refs_3_ = bf16[768,512]{1,0:T(8,128)(2,1)S(1)} collective-permute-done((bf16[768,512]{1,0:T(8,128)(2,1)S(1)}, bf16[768,512]{1,0:T(8,128)(2,1)S(1)}, u32[]{:S(2)}, u32[]{:S(2)}) %collective-permute-start.7) | collective-permute-done | bytes 786464 | tf_op jit(solution)/shard_map/ppermute | solution.py:42
  33.5 2.5 %collective-permute-start.11 = (bf16[768,512]{1,0:T(8,128)(2,1)S(1)}, bf16[768,512]{1,0:T(8,128)(2,1)S(1)}, u32[]{:S(2)}, u32[]{:S(2)}) collective-permute-start(bf16[768,512]{1,0:T(8,128)(2,1)S(1)} %collective-permute-done.7.refs_3_), channel_id=1, source_target_pairs={{0,96},{4,28},{8,104},{12,4},{16,112},{20,12},{24,120},{28,20},{32... | collective-permute-start | bytes 2359304 | tf_op jit(solution)/shard_map/ppermute | solution.py:42
  36.0 5.9 %collective-permute-done.8.refs_1_ = bf16[768,512]{1,0:T(8,128)(2,1)S(1)} collective-permute-done((bf16[768,512]{1,0:T(8,128)(2,1)S(1)}, bf16[768,512]{1,0:T(8,128)(2,1)S(1)}, u32[]{:S(2)}, u32[]{:S(2)}) %collective-permute-start.8) | collective-permute-done | bytes 786464 | tf_op jit(solution)/shard_map/ppermute | solution.py:42
  42.7 3.5 %project.6 = (f32[1024,512]{1,0:T(8,128)S(1)}, bf16[2,64,128]{2,1,0:T(8,128)(2,1)S(1)}) custom-call(bf16[1024,6144]{1,0:T(8,128)(2,1)S(1)} %get-tuple-element.73.x_ref, bf16[832,512]{1,0:T(8,128)(2,1)S(1)} %collective-permute-done.6.refs_0_, bf16[768,512]{1,0:T(8,128)(2,1)S(1)} %collective-permute-done.8.refs_1_, ...), custom_call_target="tpu_custom_call" | custom-call | flops 3221225472 | bytes 20000000 | tf_op jit(solution)/shard_map/project/pallas_call | solution.py:285
  46.3 4.3 %collective-permute-done.11.refs_1_ = bf16[768,512]{1,0:T(8,128)(2,1)S(1)} collective-permute-done((bf16[768,512]{1,0:T(8,128)(2,1)S(1)}, bf16[768,512]{1,0:T(8,128)(2,1)S(1)}, u32[]{:S(2)}, u32[]{:S(2)}) %collective-permute-start.11) | collective-permute-done | bytes 786464 | tf_op jit(solution)/shard_map/ppermute | solution.py:42
  51.6 1.8 %project.7 = (f32[1024,512]{1,0:T(8,128)S(1)}, bf16[1,64,128]{2,1,0:T(8,128)(2,1)S(1)}) custom-call(bf16[1024,6144]{1,0:T(8,128)(2,1)S(1)} %get-tuple-element.73.x_ref, bf16[832,512]{1,0:T(8,128)(2,1)S(1)} %collective-permute-done.10.refs_0_, bf16[768,512]{1,0:T(8,128)(2,1)S(1)} %collective-permute-done.11.refs_1_, f32[1024,512]{1,0:T(8,128)S(1)} %get-tuple-element.94.refs_2_), custom_call_target="tpu_custom_call" | custom-call | flops 1610612736 | bytes 10000000 | tf_op jit(solution)/shard_map/project/pallas_call | solution.py:285
  53.4 1.8 %project.8 = (f32[1024,512]{1,0:T(8,128)S(1)}, bf16[1,64,128]{2,1,0:T(8,128)(2,1)S(1)}) custom-call(bf16[1024,6144]{1,0:T(8,128)(2,1)S(1)} %get-tuple-element.73.x_ref, bf16[832,512]{1,0:T(8,128)(2,1)S(1)} %collective-permute-done.12.refs_0_, bf16[768,512]{1,0:T(8,128)(2,1)S(1)} %collective-permute-done.13.refs_1_, ...), custom_call_target="tpu_custom_call" | custom-call | flops 1610612736 | bytes 10000000 | tf_op jit(solution)/shard_map/project/pallas_call | solution.py:285
  55.3 1.8 %project.9 = (f32[1024,512]{1,0:T(8,128)S(1)}, bf16[1,64,128]{2,1,0:T(8,128)(2,1)S(1)}) custom-call(bf16[1024,6144]{1,0:T(8,128)(2,1)S(1)} %get-tuple-element.73.x_ref, bf16[832,512]{1,0:T(8,128)(2,1)S(1)} %collective-permute-done.14.refs_0_, bf16[768,512]{1,0:T(8,128)(2,1)S(1)} %collective-permute-done.15.refs_1_, f32[1024,512]{1,0:T(8,128)S(1)} %get-tuple-element.103.refs_2_), custom_call_target="tpu_custom_call" | custom-call | flops 1610612736 | bytes 10000000 | tf_op jit(solution)/shard_map/project/pallas_call | solution.py:285
  57.1 3.5 %post.1 = (bf16[1024,1024]{1,0:T(8,128)(2,1)S(1)}, f32[512,128]{1,0:T(8,128)S(1)}, f32[512,128]{1,0:T(8,128)S(1)}, bf16[1,64,128]{2,1,0:T(8,128)(2,1)S(1)}, bf16...) custom-call(f32[40,128]{1,0:T(8,128)S(1)} %get-tuple-element.97.dec, ...), custom_call_target="tpu_custom_call" | custom-call | tf_op jit(solution)/shard_map/post/pallas_call | solution.py:344
  61.0 1.3 %collective-permute-done.18.recv_ref = f32[512,128]{1,0:T(8,128)S(1)} collective-permute-done((f32[512,128]{1,0:T(8,128)S(1)}, f32[512,128]{1,0:T(8,128)S(1)}, u32[]{:S(2)}, u32[]{:S(2)}) %collective-permute-start.18) | collective-permute-done | bytes 262176 | tf_op jit(solution)/shard_map/ppermute | solution.py:26
  62.5 1.5 %collective-permute-start.19 = (bf16[512,128]{1,0:T(8,128)(2,1)S(1)}, bf16[512,128]{1,0:T(8,128)(2,1)S(1)}, u32[]{:S(2)}, u32[]{:S(2)}) collective-permute-start(bf16[512,128]{1,0:T(8,128)(2,1)S(1)} %get-tuple-element.112), channel_id=1, source_target_pairs={{0,8},{4,36},{8,16},{12,44},{16,24},{20,52},{24,0},{28,60},{32,40}... | collective-permute-start | bytes 393224 | tf_op jit(solution)/shard_map/ppermute | solution.py:42
  64.0 2.1 %collective-permute-start.20 = (bf16[512,128]{1,0:T(8,128)(2,1)S(1)}, bf16[512,128]{1,0:T(8,128)(2,1)S(1)}, u32[]{:S(2)}, u32[]{:S(2)}) collective-permute-start(bf16[512,128]{1,0:T(8,128)(2,1)S(1)} %get-tuple-element.112), channel_id=1, source_target_pairs={{0,16},{4,68},{8,24},{12,76},{16,0},{20,84},{24,8},{28,92},{32,48}... | collective-permute-start | bytes 393224 | tf_op jit(solution)/shard_map/ppermute | solution.py:42
  66.1 1.6 %collective-permute-start.21 = (bf16[512,128]{1,0:T(8,128)(2,1)S(1)}, bf16[512,128]{1,0:T(8,128)(2,1)S(1)}, u32[]{:S(2)}, u32[]{:S(2)}) collective-permute-start(bf16[512,128]{1,0:T(8,128)(2,1)S(1)} %get-tuple-element.112), channel_id=1, source_target_pairs={{0,24},{4,100},{8,0},{12,108},{16,8},{20,116},{24,16},{28,124},{32... | collective-permute-start | bytes 393224 | tf_op jit(solution)/shard_map/ppermute | solution.py:42
  67.7 2.6 %within.1.comb_ref = f32[2,1024,1024]{2,1,0:T(8,128)S(1)} custom-call(f32[8,1024]{1,0:T(8,128)S(1)} %copy-done.1, bf16[1024,1024]{1,0:T(8,128)(2,1)S(1)} %get-tuple-element.113.v_ref, bf16[8,3,128,256]{3,2,1,0:T(8,128)(2,1)S(1)} %get-tuple-element.114.st_ref, bf16[1024,1024]{1,0:T(8,128)(2,1)S(1)} %get-tuple-element.115.q_ref, ...), custom_call_target="tpu_custom_call" | custom-call | flops 3000000000 | bytes 10000000 | tf_op jit(solution)/shard_map/within/pallas_call | solution.py:385
  71.5 1.4 %collective-permute-start.22 = (bf16[512,128]{1,0:T(8,128)(2,1)S(1)}, bf16[512,128]{1,0:T(8,128)(2,1)S(1)}, u32[]{:S(2)}, u32[]{:S(2)}) collective-permute-start(bf16[512,128]{1,0:T(8,128)(2,1)S(1)} %get-tuple-element.121), channel_id=1, source_target_pairs={{0,32},{4,12},{8,40},{12,20},{16,48},{20,28},{24,56},{28,4},{32,64... | collective-permute-start | bytes 393224 | tf_op jit(solution)/shard_map/ppermute | solution.py:42
  72.9 2.9 %collective-permute-start.23 = (bf16[512,128]{1,0:T(8,128)(2,1)S(1)}, bf16[512,128]{1,0:T(8,128)(2,1)S(1)}, u32[]{:S(2)}, u32[]{:S(2)}) collective-permute-start(bf16[512,128]{1,0:T(8,128)(2,1)S(1)} %get-tuple-element.122), channel_id=1, source_target_pairs={{0,64},{4,20},{8,72},{12,28},{16,80},{20,4},{24,88},{28,12},{32,96... | collective-permute-start | bytes 393224 | tf_op jit(solution)/shard_map/ppermute | solution.py:42
  77.7 2.4 %collective-permute-done.23.r2 = bf16[512,128]{1,0:T(8,128)(2,1)S(1)} collective-permute-done((bf16[512,128]{1,0:T(8,128)(2,1)S(1)}, bf16[512,128]{1,0:T(8,128)(2,1)S(1)}, u32[]{:S(2)}, u32[]{:S(2)}) %collective-permute-start.23) | collective-permute-done | bytes 131104 | tf_op jit(solution)/shard_map/ppermute | solution.py:42
  81.2 2.2 %outer.2 = (f32[1024,512]{1,0:T(8,128)S(1)}, f32[8,128]{1,0:T(8,128)S(1)}) custom-call(f32[8,128]{1,0:T(8,128)S(1)} %get-tuple-element.68.sf, f32[8,1024]{1,0:T(8,128)S(1)} %copy-done.1, f32[512,128]{1,0:T(8,128)S(1)} %get-tuple-element.124.state_ref, f32[2,1024,1024]{2,1,0:T(8,128)S(1)} %within.1.comb_ref, bf16[1024,1024]{1,0:T(8,128)(2,1)S(1)} %copy-done), custom_call_target="tpu_custom_call" | custom-call | flops 600000000 | bytes 6000000 | tf_op jit(solution)/shard_map/outer/pallas_call | solution.py:527
  83.5 2.2 %outer.3 = (f32[1024,512]{1,0:T(8,128)S(1)}, f32[8,128]{1,0:T(8,128)S(1)}) custom-call(f32[8,128]{1,0:T(8,128)S(1)} %get-tuple-element.68.sf, f32[8,1024]{1,0:T(8,128)S(1)} %copy-done.1, f32[512,128]{1,0:T(8,128)S(1)} %collective-permute-done.25.state_ref, f32[2,1024,1024]{2,1,0:T(8,128)S(1)} %within.1.comb_ref, bf16[1024,1024]{1,0:T(8,128)(2,1)S(1)} %copy-done, ...), custom_call_target="tpu_custom_call" | custom-call | flops 600000000 | bytes 6000000 | tf_op jit(solution)/shard_map/outer/pallas_call | solution.py:527
  85.7 1.6 %collective-permute-start.26 = (f32[8,128]{1,0:T(8,128)S(1)}, f32[8,128]{1,0:T(8,128)S(1)}, u32[]{:S(2)}, u32[]{:S(2)}) collective-permute-start(f32[8,128]{1,0:T(8,128)S(1)} %get-tuple-element.130.s0), channel_id=1, source_target_pairs={{0,1},{1,2},{2,3},{3,0},{4,5},{5,6},{6,7},{7,4},{8,9},{9,10},{10,1... | collective-permute-start | bytes 12296 | tf_op jit(solution)/shard_map/ppermute | solution.py:30
  87.4 2.9 %collective-permute-start.27 = (f32[8,128]{1,0:T(8,128)S(1)}, f32[8,128]{1,0:T(8,128)S(1)}, u32[]{:S(2)}, u32[]{:S(2)}) collective-permute-start(f32[8,128]{1,0:T(8,128)S(1)} %get-tuple-element.130.s0), channel_id=1, source_target_pairs={{0,2},{1,3},{2,0},{3,1},{4,6},{5,7},{6,4},{7,5},{8,10},{9,11},{10,... | collective-permute-start | bytes 12296 | tf_op jit(solution)/shard_map/ppermute | solution.py:30
  90.3 1.3 %collective-permute-start.28 = (f32[8,128]{1,0:T(8,128)S(1)}, f32[8,128]{1,0:T(8,128)S(1)}, u32[]{:S(2)}, u32[]{:S(2)}) collective-permute-start(f32[8,128]{1,0:T(8,128)S(1)} %get-tuple-element.130.s0), channel_id=1, source_target_pairs={{0,3},{1,0},{2,1},{3,2},{4,7},{5,4},{6,5},{7,6},{8,11},{9,8},{10,9... | collective-permute-start | bytes 12296 | tf_op jit(solution)/shard_map/ppermute | solution.py:30
  92.5 1.4 %collective-permute-done.28.s3 = f32[8,128]{1,0:T(8,128)S(1)} collective-permute-done((f32[8,128]{1,0:T(8,128)S(1)}, f32[8,128]{1,0:T(8,128)S(1)}, u32[]{:S(2)}, u32[]{:S(2)}) %collective-permute-start.28) | collective-permute-done | bytes 4128 | tf_op jit(solution)/shard_map/ppermute | solution.py:30
  93.9 1.6 %norm.1 = bf16[1024,1024]{1,0:T(8,128)(2,1)} custom-call(f32[1024,512]{1,0:T(8,128)S(1)} %get-tuple-element.126.mine_ref, f32[1024,512]{1,0:T(8,128)S(1)} %get-tuple-element.129.other_ref, f32[8,128]{1,0:T(8,128)S(1)} %get-tuple-element.130.s0, f32[8,128]{1,0:T(8,128)S(1)} %collective-permute-done.26.s1, f32[8,128]{1,0:T(8,128)S(1)} %collective-permute-done.27.s2, ...), custom_call_target="tpu_custom_call" | custom-call | tf_op jit(solution)/shard_map/norm/pallas_call | solution.py:561
  (59 shorter events, 11.9 us)
Async XLA Ops:
  1.1 1.5 %collective-permute-start = (bf16[192,512]{1,0:T(8,128)(2,1)S(1)}, bf16[192,512]{1,0:T(8,128)(2,1)S(1)}, u32[]{:S(2)}, u32[]{:S(2)}) collective-permute-start(bf16[192,512]{1,0:T(8,128)(2,1)S(1)} %get-tuple-element.132), channel_id=1, source_target_pairs={{0,4},{4,0},{1,5},{5,1},{2,6},{6,2},{3,7},{7,3},{8,12},{12,8},{9,1... | collective-permute-start | bytes 589832 | tf_op jit(solution)/shard_map/ppermute | solution.py:26
  2.7 15.7 %collective-permute-start.1 = (bf16[400,512]{1,0:T(8,128)(2,1)S(1)}, bf16[400,512]{1,0:T(8,128)(2,1)S(1)}, u32[]{:S(2)}, u32[]{:S(2)}) collective-permute-start(bf16[400,512]{1,0:T(8,128)(2,1)S(1)} %fusion), channel_id=1, source_target_pairs={{0,8},{4,36},{8,16},{12,44},{16,24},{20,52},{24,0},{28,60},{32,40}... | collective-permute-start | bytes 1228808 | tf_op jit(solution)/shard_map/ppermute | solution.py:42
  4.8 13.9 %collective-permute-start.2 = (bf16[400,512]{1,0:T(8,128)(2,1)S(1)}, bf16[400,512]{1,0:T(8,128)(2,1)S(1)}, u32[]{:S(2)}, u32[]{:S(2)}) collective-permute-start(bf16[400,512]{1,0:T(8,128)(2,1)S(1)} %fusion), channel_id=1, source_target_pairs={{0,16},{4,68},{8,24},{12,76},{16,0},{20,84},{24,8},{28,92},{32,48}... | collective-permute-start | bytes 1228808 | tf_op jit(solution)/shard_map/ppermute | solution.py:42
  8.4 10.3 %collective-permute-start.3 = (bf16[400,512]{1,0:T(8,128)(2,1)S(1)}, bf16[400,512]{1,0:T(8,128)(2,1)S(1)}, u32[]{:S(2)}, u32[]{:S(2)}) collective-permute-start(bf16[400,512]{1,0:T(8,128)(2,1)S(1)} %fusion), channel_id=1, source_target_pairs={{0,24},{4,100},{8,0},{12,108},{16,8},{20,116},{24,16},{28,124},{32... | collective-permute-start | bytes 1228808 | tf_op jit(solution)/shard_map/ppermute | solution.py:42
  18.8 5.6 %collective-permute-start.5 = (bf16[768,512]{1,0:T(8,128)(2,1)S(1)}, bf16[768,512]{1,0:T(8,128)(2,1)S(1)}, u32[]{:S(2)}, u32[]{:S(2)}) collective-permute-start(bf16[768,512]{1,0:T(8,128)(2,1)S(1)} %pad_maximum_fusion.refs_1_), channel_id=1, source_target_pairs={{0,4},{4,0},{1,5},{5,1},{2,6},{6,2},{3,7},{7,3},{8,12},{12,8},{9,1... | collective-permute-start | bytes 2359304 | tf_op jit(solution)/shard_map/ppermute | solution.py:26
  19.0 5.8 %collective-permute-start.4 = (bf16[832,512]{1,0:T(8,128)(2,1)S(1)}, bf16[832,512]{1,0:T(8,128)(2,1)S(1)}, u32[]{:S(2)}, u32[]{:S(2)}) collective-permute-start(bf16[832,512]{1,0:T(8,128)(2,1)S(1)} %slice_dynamic-update-slice_fusion.2.refs_0_), channel_id=1, source_target_pairs={{0,4},{4,0},{1,5},{5,1},{2,6},{6,2},{3,7},{7,3},{8,12},{12,8},{9,1... | collective-permute-start | bytes 2555912 | tf_op jit(solution)/shard_map/ppermute | solution.py:26
  19.6 13.9 %collective-permute-start.6 = (bf16[832,512]{1,0:T(8,128)(2,1)S(1)}, bf16[832,512]{1,0:T(8,128)(2,1)S(1)}, u32[]{:S(2)}, u32[]{:S(2)}) collective-permute-start(bf16[832,512]{1,0:T(8,128)(2,1)S(1)} %slice_dynamic-update-slice_fusion.2.refs_0_), channel_id=1, source_target_pairs={{0,32},{4,12},{8,40},{12,20},{16,48},{20,28},{24,56},{28,4},{32,64... | collective-permute-start | bytes 2555912 | tf_op jit(solution)/shard_map/ppermute | solution.py:42
  21.1 12.0 %collective-permute-start.7 = (bf16[768,512]{1,0:T(8,128)(2,1)S(1)}, bf16[768,512]{1,0:T(8,128)(2,1)S(1)}, u32[]{:S(2)}, u32[]{:S(2)}) collective-permute-start(bf16[768,512]{1,0:T(8,128)(2,1)S(1)} %pad_maximum_fusion.refs_1_), channel_id=1, source_target_pairs={{0,96},{4,28},{8,104},{12,4},{16,112},{20,12},{24,120},{28,20},{32... | collective-permute-start | bytes 2359304 | tf_op jit(solution)/shard_map/ppermute | solution.py:42
  22.8 19.4 %collective-permute-start.9 = (bf16[832,512]{1,0:T(8,128)(2,1)S(1)}, bf16[832,512]{1,0:T(8,128)(2,1)S(1)}, u32[]{:S(2)}, u32[]{:S(2)}) collective-permute-start(bf16[832,512]{1,0:T(8,128)(2,1)S(1)} %slice_dynamic-update-slice_fusion.2.refs_0_), channel_id=1, source_target_pairs={{0,96},{4,28},{8,104},{12,4},{16,112},{20,12},{24,120},{28,20},{32... | collective-permute-start | bytes 2555912 | tf_op jit(solution)/shard_map/ppermute | solution.py:42
  24.4 17.5 %collective-permute-start.8 = (bf16[768,512]{1,0:T(8,128)(2,1)S(1)}, bf16[768,512]{1,0:T(8,128)(2,1)S(1)}, u32[]{:S(2)}, u32[]{:S(2)}) collective-permute-start(bf16[768,512]{1,0:T(8,128)(2,1)S(1)} %pad_maximum_fusion.refs_1_), channel_id=1, source_target_pairs={{0,32},{4,12},{8,40},{12,20},{16,48},{20,28},{24,56},{28,4},{32,64... | collective-permute-start | bytes 2359304 | tf_op jit(solution)/shard_map/ppermute | solution.py:42
  33.5 17.1 %collective-permute-start.11 = (bf16[768,512]{1,0:T(8,128)(2,1)S(1)}, bf16[768,512]{1,0:T(8,128)(2,1)S(1)}, u32[]{:S(2)}, u32[]{:S(2)}) collective-permute-start(bf16[768,512]{1,0:T(8,128)(2,1)S(1)} %collective-permute-done.7.refs_3_), channel_id=1, source_target_pairs={{0,96},{4,28},{8,104},{12,4},{16,112},{20,12},{24,120},{28,20},{32... | collective-permute-start | bytes 2359304 | tf_op jit(solution)/shard_map/ppermute | solution.py:42
  36.0 15.0 %collective-permute-start.10 = (bf16[832,512]{1,0:T(8,128)(2,1)S(1)}, bf16[832,512]{1,0:T(8,128)(2,1)S(1)}, u32[]{:S(2)}, u32[]{:S(2)}) collective-permute-start(bf16[832,512]{1,0:T(8,128)(2,1)S(1)} %collective-permute-done.6.refs_0_), channel_id=1, source_target_pairs={{0,32},{4,12},{8,40},{12,20},{16,48},{20,28},{24,56},{28,4},{32,64... | collective-permute-start | bytes 2555912 | tf_op jit(solution)/shard_map/ppermute | solution.py:42
  42.2 8.9 %collective-permute-start.13 = (bf16[768,512]{1,0:T(8,128)(2,1)S(1)}, bf16[768,512]{1,0:T(8,128)(2,1)S(1)}, u32[]{:S(2)}, u32[]{:S(2)}) collective-permute-start(bf16[768,512]{1,0:T(8,128)(2,1)S(1)} %collective-permute-done.8.refs_1_), channel_id=1, source_target_pairs={{0,4},{4,0},{1,5},{5,1},{2,6},{6,2},{3,7},{7,3},{8,12},{12,8},{9,1... | collective-permute-start | bytes 2359304 | tf_op jit(solution)/shard_map/ppermute | solution.py:26
  42.2 11.2 %collective-permute-start.12 = (bf16[832,512]{1,0:T(8,128)(2,1)S(1)}, bf16[832,512]{1,0:T(8,128)(2,1)S(1)}, u32[]{:S(2)}, u32[]{:S(2)}) collective-permute-start(bf16[832,512]{1,0:T(8,128)(2,1)S(1)} %collective-permute-done.6.refs_0_), channel_id=1, source_target_pairs={{0,4},{4,0},{1,5},{5,1},{2,6},{6,2},{3,7},{7,3},{8,12},{12,8},{9,1... | collective-permute-start | bytes 2555912 | tf_op jit(solution)/shard_map/ppermute | solution.py:26
  46.2 9.1 %collective-permute-start.14 = (bf16[832,512]{1,0:T(8,128)(2,1)S(1)}, bf16[832,512]{1,0:T(8,128)(2,1)S(1)}, u32[]{:S(2)}, u32[]{:S(2)}) collective-permute-start(bf16[832,512]{1,0:T(8,128)(2,1)S(1)} %collective-permute-done.9.refs_2_), channel_id=1, source_target_pairs={{0,4},{4,0},{1,5},{5,1},{2,6},{6,2},{3,7},{7,3},{8,12},{12,8},{9,1... | collective-permute-start | bytes 2555912 | tf_op jit(solution)/shard_map/ppermute | solution.py:26
  50.6 4.6 %collective-permute-start.15 = (bf16[768,512]{1,0:T(8,128)(2,1)S(1)}, bf16[768,512]{1,0:T(8,128)(2,1)S(1)}, u32[]{:S(2)}, u32[]{:S(2)}) collective-permute-start(bf16[768,512]{1,0:T(8,128)(2,1)S(1)} %collective-permute-done.7.refs_3_), channel_id=1, source_target_pairs={{0,4},{4,0},{1,5},{5,1},{2,6},{6,2},{3,7},{7,3},{8,12},{12,8},{9,1... | collective-permute-start | bytes 2359304 | tf_op jit(solution)/shard_map/ppermute | solution.py:26
  51.0 6.1 %collective-permute-start.16 = (bf16[832,512]{1,0:T(8,128)(2,1)S(1)}, bf16[832,512]{1,0:T(8,128)(2,1)S(1)}, u32[]{:S(2)}, u32[]{:S(2)}) collective-permute-start(bf16[832,512]{1,0:T(8,128)(2,1)S(1)} %collective-permute-done.10.refs_0_), channel_id=1, source_target_pairs={{0,4},{4,0},{1,5},{5,1},{2,6},{6,2},{3,7},{7,3},{8,12},{12,8},{9,1... | collective-permute-start | bytes 2555912 | tf_op jit(solution)/shard_map/ppermute | solution.py:26
  51.1 6.0 %collective-permute-start.17 = (bf16[768,512]{1,0:T(8,128)(2,1)S(1)}, bf16[768,512]{1,0:T(8,128)(2,1)S(1)}, u32[]{:S(2)}, u32[]{:S(2)}) collective-permute-start(bf16[768,512]{1,0:T(8,128)(2,1)S(1)} %collective-permute-done.11.refs_1_), channel_id=1, source_target_pairs={{0,4},{4,0},{1,5},{5,1},{2,6},{6,2},{3,7},{7,3},{8,12},{12,8},{9,1... | collective-permute-start | bytes 2359304 | tf_op jit(solution)/shard_map/ppermute | solution.py:26
  57.1 10.5 %copy-start.1 = (f32[8,1024]{1,0:T(8,128)S(1)}, f32[8,1024]{1,0:T(8,128)}, u32[]{:S(2)}) copy-start(f32[8,1024]{1,0:T(8,128)} %ld_ref.2) | copy-start | bytes 98308
  60.7 1.6 %collective-permute-start.18 = (f32[512,128]{1,0:T(8,128)S(1)}, f32[512,128]{1,0:T(8,128)S(1)}, u32[]{:S(2)}, u32[]{:S(2)}) collective-permute-start(f32[512,128]{1,0:T(8,128)S(1)} %get-tuple-element.109), channel_id=1, source_target_pairs={{0,4},{4,0},{1,5},{5,1},{2,6},{6,2},{3,7},{7,3},{8,12},{12,8},{9,1... | collective-permute-start | bytes 786440 | tf_op jit(solution)/shard_map/ppermute | solution.py:26
  62.5 7.9 %collective-permute-start.19 = (bf16[512,128]{1,0:T(8,128)(2,1)S(1)}, bf16[512,128]{1,0:T(8,128)(2,1)S(1)}, u32[]{:S(2)}, u32[]{:S(2)}) collective-permute-start(bf16[512,128]{1,0:T(8,128)(2,1)S(1)} %get-tuple-element.112), channel_id=1, source_target_pairs={{0,8},{4,36},{8,16},{12,44},{16,24},{20,52},{24,0},{28,60},{32,40}... | collective-permute-start | bytes 393224 | tf_op jit(solution)/shard_map/ppermute | solution.py:42
  64.0 6.5 %collective-permute-start.20 = (bf16[512,128]{1,0:T(8,128)(2,1)S(1)}, bf16[512,128]{1,0:T(8,128)(2,1)S(1)}, u32[]{:S(2)}, u32[]{:S(2)}) collective-permute-start(bf16[512,128]{1,0:T(8,128)(2,1)S(1)} %get-tuple-element.112), channel_id=1, source_target_pairs={{0,16},{4,68},{8,24},{12,76},{16,0},{20,84},{24,8},{28,92},{32,48}... | collective-permute-start | bytes 393224 | tf_op jit(solution)/shard_map/ppermute | solution.py:42
  66.1 5.0 %collective-permute-start.21 = (bf16[512,128]{1,0:T(8,128)(2,1)S(1)}, bf16[512,128]{1,0:T(8,128)(2,1)S(1)}, u32[]{:S(2)}, u32[]{:S(2)}) collective-permute-start(bf16[512,128]{1,0:T(8,128)(2,1)S(1)} %get-tuple-element.112), channel_id=1, source_target_pairs={{0,24},{4,100},{8,0},{12,108},{16,8},{20,116},{24,16},{28,124},{32... | collective-permute-start | bytes 393224 | tf_op jit(solution)/shard_map/ppermute | solution.py:42
  67.7 13.6 %copy-start = (bf16[1024,1024]{1,0:T(8,128)(2,1)S(1)}, bf16[1024,1024]{1,0:T(8,128)(2,1)}, u32[]{:S(2)}) copy-start(bf16[1024,1024]{1,0:T(8,128)(2,1)} %q_ref.1) | copy-start | bytes 6291460
  71.5 6.2 %collective-permute-start.22 = (bf16[512,128]{1,0:T(8,128)(2,1)S(1)}, bf16[512,128]{1,0:T(8,128)(2,1)S(1)}, u32[]{:S(2)}, u32[]{:S(2)}) collective-permute-start(bf16[512,128]{1,0:T(8,128)(2,1)S(1)} %get-tuple-element.121), channel_id=1, source_target_pairs={{0,32},{4,12},{8,40},{12,20},{16,48},{20,28},{24,56},{28,4},{32,64... | collective-permute-start | bytes 393224 | tf_op jit(solution)/shard_map/ppermute | solution.py:42
  72.9 7.3 %collective-permute-start.23 = (bf16[512,128]{1,0:T(8,128)(2,1)S(1)}, bf16[512,128]{1,0:T(8,128)(2,1)S(1)}, u32[]{:S(2)}, u32[]{:S(2)}) collective-permute-start(bf16[512,128]{1,0:T(8,128)(2,1)S(1)} %get-tuple-element.122), channel_id=1, source_target_pairs={{0,64},{4,20},{8,72},{12,28},{16,80},{20,4},{24,88},{28,12},{32,96... | collective-permute-start | bytes 393224 | tf_op jit(solution)/shard_map/ppermute | solution.py:42
  75.8 5.0 %collective-permute-start.24 = (bf16[512,128]{1,0:T(8,128)(2,1)S(1)}, bf16[512,128]{1,0:T(8,128)(2,1)S(1)}, u32[]{:S(2)}, u32[]{:S(2)}) collective-permute-start(bf16[512,128]{1,0:T(8,128)(2,1)S(1)} %get-tuple-element.123), channel_id=1, source_target_pairs={{0,96},{4,28},{8,104},{12,4},{16,112},{20,12},{24,120},{28,20},{32... | collective-permute-start | bytes 393224 | tf_op jit(solution)/shard_map/ppermute | solution.py:42
  80.9 2.5 %collective-permute-start.25 = (f32[512,128]{1,0:T(8,128)S(1)}, f32[512,128]{1,0:T(8,128)S(1)}, u32[]{:S(2)}, u32[]{:S(2)}) collective-permute-start(f32[512,128]{1,0:T(8,128)S(1)} %get-tuple-element.127), channel_id=1, source_target_pairs={{0,4},{4,0},{1,5},{5,1},{2,6},{6,2},{3,7},{7,3},{8,12},{12,8},{9,1... | collective-permute-start | bytes 786440 | tf_op jit(solution)/shard_map/ppermute | solution.py:26
  83.5 10.4 %copy-start.2 = (f32[1024]{0:T(1024)S(1)}, f32[1024]{0:T(1024)}, u32[]{:S(2)}) copy-start(f32[1024]{0:T(1024)} %param.13) | copy-start | bytes 12292
  85.7 5.9 %collective-permute-start.26 = (f32[8,128]{1,0:T(8,128)S(1)}, f32[8,128]{1,0:T(8,128)S(1)}, u32[]{:S(2)}, u32[]{:S(2)}) collective-permute-start(f32[8,128]{1,0:T(8,128)S(1)} %get-tuple-element.130.s0), channel_id=1, source_target_pairs={{0,1},{1,2},{2,3},{3,0},{4,5},{5,6},{6,7},{7,4},{8,9},{9,10},{10,1... | collective-permute-start | bytes 12296 | tf_op jit(solution)/shard_map/ppermute | solution.py:30
  87.4 5.1 %collective-permute-start.27 = (f32[8,128]{1,0:T(8,128)S(1)}, f32[8,128]{1,0:T(8,128)S(1)}, u32[]{:S(2)}, u32[]{:S(2)}) collective-permute-start(f32[8,128]{1,0:T(8,128)S(1)} %get-tuple-element.130.s0), channel_id=1, source_target_pairs={{0,2},{1,3},{2,0},{3,1},{4,6},{5,7},{6,4},{7,5},{8,10},{9,11},{10,... | collective-permute-start | bytes 12296 | tf_op jit(solution)/shard_map/ppermute | solution.py:30
  90.3 3.6 %collective-permute-start.28 = (f32[8,128]{1,0:T(8,128)S(1)}, f32[8,128]{1,0:T(8,128)S(1)}, u32[]{:S(2)}, u32[]{:S(2)}) collective-permute-start(f32[8,128]{1,0:T(8,128)S(1)} %get-tuple-element.130.s0), channel_id=1, source_target_pairs={{0,3},{1,0},{2,1},{3,2},{4,7},{5,4},{6,5},{7,6},{8,11},{9,8},{10,9... | collective-permute-start | bytes 12296 | tf_op jit(solution)/shard_map/ppermute | solution.py:30

commit v7 on v6

--- a/solution.py
+++ b/solution.py
@@ -624,7 +624,7 @@
     sf, qv = vmem(sf), vmem(q)
     mine, sq = outer(0, sf, ld, state, comb, qv)
     other, sq = outer(1, sf, ld, vmem(swap(give)), comb, qv, sq)
-    sqs = [sq] + [vmem(ring(sq, "head", d)) for d in (1, 2, 3)]
+    sqs = [sq] + [vmem(ring(sq, "head", d)) for d in (2, 1, 3)]
     return norm(mine, other, sqs, gain.reshape(1, -1))
 
 

time: 95.8 us -> 95.9 us (level)
  transfers between devices with their start and end apart: 29 -> 29, of which waited for: 16 -> 15; matrix products, arithmetic and copies ran while one was open for 0% -> 0% of each run, Pallas kernels for 29% -> 29%
where the time goes in v7:
time: 95.9 us; the launch traced here: 95.6 us
  Pallas kernels  35.5 us (37%)
  starting transfers between devices  33.7 us (35%)
  waiting for transfers between devices  24.5 us (26%)
  local copies, waits for them, and re-layouts  1.19 us (1%)
    ppermute x15, starting transfers between devices, crossed(): return lax.ppermute(a, SEQ, pairs)  24.9 us
    ppermute x15, waiting for transfers between devices, crossed(): return lax.ppermute(a, SEQ, pairs)  21.1 us
    pallas_call x5, Pallas kernels, mm(): pl.pallas_call(functools.partial(mm_kernel, jobs, plane, here), in_specs=...  12.4 us
    pallas_call x1, Pallas kernels, pre(): pl.pallas_call(pre_kernel, in_specs=[HB] * 4, out_specs=[HB, HB, VM], out...  9.04 us
    ppermute x3, starting transfers between devices, ring(): return lax.ppermute(a, axis, [(i, (i + step) % 4) for i in range(4)])  6.51 us
    pallas_call x2, Pallas kernels, outer(): pl.pallas_call(functools.partial(outer_kernel, side), in_specs=[VM] * (5...  4.45 us
    pallas_call x1, Pallas kernels, post(): pl.pallas_call(functools.partial(post_kernel, job), in_specs=[VM, HB, HB,...  3.52 us
    pallas_call x1, Pallas kernels, within(): pl.pallas_call(within_kernel, in_specs=[VM] * 5, out_specs=VM, out_shape=...  2.65 us
  transfers between devices with their start and end apart: 29, of which 15 were waited for; matrix products, arithmetic and copies ran while one was open for 0% of the time, Pallas kernels for 29%

profile of v7, /device:TPU:0, one launch (start us, length us, event | category | flops | bytes accessed | tf_op | source)
XLA Modules:
  0.0 95.6 jit_solution(6716685151933123766)
XLA Ops:
  0.0 1.0 %constant_dynamic-slice_fusion.1 = (bf16[192,512]{1,0:T(8,128)(2,1)S(1)}, bf16[192,512]{1,0:T(8,128)(2,1)S(1)}) fusion(bf16[192,1024]{1,0:T(8,128)(2,1)} %param.10, s32[]{:T(128)S(6)} %select_n.15, s32[]{:T(128)S(6)} %select_n.16), kind=kLoop, calls=%fused_computation.11 | loop fusion | bytes 786440 | tf_op jit(solution)/shard_map/dynamic_slice | solution.py:577
  2.7 2.1 %collective-permute-start.1 = (bf16[400,512]{1,0:T(8,128)(2,1)S(1)}, bf16[400,512]{1,0:T(8,128)(2,1)S(1)}, u32[]{:S(2)}, u32[]{:S(2)}) collective-permute-start(bf16[400,512]{1,0:T(8,128)(2,1)S(1)} %fusion), channel_id=1, source_target_pairs={{0,8},{4,36},{8,16},{12,44},{16,24},{20,52},{24,0},{28,60},{32,40}... | collective-permute-start | bytes 1228808 | tf_op jit(solution)/shard_map/ppermute | solution.py:42
  4.8 3.6 %collective-permute-start.2 = (bf16[400,512]{1,0:T(8,128)(2,1)S(1)}, bf16[400,512]{1,0:T(8,128)(2,1)S(1)}, u32[]{:S(2)}, u32[]{:S(2)}) collective-permute-start(bf16[400,512]{1,0:T(8,128)(2,1)S(1)} %fusion), channel_id=1, source_target_pairs={{0,16},{4,68},{8,24},{12,76},{16,0},{20,84},{24,8},{28,92},{32,48}... | collective-permute-start | bytes 1228808 | tf_op jit(solution)/shard_map/ppermute | solution.py:42
  8.4 1.0 %collective-permute-start.3 = (bf16[400,512]{1,0:T(8,128)(2,1)S(1)}, bf16[400,512]{1,0:T(8,128)(2,1)S(1)}, u32[]{:S(2)}, u32[]{:S(2)}) collective-permute-start(bf16[400,512]{1,0:T(8,128)(2,1)S(1)} %fusion), channel_id=1, source_target_pairs={{0,24},{4,100},{8,0},{12,108},{16,8},{20,116},{24,16},{28,124},{32... | collective-permute-start | bytes 1228808 | tf_op jit(solution)/shard_map/ppermute | solution.py:42
  9.4 9.0 %pre.1 = (bf16[8,4,256,256]{3,2,1,0:T(8,128)(2,1)}, bf16[8,4,128,256]{3,2,1,0:T(8,128)(2,1)}, bf16[1024,6144]{1,0:T(8,128)(2,1)S(1)}) custom-call(f32[8,1024]{1,0:T(8,128)} %ld_ref.2, bf16[1024,1024]{1,0:T(8,128)(2,1)} %q_ref.1, bf16[1024,1024]{1,0:T(8,128)(2,1)} %k_hbm, bf16[1024,6144]{1,0:T(8,128)(2,1)} %x_hbm.1), custom_call_target="tpu_custom_call" | custom-call | flops 1000000000 | bytes 10000000 | tf_op jit(solution)/shard_map/pre/pallas_call | solution.py:204
  19.6 1.5 %collective-permute-start.6 = (bf16[832,512]{1,0:T(8,128)(2,1)S(1)}, bf16[832,512]{1,0:T(8,128)(2,1)S(1)}, u32[]{:S(2)}, u32[]{:S(2)}) collective-permute-start(bf16[832,512]{1,0:T(8,128)(2,1)S(1)} %slice_dynamic-update-slice_fusion.2.refs_0_), channel_id=1, source_target_pairs={{0,32},{4,12},{8,40},{12,20},{16,48},{20,28},{24,56},{28,4},{32,64... | collective-permute-start | bytes 2555912 | tf_op jit(solution)/shard_map/ppermute | solution.py:42
  21.1 1.7 %collective-permute-start.7 = (bf16[768,512]{1,0:T(8,128)(2,1)S(1)}, bf16[768,512]{1,0:T(8,128)(2,1)S(1)}, u32[]{:S(2)}, u32[]{:S(2)}) collective-permute-start(bf16[768,512]{1,0:T(8,128)(2,1)S(1)} %pad_maximum_fusion.refs_1_), channel_id=1, source_target_pairs={{0,96},{4,28},{8,104},{12,4},{16,112},{20,12},{24,120},{28,20},{32... | collective-permute-start | bytes 2359304 | tf_op jit(solution)/shard_map/ppermute | solution.py:42
  22.8 1.5 %collective-permute-start.9 = (bf16[832,512]{1,0:T(8,128)(2,1)S(1)}, bf16[832,512]{1,0:T(8,128)(2,1)S(1)}, u32[]{:S(2)}, u32[]{:S(2)}) collective-permute-start(bf16[832,512]{1,0:T(8,128)(2,1)S(1)} %slice_dynamic-update-slice_fusion.2.refs_0_), channel_id=1, source_target_pairs={{0,96},{4,28},{8,104},{12,4},{16,112},{20,12},{24,120},{28,20},{32... | collective-permute-start | bytes 2555912 | tf_op jit(solution)/shard_map/ppermute | solution.py:42
  24.9 3.5 %project.5 = (f32[4,1024,512]{2,1,0:T(8,128)S(1)}, bf16[2,64,128]{2,1,0:T(8,128)(2,1)S(1)}) custom-call(bf16[1024,6144]{1,0:T(8,128)(2,1)S(1)} %get-tuple-element.73.x_ref, bf16[832,512]{1,0:T(8,128)(2,1)S(1)} %slice_dynamic-update-slice_fusion.2.refs_0_, bf16[768,512]{1,0:T(8,128)(2,1)S(1)} %pad_maximum_fusion.refs_1_, ...), custom_call_target="tpu_custom_call" | custom-call | flops 3221225472 | bytes 20000000 | tf_op jit(solution)/shard_map/project/pallas_call | solution.py:285
  28.3 4.7 %collective-permute-done.7.refs_3_ = bf16[768,512]{1,0:T(8,128)(2,1)S(1)} collective-permute-done((bf16[768,512]{1,0:T(8,128)(2,1)S(1)}, bf16[768,512]{1,0:T(8,128)(2,1)S(1)}, u32[]{:S(2)}, u32[]{:S(2)}) %collective-permute-start.7) | collective-permute-done | bytes 786464 | tf_op jit(solution)/shard_map/ppermute | solution.py:42
  33.5 2.5 %collective-permute-start.11 = (bf16[768,512]{1,0:T(8,128)(2,1)S(1)}, bf16[768,512]{1,0:T(8,128)(2,1)S(1)}, u32[]{:S(2)}, u32[]{:S(2)}) collective-permute-start(bf16[768,512]{1,0:T(8,128)(2,1)S(1)} %collective-permute-done.7.refs_3_), channel_id=1, source_target_pairs={{0,96},{4,28},{8,104},{12,4},{16,112},{20,12},{24,120},{28,20},{32... | collective-permute-start | bytes 2359304 | tf_op jit(solution)/shard_map/ppermute | solution.py:42
  36.0 5.9 %collective-permute-done.8.refs_1_ = bf16[768,512]{1,0:T(8,128)(2,1)S(1)} collective-permute-done((bf16[768,512]{1,0:T(8,128)(2,1)S(1)}, bf16[768,512]{1,0:T(8,128)(2,1)S(1)}, u32[]{:S(2)}, u32[]{:S(2)}) %collective-permute-start.8) | collective-permute-done | bytes 786464 | tf_op jit(solution)/shard_map/ppermute | solution.py:42
  42.7 3.5 %project.6 = (f32[1024,512]{1,0:T(8,128)S(1)}, bf16[2,64,128]{2,1,0:T(8,128)(2,1)S(1)}) custom-call(bf16[1024,6144]{1,0:T(8,128)(2,1)S(1)} %get-tuple-element.73.x_ref, bf16[832,512]{1,0:T(8,128)(2,1)S(1)} %collective-permute-done.6.refs_0_, bf16[768,512]{1,0:T(8,128)(2,1)S(1)} %collective-permute-done.8.refs_1_, ...), custom_call_target="tpu_custom_call" | custom-call | flops 3221225472 | bytes 20000000 | tf_op jit(solution)/shard_map/project/pallas_call | solution.py:285
  46.3 4.3 %collective-permute-done.11.refs_1_ = bf16[768,512]{1,0:T(8,128)(2,1)S(1)} collective-permute-done((bf16[768,512]{1,0:T(8,128)(2,1)S(1)}, bf16[768,512]{1,0:T(8,128)(2,1)S(1)}, u32[]{:S(2)}, u32[]{:S(2)}) %collective-permute-start.11) | collective-permute-done | bytes 786464 | tf_op jit(solution)/shard_map/ppermute | solution.py:42
  51.6 1.8 %project.7 = (f32[1024,512]{1,0:T(8,128)S(1)}, bf16[1,64,128]{2,1,0:T(8,128)(2,1)S(1)}) custom-call(bf16[1024,6144]{1,0:T(8,128)(2,1)S(1)} %get-tuple-element.73.x_ref, bf16[832,512]{1,0:T(8,128)(2,1)S(1)} %collective-permute-done.10.refs_0_, bf16[768,512]{1,0:T(8,128)(2,1)S(1)} %collective-permute-done.11.refs_1_, f32[1024,512]{1,0:T(8,128)S(1)} %get-tuple-element.94.refs_2_), custom_call_target="tpu_custom_call" | custom-call | flops 1610612736 | bytes 10000000 | tf_op jit(solution)/shard_map/project/pallas_call | solution.py:285
  53.4 1.8 %project.8 = (f32[1024,512]{1,0:T(8,128)S(1)}, bf16[1,64,128]{2,1,0:T(8,128)(2,1)S(1)}) custom-call(bf16[1024,6144]{1,0:T(8,128)(2,1)S(1)} %get-tuple-element.73.x_ref, bf16[832,512]{1,0:T(8,128)(2,1)S(1)} %collective-permute-done.12.refs_0_, bf16[768,512]{1,0:T(8,128)(2,1)S(1)} %collective-permute-done.13.refs_1_, ...), custom_call_target="tpu_custom_call" | custom-call | flops 1610612736 | bytes 10000000 | tf_op jit(solution)/shard_map/project/pallas_call | solution.py:285
  55.3 1.8 %project.9 = (f32[1024,512]{1,0:T(8,128)S(1)}, bf16[1,64,128]{2,1,0:T(8,128)(2,1)S(1)}) custom-call(bf16[1024,6144]{1,0:T(8,128)(2,1)S(1)} %get-tuple-element.73.x_ref, bf16[832,512]{1,0:T(8,128)(2,1)S(1)} %collective-permute-done.14.refs_0_, bf16[768,512]{1,0:T(8,128)(2,1)S(1)} %collective-permute-done.15.refs_1_, f32[1024,512]{1,0:T(8,128)S(1)} %get-tuple-element.103.refs_2_), custom_call_target="tpu_custom_call" | custom-call | flops 1610612736 | bytes 10000000 | tf_op jit(solution)/shard_map/project/pallas_call | solution.py:285
  57.1 3.5 %post.1 = (bf16[1024,1024]{1,0:T(8,128)(2,1)S(1)}, f32[512,128]{1,0:T(8,128)S(1)}, f32[512,128]{1,0:T(8,128)S(1)}, bf16[1,64,128]{2,1,0:T(8,128)(2,1)S(1)}, bf16...) custom-call(f32[40,128]{1,0:T(8,128)S(1)} %get-tuple-element.97.dec, ...), custom_call_target="tpu_custom_call" | custom-call | tf_op jit(solution)/shard_map/post/pallas_call | solution.py:344
  61.0 1.3 %collective-permute-done.18.recv_ref = f32[512,128]{1,0:T(8,128)S(1)} collective-permute-done((f32[512,128]{1,0:T(8,128)S(1)}, f32[512,128]{1,0:T(8,128)S(1)}, u32[]{:S(2)}, u32[]{:S(2)}) %collective-permute-start.18) | collective-permute-done | bytes 262176 | tf_op jit(solution)/shard_map/ppermute | solution.py:26
  62.5 1.5 %collective-permute-start.19 = (bf16[512,128]{1,0:T(8,128)(2,1)S(1)}, bf16[512,128]{1,0:T(8,128)(2,1)S(1)}, u32[]{:S(2)}, u32[]{:S(2)}) collective-permute-start(bf16[512,128]{1,0:T(8,128)(2,1)S(1)} %get-tuple-element.112), channel_id=1, source_target_pairs={{0,8},{4,36},{8,16},{12,44},{16,24},{20,52},{24,0},{28,60},{32,40}... | collective-permute-start | bytes 393224 | tf_op jit(solution)/shard_map/ppermute | solution.py:42
  64.0 2.1 %collective-permute-start.20 = (bf16[512,128]{1,0:T(8,128)(2,1)S(1)}, bf16[512,128]{1,0:T(8,128)(2,1)S(1)}, u32[]{:S(2)}, u32[]{:S(2)}) collective-permute-start(bf16[512,128]{1,0:T(8,128)(2,1)S(1)} %get-tuple-element.112), channel_id=1, source_target_pairs={{0,16},{4,68},{8,24},{12,76},{16,0},{20,84},{24,8},{28,92},{32,48}... | collective-permute-start | bytes 393224 | tf_op jit(solution)/shard_map/ppermute | solution.py:42
  66.1 1.6 %collective-permute-start.21 = (bf16[512,128]{1,0:T(8,128)(2,1)S(1)}, bf16[512,128]{1,0:T(8,128)(2,1)S(1)}, u32[]{:S(2)}, u32[]{:S(2)}) collective-permute-start(bf16[512,128]{1,0:T(8,128)(2,1)S(1)} %get-tuple-element.112), channel_id=1, source_target_pairs={{0,24},{4,100},{8,0},{12,108},{16,8},{20,116},{24,16},{28,124},{32... | collective-permute-start | bytes 393224 | tf_op jit(solution)/shard_map/ppermute | solution.py:42
  67.7 2.6 %within.1.comb_ref = f32[2,1024,1024]{2,1,0:T(8,128)S(1)} custom-call(f32[8,1024]{1,0:T(8,128)S(1)} %copy-done.1, bf16[1024,1024]{1,0:T(8,128)(2,1)S(1)} %get-tuple-element.113.v_ref, bf16[8,3,128,256]{3,2,1,0:T(8,128)(2,1)S(1)} %get-tuple-element.114.st_ref, bf16[1024,1024]{1,0:T(8,128)(2,1)S(1)} %get-tuple-element.115.q_ref, ...), custom_call_target="tpu_custom_call" | custom-call | flops 3000000000 | bytes 10000000 | tf_op jit(solution)/shard_map/within/pallas_call | solution.py:385
  71.5 1.4 %collective-permute-start.22 = (bf16[512,128]{1,0:T(8,128)(2,1)S(1)}, bf16[512,128]{1,0:T(8,128)(2,1)S(1)}, u32[]{:S(2)}, u32[]{:S(2)}) collective-permute-start(bf16[512,128]{1,0:T(8,128)(2,1)S(1)} %get-tuple-element.121), channel_id=1, source_target_pairs={{0,32},{4,12},{8,40},{12,20},{16,48},{20,28},{24,56},{28,4},{32,64... | collective-permute-start | bytes 393224 | tf_op jit(solution)/shard_map/ppermute | solution.py:42
  72.9 2.9 %collective-permute-start.23 = (bf16[512,128]{1,0:T(8,128)(2,1)S(1)}, bf16[512,128]{1,0:T(8,128)(2,1)S(1)}, u32[]{:S(2)}, u32[]{:S(2)}) collective-permute-start(bf16[512,128]{1,0:T(8,128)(2,1)S(1)} %get-tuple-element.122), channel_id=1, source_target_pairs={{0,64},{4,20},{8,72},{12,28},{16,80},{20,4},{24,88},{28,12},{32,96... | collective-permute-start | bytes 393224 | tf_op jit(solution)/shard_map/ppermute | solution.py:42
  77.7 2.4 %collective-permute-done.23.r2 = bf16[512,128]{1,0:T(8,128)(2,1)S(1)} collective-permute-done((bf16[512,128]{1,0:T(8,128)(2,1)S(1)}, bf16[512,128]{1,0:T(8,128)(2,1)S(1)}, u32[]{:S(2)}, u32[]{:S(2)}) %collective-permute-start.23) | collective-permute-done | bytes 131104 | tf_op jit(solution)/shard_map/ppermute | solution.py:42
  81.2 2.2 %outer.2 = (f32[1024,512]{1,0:T(8,128)S(1)}, f32[8,128]{1,0:T(8,128)S(1)}) custom-call(f32[8,128]{1,0:T(8,128)S(1)} %get-tuple-element.68.sf, f32[8,1024]{1,0:T(8,128)S(1)} %copy-done.1, f32[512,128]{1,0:T(8,128)S(1)} %get-tuple-element.124.state_ref, f32[2,1024,1024]{2,1,0:T(8,128)S(1)} %within.1.comb_ref, bf16[1024,1024]{1,0:T(8,128)(2,1)S(1)} %copy-done), custom_call_target="tpu_custom_call" | custom-call | flops 600000000 | bytes 6000000 | tf_op jit(solution)/shard_map/outer/pallas_call | solution.py:527
  83.5 2.2 %outer.3 = (f32[1024,512]{1,0:T(8,128)S(1)}, f32[8,128]{1,0:T(8,128)S(1)}) custom-call(f32[8,128]{1,0:T(8,128)S(1)} %get-tuple-element.68.sf, f32[8,1024]{1,0:T(8,128)S(1)} %copy-done.1, f32[512,128]{1,0:T(8,128)S(1)} %collective-permute-done.25.state_ref, f32[2,1024,1024]{2,1,0:T(8,128)S(1)} %within.1.comb_ref, bf16[1024,1024]{1,0:T(8,128)(2,1)S(1)} %copy-done, ...), custom_call_target="tpu_custom_call" | custom-call | flops 600000000 | bytes 6000000 | tf_op jit(solution)/shard_map/outer/pallas_call | solution.py:527
  85.7 3.3 %collective-permute-start.26 = (f32[8,128]{1,0:T(8,128)S(1)}, f32[8,128]{1,0:T(8,128)S(1)}, u32[]{:S(2)}, u32[]{:S(2)}) collective-permute-start(f32[8,128]{1,0:T(8,128)S(1)} %get-tuple-element.130.s0), channel_id=1, source_target_pairs={{0,2},{1,3},{2,0},{3,1},{4,6},{5,7},{6,4},{7,5},{8,10},{9,11},{10,... | collective-permute-start | bytes 12296 | tf_op jit(solution)/shard_map/ppermute | solution.py:30
  89.7 2.6 %collective-permute-start.28 = (f32[8,128]{1,0:T(8,128)S(1)}, f32[8,128]{1,0:T(8,128)S(1)}, u32[]{:S(2)}, u32[]{:S(2)}) collective-permute-start(f32[8,128]{1,0:T(8,128)S(1)} %get-tuple-element.130.s0), channel_id=1, source_target_pairs={{0,3},{1,0},{2,1},{3,2},{4,7},{5,4},{6,5},{7,6},{8,11},{9,8},{10,9... | collective-permute-start | bytes 12296 | tf_op jit(solution)/shard_map/ppermute | solution.py:30
  92.2 1.6 %collective-permute-done.27.s2 = f32[8,128]{1,0:T(8,128)S(1)} collective-permute-done((f32[8,128]{1,0:T(8,128)S(1)}, f32[8,128]{1,0:T(8,128)S(1)}, u32[]{:S(2)}, u32[]{:S(2)}) %collective-permute-start.27) | collective-permute-done | bytes 4128 | tf_op jit(solution)/shard_map/ppermute | solution.py:30
  93.8 1.6 %norm.1 = bf16[1024,1024]{1,0:T(8,128)(2,1)} custom-call(f32[1024,512]{1,0:T(8,128)S(1)} %get-tuple-element.126.mine_ref, f32[1024,512]{1,0:T(8,128)S(1)} %get-tuple-element.129.other_ref, f32[8,128]{1,0:T(8,128)S(1)} %get-tuple-element.130.s0, f32[8,128]{1,0:T(8,128)S(1)} %collective-permute-done.26.s1, f32[8,128]{1,0:T(8,128)S(1)} %collective-permute-done.27.s2, ...), custom_call_target="tpu_custom_call" | custom-call | tf_op jit(solution)/shard_map/norm/pallas_call | solution.py:561
  (59 shorter events, 10.8 us)
Async XLA Ops:
  1.1 1.5 %collective-permute-start = (bf16[192,512]{1,0:T(8,128)(2,1)S(1)}, bf16[192,512]{1,0:T(8,128)(2,1)S(1)}, u32[]{:S(2)}, u32[]{:S(2)}) collective-permute-start(bf16[192,512]{1,0:T(8,128)(2,1)S(1)} %get-tuple-element.132), channel_id=1, source_target_pairs={{0,4},{4,0},{1,5},{5,1},{2,6},{6,2},{3,7},{7,3},{8,12},{12,8},{9,1... | collective-permute-start | bytes 589832 | tf_op jit(solution)/shard_map/ppermute | solution.py:26
  2.7 15.7 %collective-permute-start.1 = (bf16[400,512]{1,0:T(8,128)(2,1)S(1)}, bf16[400,512]{1,0:T(8,128)(2,1)S(1)}, u32[]{:S(2)}, u32[]{:S(2)}) collective-permute-start(bf16[400,512]{1,0:T(8,128)(2,1)S(1)} %fusion), channel_id=1, source_target_pairs={{0,8},{4,36},{8,16},{12,44},{16,24},{20,52},{24,0},{28,60},{32,40}... | collective-permute-start | bytes 1228808 | tf_op jit(solution)/shard_map/ppermute | solution.py:42
  4.8 13.9 %collective-permute-start.2 = (bf16[400,512]{1,0:T(8,128)(2,1)S(1)}, bf16[400,512]{1,0:T(8,128)(2,1)S(1)}, u32[]{:S(2)}, u32[]{:S(2)}) collective-permute-start(bf16[400,512]{1,0:T(8,128)(2,1)S(1)} %fusion), channel_id=1, source_target_pairs={{0,16},{4,68},{8,24},{12,76},{16,0},{20,84},{24,8},{28,92},{32,48}... | collective-permute-start | bytes 1228808 | tf_op jit(solution)/shard_map/ppermute | solution.py:42
  8.4 10.3 %collective-permute-start.3 = (bf16[400,512]{1,0:T(8,128)(2,1)S(1)}, bf16[400,512]{1,0:T(8,128)(2,1)S(1)}, u32[]{:S(2)}, u32[]{:S(2)}) collective-permute-start(bf16[400,512]{1,0:T(8,128)(2,1)S(1)} %fusion), channel_id=1, source_target_pairs={{0,24},{4,100},{8,0},{12,108},{16,8},{20,116},{24,16},{28,124},{32... | collective-permute-start | bytes 1228808 | tf_op jit(solution)/shard_map/ppermute | solution.py:42
  18.8 5.6 %collective-permute-start.5 = (bf16[768,512]{1,0:T(8,128)(2,1)S(1)}, bf16[768,512]{1,0:T(8,128)(2,1)S(1)}, u32[]{:S(2)}, u32[]{:S(2)}) collective-permute-start(bf16[768,512]{1,0:T(8,128)(2,1)S(1)} %pad_maximum_fusion.refs_1_), channel_id=1, source_target_pairs={{0,4},{4,0},{1,5},{5,1},{2,6},{6,2},{3,7},{7,3},{8,12},{12,8},{9,1... | collective-permute-start | bytes 2359304 | tf_op jit(solution)/shard_map/ppermute | solution.py:26
  19.0 5.8 %collective-permute-start.4 = (bf16[832,512]{1,0:T(8,128)(2,1)S(1)}, bf16[832,512]{1,0:T(8,128)(2,1)S(1)}, u32[]{:S(2)}, u32[]{:S(2)}) collective-permute-start(bf16[832,512]{1,0:T(8,128)(2,1)S(1)} %slice_dynamic-update-slice_fusion.2.refs_0_), channel_id=1, source_target_pairs={{0,4},{4,0},{1,5},{5,1},{2,6},{6,2},{3,7},{7,3},{8,12},{12,8},{9,1... | collective-permute-start | bytes 2555912 | tf_op jit(solution)/shard_map/ppermute | solution.py:26
  19.6 13.9 %collective-permute-start.6 = (bf16[832,512]{1,0:T(8,128)(2,1)S(1)}, bf16[832,512]{1,0:T(8,128)(2,1)S(1)}, u32[]{:S(2)}, u32[]{:S(2)}) collective-permute-start(bf16[832,512]{1,0:T(8,128)(2,1)S(1)} %slice_dynamic-update-slice_fusion.2.refs_0_), channel_id=1, source_target_pairs={{0,32},{4,12},{8,40},{12,20},{16,48},{20,28},{24,56},{28,4},{32,64... | collective-permute-start | bytes 2555912 | tf_op jit(solution)/shard_map/ppermute | solution.py:42
  21.1 12.0 %collective-permute-start.7 = (bf16[768,512]{1,0:T(8,128)(2,1)S(1)}, bf16[768,512]{1,0:T(8,128)(2,1)S(1)}, u32[]{:S(2)}, u32[]{:S(2)}) collective-permute-start(bf16[768,512]{1,0:T(8,128)(2,1)S(1)} %pad_maximum_fusion.refs_1_), channel_id=1, source_target_pairs={{0,96},{4,28},{8,104},{12,4},{16,112},{20,12},{24,120},{28,20},{32... | collective-permute-start | bytes 2359304 | tf_op jit(solution)/shard_map/ppermute | solution.py:42
  22.8 19.4 %collective-permute-start.9 = (bf16[832,512]{1,0:T(8,128)(2,1)S(1)}, bf16[832,512]{1,0:T(8,128)(2,1)S(1)}, u32[]{:S(2)}, u32[]{:S(2)}) collective-permute-start(bf16[832,512]{1,0:T(8,128)(2,1)S(1)} %slice_dynamic-update-slice_fusion.2.refs_0_), channel_id=1, source_target_pairs={{0,96},{4,28},{8,104},{12,4},{16,112},{20,12},{24,120},{28,20},{32... | collective-permute-start | bytes 2555912 | tf_op jit(solution)/shard_map/ppermute | solution.py:42
  24.4 17.5 %collective-permute-start.8 = (bf16[768,512]{1,0:T(8,128)(2,1)S(1)}, bf16[768,512]{1,0:T(8,128)(2,1)S(1)}, u32[]{:S(2)}, u32[]{:S(2)}) collective-permute-start(bf16[768,512]{1,0:T(8,128)(2,1)S(1)} %pad_maximum_fusion.refs_1_), channel_id=1, source_target_pairs={{0,32},{4,12},{8,40},{12,20},{16,48},{20,28},{24,56},{28,4},{32,64... | collective-permute-start | bytes 2359304 | tf_op jit(solution)/shard_map/ppermute | solution.py:42
  33.5 17.1 %collective-permute-start.11 = (bf16[768,512]{1,0:T(8,128)(2,1)S(1)}, bf16[768,512]{1,0:T(8,128)(2,1)S(1)}, u32[]{:S(2)}, u32[]{:S(2)}) collective-permute-start(bf16[768,512]{1,0:T(8,128)(2,1)S(1)} %collective-permute-done.7.refs_3_), channel_id=1, source_target_pairs={{0,96},{4,28},{8,104},{12,4},{16,112},{20,12},{24,120},{28,20},{32... | collective-permute-start | bytes 2359304 | tf_op jit(solution)/shard_map/ppermute | solution.py:42
  36.0 15.0 %collective-permute-start.10 = (bf16[832,512]{1,0:T(8,128)(2,1)S(1)}, bf16[832,512]{1,0:T(8,128)(2,1)S(1)}, u32[]{:S(2)}, u32[]{:S(2)}) collective-permute-start(bf16[832,512]{1,0:T(8,128)(2,1)S(1)} %collective-permute-done.6.refs_0_), channel_id=1, source_target_pairs={{0,32},{4,12},{8,40},{12,20},{16,48},{20,28},{24,56},{28,4},{32,64... | collective-permute-start | bytes 2555912 | tf_op jit(solution)/shard_map/ppermute | solution.py:42
  42.2 8.9 %collective-permute-start.13 = (bf16[768,512]{1,0:T(8,128)(2,1)S(1)}, bf16[768,512]{1,0:T(8,128)(2,1)S(1)}, u32[]{:S(2)}, u32[]{:S(2)}) collective-permute-start(bf16[768,512]{1,0:T(8,128)(2,1)S(1)} %collective-permute-done.8.refs_1_), channel_id=1, source_target_pairs={{0,4},{4,0},{1,5},{5,1},{2,6},{6,2},{3,7},{7,3},{8,12},{12,8},{9,1... | collective-permute-start | bytes 2359304 | tf_op jit(solution)/shard_map/ppermute | solution.py:26
  42.2 11.2 %collective-permute-start.12 = (bf16[832,512]{1,0:T(8,128)(2,1)S(1)}, bf16[832,512]{1,0:T(8,128)(2,1)S(1)}, u32[]{:S(2)}, u32[]{:S(2)}) collective-permute-start(bf16[832,512]{1,0:T(8,128)(2,1)S(1)} %collective-permute-done.6.refs_0_), channel_id=1, source_target_pairs={{0,4},{4,0},{1,5},{5,1},{2,6},{6,2},{3,7},{7,3},{8,12},{12,8},{9,1... | collective-permute-start | bytes 2555912 | tf_op jit(solution)/shard_map/ppermute | solution.py:26
  46.2 9.1 %collective-permute-start.14 = (bf16[832,512]{1,0:T(8,128)(2,1)S(1)}, bf16[832,512]{1,0:T(8,128)(2,1)S(1)}, u32[]{:S(2)}, u32[]{:S(2)}) collective-permute-start(bf16[832,512]{1,0:T(8,128)(2,1)S(1)} %collective-permute-done.9.refs_2_), channel_id=1, source_target_pairs={{0,4},{4,0},{1,5},{5,1},{2,6},{6,2},{3,7},{7,3},{8,12},{12,8},{9,1... | collective-permute-start | bytes 2555912 | tf_op jit(solution)/shard_map/ppermute | solution.py:26
  50.6 4.6 %collective-permute-start.15 = (bf16[768,512]{1,0:T(8,128)(2,1)S(1)}, bf16[768,512]{1,0:T(8,128)(2,1)S(1)}, u32[]{:S(2)}, u32[]{:S(2)}) collective-permute-start(bf16[768,512]{1,0:T(8,128)(2,1)S(1)} %collective-permute-done.7.refs_3_), channel_id=1, source_target_pairs={{0,4},{4,0},{1,5},{5,1},{2,6},{6,2},{3,7},{7,3},{8,12},{12,8},{9,1... | collective-permute-start | bytes 2359304 | tf_op jit(solution)/shard_map/ppermute | solution.py:26
  51.0 6.1 %collective-permute-start.16 = (bf16[832,512]{1,0:T(8,128)(2,1)S(1)}, bf16[832,512]{1,0:T(8,128)(2,1)S(1)}, u32[]{:S(2)}, u32[]{:S(2)}) collective-permute-start(bf16[832,512]{1,0:T(8,128)(2,1)S(1)} %collective-permute-done.10.refs_0_), channel_id=1, source_target_pairs={{0,4},{4,0},{1,5},{5,1},{2,6},{6,2},{3,7},{7,3},{8,12},{12,8},{9,1... | collective-permute-start | bytes 2555912 | tf_op jit(solution)/shard_map/ppermute | solution.py:26
  51.1 6.0 %collective-permute-start.17 = (bf16[768,512]{1,0:T(8,128)(2,1)S(1)}, bf16[768,512]{1,0:T(8,128)(2,1)S(1)}, u32[]{:S(2)}, u32[]{:S(2)}) collective-permute-start(bf16[768,512]{1,0:T(8,128)(2,1)S(1)} %collective-permute-done.11.refs_1_), channel_id=1, source_target_pairs={{0,4},{4,0},{1,5},{5,1},{2,6},{6,2},{3,7},{7,3},{8,12},{12,8},{9,1... | collective-permute-start | bytes 2359304 | tf_op jit(solution)/shard_map/ppermute | solution.py:26
  57.1 10.5 %copy-start.1 = (f32[8,1024]{1,0:T(8,128)S(1)}, f32[8,1024]{1,0:T(8,128)}, u32[]{:S(2)}) copy-start(f32[8,1024]{1,0:T(8,128)} %ld_ref.2) | copy-start | bytes 98308
  60.7 1.6 %collective-permute-start.18 = (f32[512,128]{1,0:T(8,128)S(1)}, f32[512,128]{1,0:T(8,128)S(1)}, u32[]{:S(2)}, u32[]{:S(2)}) collective-permute-start(f32[512,128]{1,0:T(8,128)S(1)} %get-tuple-element.109), channel_id=1, source_target_pairs={{0,4},{4,0},{1,5},{5,1},{2,6},{6,2},{3,7},{7,3},{8,12},{12,8},{9,1... | collective-permute-start | bytes 786440 | tf_op jit(solution)/shard_map/ppermute | solution.py:26
  62.5 7.9 %collective-permute-start.19 = (bf16[512,128]{1,0:T(8,128)(2,1)S(1)}, bf16[512,128]{1,0:T(8,128)(2,1)S(1)}, u32[]{:S(2)}, u32[]{:S(2)}) collective-permute-start(bf16[512,128]{1,0:T(8,128)(2,1)S(1)} %get-tuple-element.112), channel_id=1, source_target_pairs={{0,8},{4,36},{8,16},{12,44},{16,24},{20,52},{24,0},{28,60},{32,40}... | collective-permute-start | bytes 393224 | tf_op jit(solution)/shard_map/ppermute | solution.py:42
  64.0 6.5 %collective-permute-start.20 = (bf16[512,128]{1,0:T(8,128)(2,1)S(1)}, bf16[512,128]{1,0:T(8,128)(2,1)S(1)}, u32[]{:S(2)}, u32[]{:S(2)}) collective-permute-start(bf16[512,128]{1,0:T(8,128)(2,1)S(1)} %get-tuple-element.112), channel_id=1, source_target_pairs={{0,16},{4,68},{8,24},{12,76},{16,0},{20,84},{24,8},{28,92},{32,48}... | collective-permute-start | bytes 393224 | tf_op jit(solution)/shard_map/ppermute | solution.py:42
  66.1 5.0 %collective-permute-start.21 = (bf16[512,128]{1,0:T(8,128)(2,1)S(1)}, bf16[512,128]{1,0:T(8,128)(2,1)S(1)}, u32[]{:S(2)}, u32[]{:S(2)}) collective-permute-start(bf16[512,128]{1,0:T(8,128)(2,1)S(1)} %get-tuple-element.112), channel_id=1, source_target_pairs={{0,24},{4,100},{8,0},{12,108},{16,8},{20,116},{24,16},{28,124},{32... | collective-permute-start | bytes 393224 | tf_op jit(solution)/shard_map/ppermute | solution.py:42
  67.7 13.6 %copy-start = (bf16[1024,1024]{1,0:T(8,128)(2,1)S(1)}, bf16[1024,1024]{1,0:T(8,128)(2,1)}, u32[]{:S(2)}) copy-start(bf16[1024,1024]{1,0:T(8,128)(2,1)} %q_ref.1) | copy-start | bytes 6291460
  71.5 6.2 %collective-permute-start.22 = (bf16[512,128]{1,0:T(8,128)(2,1)S(1)}, bf16[512,128]{1,0:T(8,128)(2,1)S(1)}, u32[]{:S(2)}, u32[]{:S(2)}) collective-permute-start(bf16[512,128]{1,0:T(8,128)(2,1)S(1)} %get-tuple-element.121), channel_id=1, source_target_pairs={{0,32},{4,12},{8,40},{12,20},{16,48},{20,28},{24,56},{28,4},{32,64... | collective-permute-start | bytes 393224 | tf_op jit(solution)/shard_map/ppermute | solution.py:42
  72.9 7.3 %collective-permute-start.23 = (bf16[512,128]{1,0:T(8,128)(2,1)S(1)}, bf16[512,128]{1,0:T(8,128)(2,1)S(1)}, u32[]{:S(2)}, u32[]{:S(2)}) collective-permute-start(bf16[512,128]{1,0:T(8,128)(2,1)S(1)} %get-tuple-element.122), channel_id=1, source_target_pairs={{0,64},{4,20},{8,72},{12,28},{16,80},{20,4},{24,88},{28,12},{32,96... | collective-permute-start | bytes 393224 | tf_op jit(solution)/shard_map/ppermute | solution.py:42
  75.8 5.0 %collective-permute-start.24 = (bf16[512,128]{1,0:T(8,128)(2,1)S(1)}, bf16[512,128]{1,0:T(8,128)(2,1)S(1)}, u32[]{:S(2)}, u32[]{:S(2)}) collective-permute-start(bf16[512,128]{1,0:T(8,128)(2,1)S(1)} %get-tuple-element.123), channel_id=1, source_target_pairs={{0,96},{4,28},{8,104},{12,4},{16,112},{20,12},{24,120},{28,20},{32... | collective-permute-start | bytes 393224 | tf_op jit(solution)/shard_map/ppermute | solution.py:42
  80.9 2.5 %collective-permute-start.25 = (f32[512,128]{1,0:T(8,128)S(1)}, f32[512,128]{1,0:T(8,128)S(1)}, u32[]{:S(2)}, u32[]{:S(2)}) collective-permute-start(f32[512,128]{1,0:T(8,128)S(1)} %get-tuple-element.127), channel_id=1, source_target_pairs={{0,4},{4,0},{1,5},{5,1},{2,6},{6,2},{3,7},{7,3},{8,12},{12,8},{9,1... | collective-permute-start | bytes 786440 | tf_op jit(solution)/shard_map/ppermute | solution.py:26
  83.5 10.3 %copy-start.2 = (f32[1024]{0:T(1024)S(1)}, f32[1024]{0:T(1024)}, u32[]{:S(2)}) copy-start(f32[1024]{0:T(1024)} %param.13) | copy-start | bytes 12292
  85.7 6.5 %collective-permute-start.26 = (f32[8,128]{1,0:T(8,128)S(1)}, f32[8,128]{1,0:T(8,128)S(1)}, u32[]{:S(2)}, u32[]{:S(2)}) collective-permute-start(f32[8,128]{1,0:T(8,128)S(1)} %get-tuple-element.130.s0), channel_id=1, source_target_pairs={{0,2},{1,3},{2,0},{3,1},{4,6},{5,7},{6,4},{7,5},{8,10},{9,11},{10,... | collective-permute-start | bytes 12296 | tf_op jit(solution)/shard_map/ppermute | solution.py:30
  89.0 4.8 %collective-permute-start.27 = (f32[8,128]{1,0:T(8,128)S(1)}, f32[8,128]{1,0:T(8,128)S(1)}, u32[]{:S(2)}, u32[]{:S(2)}) collective-permute-start(f32[8,128]{1,0:T(8,128)S(1)} %get-tuple-element.130.s0), channel_id=1, source_target_pairs={{0,1},{1,2},{2,3},{3,0},{4,5},{5,6},{6,7},{7,4},{8,9},{9,10},{10,1... | collective-permute-start | bytes 12296 | tf_op jit(solution)/shard_map/ppermute | solution.py:30
  89.7 4.1 %collective-permute-start.28 = (f32[8,128]{1,0:T(8,128)S(1)}, f32[8,128]{1,0:T(8,128)S(1)}, u32[]{:S(2)}, u32[]{:S(2)}) collective-permute-start(f32[8,128]{1,0:T(8,128)S(1)} %get-tuple-element.130.s0), channel_id=1, source_target_pairs={{0,3},{1,0},{2,1},{3,2},{4,7},{5,4},{6,5},{7,6},{8,11},{9,8},{10,9... | collective-permute-start | bytes 12296 | tf_op jit(solution)/shard_map/ppermute | solution.py:30
